TPU v7x, 128 devices: a whole 4x4x4 slice. The times are simulated.
128 devices in a mesh: rows: 8 (over z, core), lag: 16 (over y, x).
Axes of the slice: x: 4, y: 4, z: 4, core: 2. Of those that a mesh axis runs over, the one named last changes fastest.
Arguments:
- excitation: bfloat16 [4, 4096, 128], P(None, 'rows'), may hold values from -6 to 6
- pending: float32 [16, 4096, 128], P('lag', 'rows'), may hold values from -6 to 6
- inverse: float32 [32, 128, 128], P('rows'), may hold values from -0.5 to 0.5
- interaction: bfloat16 [12288, 128, 128], P(('rows', 'lag')), may hold values from -0.02734375 to 0.02734375
- slot_row: int32 [12288], P(('rows', 'lag')), may hold values from 0 to 3
- slot_owner: int32 [12288], P(('rows', 'lag')), may hold values from 0 to 7
- slot_pos: int32 [12288], P(('rows', 'lag')), may hold values from 0 to 1
- needed: int32 [128, 8, 2], P(('rows', 'lag')), may hold values from 0 to 3
- block_count: int32 [8, 16], P('rows', 'lag'), may hold values from 6 to 96, as said below
Outputs:
- currents: bfloat16 [4, 4096, 128], P(None, 'rows')
- carried: float32 [16, 4096, 128], P('lag', 'rows')
Inputs may be any that keep to these rules, and one draw needn't show every extreme that they name: `block_count`: every row owner and lag has at least 6 live slots, and some row owner and lag has all 96 live.
All inputs are finite; a program needn't handle non-finite values.
Results may differ from a plain program's by a relative error of at most 0.002.
Values may be sent and summed in bfloat16 or wider, within the bound.
No kernel may reach another device: no remote copies, remote signals or barrier semaphores. Data moves between devices by JAX's collectives and lax.ppermute only.
A program may use at most 64 MiB of HBM per device.

v0:
```python
import jax
import jax.numpy as jnp
from jax import lax
from jax.sharding import PartitionSpec as P


def from_root(block, axis, owner):
    block = jnp.where(lax.axis_index(axis) == owner, block, jnp.zeros_like(block))
    return lax.psum(block, axis)


def from_behind(value, axis, steps):
    count = lax.axis_size(axis)
    first, last = (max(0, -steps), min(count, count - steps))
    return lax.ppermute(value, axis, [(source, source + steps) for source in range(first, last)])


def place_rows(placing, products):
    high_part = lax.optimization_barrier(products.astype(jnp.bfloat16))
    low_part = (products - high_part.astype(jnp.float32)).astype(jnp.bfloat16)
    first = jnp.einsum("bk,kie->bie", placing, high_part, preferred_element_type=jnp.float32)
    second = jnp.einsum("bk,kie->bie", placing, low_part, preferred_element_type=jnp.float32)
    return first + second


def per_device(
    excitation, pending, inverse, interaction, slot_row, slot_owner, slot_pos, needed, block_count
):
    row_blocks, block_size, _ = inverse.shape
    slot_total = interaction.shape[0]
    exc_width = excitation.shape[2]
    capacity = needed.shape[2]
    live_slots = jnp.arange(slot_total, dtype=jnp.int32) < block_count[0, 0]
    placing = (
        (slot_row[None, :] == jnp.arange(row_blocks, dtype=jnp.int32)[:, None])
        & live_slots[None, :]
    ).astype(jnp.bfloat16)
    need_table = needed[0]
    asked = lax.all_to_all(need_table, "rows", split_axis=0, concat_axis=0, tiled=True)
    send_index = asked.reshape(-1)
    source = slot_owner * capacity + slot_pos
    accumulated = pending[0]
    outputs = []
    for step_index in range(excitation.shape[0]):
        right_side = (excitation[step_index].astype(jnp.float32) - accumulated).reshape(
            row_blocks, block_size, exc_width
        )
        solved = jnp.einsum(
            "bij,bje->bie", inverse, right_side, precision=lax.Precision.HIGHEST
        ).astype(jnp.bfloat16)
        solved = from_root(solved, "lag", 0)
        outputs.append(solved.reshape(row_blocks * block_size, exc_width))
        outgoing = jnp.take(solved, send_index, axis=0)
        arrived = lax.all_to_all(outgoing, "rows", split_axis=0, concat_axis=0, tiled=True)
        picked = jnp.take(arrived, source, axis=0)
        products = jnp.einsum(
            "kij,kje->kie", interaction, picked, preferred_element_type=jnp.float32
        )
        lag_term = place_rows(placing, products)
        handed = from_behind(accumulated, "lag", -1)
        accumulated = handed + lag_term.reshape(row_blocks * block_size, exc_width)
    return (jnp.stack(outputs), accumulated[None])


def solution(mesh):
    in_specs = (
        P(None, "rows", None),
        P("lag", "rows", None),
        P("rows", None, None),
        P(("rows", "lag"), None, None),
        P(("rows", "lag")),
        P(("rows", "lag")),
        P(("rows", "lag")),
        P(("rows", "lag"), None, None),
        P("rows", "lag"),
    )
    out_specs = (P(None, "rows", None), P("lag", "rows", None))
    return jax.shard_map(
        per_device, mesh=mesh, in_specs=in_specs, out_specs=out_specs, check_vma=False
    )
```

profile of v0, /device:TPU:25, one launch (start us, length us, event | category | flops | bytes accessed | tf_op | source)
XLA Modules:
  0.0 564.5 jit_solution(6836845720769716552)
XLA Ops:
  7.2 1.5 copy.47
  8.7 6.0 %all-to-all-start = ((s32[8,1,2]{2,1,0:T(1,128)}), s32[8,1,2]{2,1,0:T(1,128)S(1)}, u32[]{:S(2)}, u32[]{:S(2)}) async-start(s32[8,1,2]{2,1,0:T(1,128)} %copy.47), calls=%async_computation | async-start | bytes 8192 | tf_op jit(solution)/shard_map/all_to_all | solution.py:39
  14.7 1.0 convert_subtract_fusion.3
  15.7 2.2 fusion.21
  18.0 4.6 collective-permute-start
  23.8 77.0 %all-reduce.5.cloned.1.call-done = bf16[4,128,128]{1,2,0:T(8,128)(2,1)} async-done(((bf16[4,128,128]{1,2,0:T(8,128)(2,1)}), bf16[4,128,128]{1,2,0:T(8,128)(2,1)}) %all-reduce.5.cloned.1.call-update) | async-done | bytes 131088 | tf_op jit(solution)/shard_map/psum | solution.py:9
  100.8 2.3 gather_fusion
  103.1 1.9 broadcast_select_fusion.3
  105.1 7.0 %all-to-all-start.1 = ((bf16[16,128,128]{1,2,0:T(8,128)(2,1)}), bf16[16,128,128]{1,2,0:T(8,128)(2,1)}, u32[]{:S(2)}, u32[]{:S(2)}) async-start(bf16[16,128,128]{1,2,0:T(8,128)(2,1)} %broadcast_select_fusion.3), calls=%async_computation.1 | async-start | bytes 1048576 | tf_op jit(solution)/shard_map/all_to_all | solution.py:54
  112.8 8.7 %all-to-all-done.1 = bf16[16,128,128]{1,2,0:T(8,128)(2,1)} async-done(((bf16[16,128,128]{1,2,0:T(8,128)(2,1)}), bf16[16,128,128]{1,2,0:T(8,128)(2,1)}, u32[]{:S(2)}, u32[]{:S(2)}) %all-to-all-start.1) | async-done | bytes 524320 | tf_op jit(solution)/shard_map/all_to_all | solution.py:54
  121.5 3.8 gather_fusion.1
  125.3 7.8 %bitcast_convert_fusion.3 = (bf16[96,128,128]{1,2,0:T(8,128)(2,1)}, f32[96,128,128]{2,1,0:T(8,128)}) fusion(bf16[96,128,128]{2,1,0:T(8,128)(2,1)S(1)} %copy-done, bf16[96,128,128]{1,2,0:T(8,128)(2,1)} %gather_fusion.1, pred[96]{0:T(512)(128)(4,1)S(1)} %get-tuple-element.10), kind=kOutput, calls=%fused_computation.18 | convolution fusion | flops 405798912 | bytes 15728736 | tf_op jit(solution)/shard_map/kij,kje->kie/dot_general | solution.py:56
  133.1 4.9 copy.48
  138.0 6.7 %fusion.3 = bf16[96,128,128]{1,2,0:T(8,128)(2,1)} fusion(f32[96,128,128]{2,1,0:T(8,128)} %get-tuple-element.13, bf16[96,128,128]{1,2,0:T(8,128)(2,1)} %get-tuple-element.12), kind=kLoop, calls=%fused_computation.19 | loop fusion | flops 4718592 | bytes 12582912 | tf_op jit(solution)/shard_map/convert_element_type | solution.py:20
  144.7 5.0 copy.49
  149.7 2.5 fusion.34
  153.1 1.8 convert_subtract_fusion.2
  154.9 1.3 fusion.23
  156.2 78.8 %all-reduce.7.cloned.1.call-done = bf16[4,128,128]{1,2,0:T(8,128)(2,1)} async-done(((bf16[4,128,128]{1,2,0:T(8,128)(2,1)}), bf16[4,128,128]{1,2,0:T(8,128)(2,1)}) %all-reduce.7.cloned.1.call-update) | async-done | bytes 131088 | tf_op jit(solution)/shard_map/psum | solution.py:9
  235.0 2.3 gather_fusion.2
  237.3 1.9 broadcast_select_fusion.2
  239.3 7.0 %all-to-all-start.2 = ((bf16[16,128,128]{1,2,0:T(8,128)(2,1)}), bf16[16,128,128]{1,2,0:T(8,128)(2,1)}, u32[]{:S(2)}, u32[]{:S(2)}) async-start(bf16[16,128,128]{1,2,0:T(8,128)(2,1)} %broadcast_select_fusion.2), calls=%async_computation.2 | async-start | bytes 1048576 | tf_op jit(solution)/shard_map/all_to_all | solution.py:54
  246.2 3.3 collective-permute-start.1
  249.5 6.2 %all-to-all-done.2 = bf16[16,128,128]{1,2,0:T(8,128)(2,1)} async-done(((bf16[16,128,128]{1,2,0:T(8,128)(2,1)}), bf16[16,128,128]{1,2,0:T(8,128)(2,1)}, u32[]{:S(2)}, u32[]{:S(2)}) %all-to-all-start.2) | async-done | bytes 524320 | tf_op jit(solution)/shard_map/all_to_all | solution.py:54
  255.7 3.8 gather_fusion.3
  259.5 7.9 %bitcast_convert_fusion.2 = (bf16[96,128,128]{1,2,0:T(8,128)(2,1)}, f32[96,128,128]{2,1,0:T(8,128)}) fusion(bf16[96,128,128]{2,1,0:T(8,128)(2,1)S(1)} %copy-done, bf16[96,128,128]{1,2,0:T(8,128)(2,1)} %gather_fusion.3, pred[96]{0:T(512)(128)(4,1)S(1)} %get-tuple-element.10), kind=kOutput, calls=%fused_computation.15 | convolution fusion | flops 405798912 | bytes 15728736 | tf_op jit(solution)/shard_map/kij,kje->kie/dot_general | solution.py:56
  267.4 4.9 copy.53
  272.3 6.9 %fusion.2 = bf16[96,128,128]{1,2,0:T(8,128)(2,1)} fusion(f32[96,128,128]{2,1,0:T(8,128)} %get-tuple-element.15, bf16[96,128,128]{1,2,0:T(8,128)(2,1)} %get-tuple-element.14), kind=kLoop, calls=%fused_computation.16 | loop fusion | flops 4718592 | bytes 12582912 | tf_op jit(solution)/shard_map/convert_element_type | solution.py:20
  279.2 1.2 fusion.35
  280.4 4.9 copy.54
  285.3 2.4 convolution_add_fusion.2
  287.7 1.8 convert_subtract_fusion.1
  289.5 1.3 fusion.25
  290.8 78.8 %all-reduce.9.cloned.1.call-done = bf16[4,128,128]{1,2,0:T(8,128)(2,1)} async-done(((bf16[4,128,128]{1,2,0:T(8,128)(2,1)}), bf16[4,128,128]{1,2,0:T(8,128)(2,1)}) %all-reduce.9.cloned.1.call-update) | async-done | bytes 131088 | tf_op jit(solution)/shard_map/psum | solution.py:9
  369.6 2.3 gather_fusion.4
  371.9 1.9 broadcast_select_fusion.1
  373.8 7.0 %all-to-all-start.3 = ((bf16[16,128,128]{1,2,0:T(8,128)(2,1)}), bf16[16,128,128]{1,2,0:T(8,128)(2,1)}, u32[]{:S(2)}, u32[]{:S(2)}) async-start(bf16[16,128,128]{1,2,0:T(8,128)(2,1)} %broadcast_select_fusion.1), calls=%async_computation.3 | async-start | bytes 1048576 | tf_op jit(solution)/shard_map/all_to_all | solution.py:54
  380.8 3.1 collective-permute-start.2
  383.9 6.3 %all-to-all-done.3 = bf16[16,128,128]{1,2,0:T(8,128)(2,1)} async-done(((bf16[16,128,128]{1,2,0:T(8,128)(2,1)}), bf16[16,128,128]{1,2,0:T(8,128)(2,1)}, u32[]{:S(2)}, u32[]{:S(2)}) %all-to-all-start.3) | async-done | bytes 524320 | tf_op jit(solution)/shard_map/all_to_all | solution.py:54
  390.3 3.8 gather_fusion.5
  394.0 7.9 %bitcast_convert_fusion.1 = (bf16[96,128,128]{1,2,0:T(8,128)(2,1)}, f32[96,128,128]{2,1,0:T(8,128)}) fusion(bf16[96,128,128]{2,1,0:T(8,128)(2,1)S(1)} %copy-done, bf16[96,128,128]{1,2,0:T(8,128)(2,1)} %gather_fusion.5, pred[96]{0:T(512)(128)(4,1)S(1)} %get-tuple-element.10), kind=kOutput, calls=%fused_computation.12 | convolution fusion | flops 405798912 | bytes 15728736 | tf_op jit(solution)/shard_map/kij,kje->kie/dot_general | solution.py:56
  401.9 4.9 copy.58
  406.8 6.9 %fusion.1 = bf16[96,128,128]{1,2,0:T(8,128)(2,1)} fusion(f32[96,128,128]{2,1,0:T(8,128)} %get-tuple-element.17, bf16[96,128,128]{1,2,0:T(8,128)(2,1)} %get-tuple-element.16), kind=kLoop, calls=%fused_computation.13 | loop fusion | flops 4718592 | bytes 12582912 | tf_op jit(solution)/shard_map/convert_element_type | solution.py:20
  413.7 1.2 fusion.36
  414.9 4.9 copy.59
  419.8 2.4 convolution_add_fusion.1
  422.3 1.8 convert_subtract_fusion
  424.1 1.3 fusion.27
  425.4 78.9 %all-reduce.11.cloned.1.call-done = bf16[4,128,128]{1,2,0:T(8,128)(2,1)} async-done(((bf16[4,128,128]{1,2,0:T(8,128)(2,1)}), bf16[4,128,128]{1,2,0:T(8,128)(2,1)}) %all-reduce.11.cloned.1.call-update) | async-done | bytes 131088 | tf_op jit(solution)/shard_map/psum | solution.py:9
  504.2 2.4 gather_fusion.6
  506.6 2.0 broadcast_select_fusion
  508.6 7.0 %all-to-all-start.4 = ((bf16[16,128,128]{1,2,0:T(8,128)(2,1)}), bf16[16,128,128]{1,2,0:T(8,128)(2,1)}, u32[]{:S(2)}, u32[]{:S(2)}) async-start(bf16[16,128,128]{1,2,0:T(8,128)(2,1)} %broadcast_select_fusion), calls=%async_computation.4 | async-start | bytes 1048576 | tf_op jit(solution)/shard_map/all_to_all | solution.py:54
  515.7 1.0 copy.52
  516.7 1.6 copy.57
  518.4 3.3 collective-permute-start.3
  521.7 0.8 copy.62
  522.5 1.8 pad_maximum_fusion
  525.0 3.8 gather_fusion.7
  528.8 7.9 %bitcast_convert_fusion = (bf16[96,128,128]{1,2,0:T(8,128)(2,1)}, f32[96,128,128]{2,1,0:T(8,128)}) fusion(bf16[96,128,128]{2,1,0:T(8,128)(2,1)S(1)} %copy-done, bf16[96,128,128]{1,2,0:T(8,128)(2,1)} %gather_fusion.7, pred[96]{0:T(512)(128)(4,1)S(1)} %get-tuple-element.10), kind=kOutput, calls=%fused_computation.9 | convolution fusion | flops 405798912 | bytes 15728736 | tf_op jit(solution)/shard_map/kij,kje->kie/dot_general | solution.py:56
  536.6 4.9 copy.63
  541.6 6.9 %fusion = bf16[96,128,128]{1,2,0:T(8,128)(2,1)} fusion(f32[96,128,128]{2,1,0:T(8,128)} %get-tuple-element.19, bf16[96,128,128]{1,2,0:T(8,128)(2,1)} %get-tuple-element.18), kind=kLoop, calls=%fused_computation.10 | loop fusion | flops 4718592 | bytes 12582912 | tf_op jit(solution)/shard_map/convert_element_type | solution.py:20
  549.0 4.9 copy.64
  553.9 2.4 convolution_add_fusion
  556.3 1.7 bitcast_add_fusion
  (55 shorter events, 3.7 us)
Async XLA Ops:
  7.2 118.1 %copy-start = (bf16[96,128,128]{2,1,0:T(8,128)(2,1)S(1)}, bf16[96,128,128]{2,1,0:T(8,128)(2,1)}, u32[]{:S(2)}) copy-start(bf16[96,128,128]{2,1,0:T(8,128)(2,1)} %param.16) | copy-start | bytes 9437188
  7.2 104.9 %copy-start.9 = (s32[96]{0:T(128)S(1)}, s32[96]{0:T(128)}, u32[]{:S(2)}) copy-start(s32[96]{0:T(128)} %param.19) | copy-start | bytes 1156
  7.2 104.8 %copy-start.10 = (s32[96]{0:T(128)S(1)}, s32[96]{0:T(128)}, u32[]{:S(2)}) copy-start(s32[96]{0:T(128)} %param.18) | copy-start | bytes 1156
  7.2 105.5 %copy-start.11 = (s32[96]{0:T(128)S(1)}, s32[96]{0:T(128)}, u32[]{:S(2)}) copy-start(s32[96]{0:T(128)} %param.17) | copy-start | bytes 1156
  8.7 13.8 %all-to-all-start = ((s32[8,1,2]{2,1,0:T(1,128)}), s32[8,1,2]{2,1,0:T(1,128)S(1)}, u32[]{:S(2)}, u32[]{:S(2)}) async-start(s32[8,1,2]{2,1,0:T(1,128)} %copy.47), calls=%async_computation | async-start | bytes 8192 | tf_op jit(solution)/shard_map/all_to_all | solution.py:39
  14.7 86.1 %all-reduce.5.cloned.1.call-start = ((), (), s32[]{:S(2)}) async-start(), calls=%async_computation.5 | async-start | bytes 262144 | tf_op jit(solution)/shard_map/psum | solution.py:9
  18.0 135.2 %collective-permute-start = (f32[512,128]{1,0:T(8,128)}, f32[512,128]{1,0:T(8,128)}, u32[]{:S(2)}, u32[]{:S(2)}) collective-permute-start(f32[512,128]{1,0:T(8,128)} %bitcast.100), channel_id=1, source_target_pairs={{1,0},{2,1},{3,2},{4,3},{5,4},{6,5},{7,6},{8,7},{9,8},{10,9},{11,1... | collective-permute-start | bytes 786440 | tf_op jit(solution)/shard_map/ppermute | solution.py:15
  23.8 348.1 %copy-start.8 = (pred[16]{0:T(512)(128)(4,1)}, pred[16]{0:T(512)(128)(4,1)S(1)}, u32[]{:S(2)}) copy-start(pred[16]{0:T(512)(128)(4,1)S(1)} %compare_and_fusion.1) | copy-start | bytes 52
  105.1 16.4 %all-to-all-start.1 = ((bf16[16,128,128]{1,2,0:T(8,128)(2,1)}), bf16[16,128,128]{1,2,0:T(8,128)(2,1)}, u32[]{:S(2)}, u32[]{:S(2)}) async-start(bf16[16,128,128]{1,2,0:T(8,128)(2,1)} %broadcast_select_fusion.3), calls=%async_computation.1 | async-start | bytes 1048576 | tf_op jit(solution)/shard_map/all_to_all | solution.py:54
  112.0 123.0 %all-reduce.7.cloned.1.call-start = ((), (), s32[]{:S(2)}) async-start(), calls=%async_computation.6 | async-start | bytes 262144 | tf_op jit(solution)/shard_map/psum | solution.py:9
  149.7 2.8 copy-start.4
  152.6 2.3 copy-start.5
  239.3 16.4 %all-to-all-start.2 = ((bf16[16,128,128]{1,2,0:T(8,128)(2,1)}), bf16[16,128,128]{1,2,0:T(8,128)(2,1)}, u32[]{:S(2)}, u32[]{:S(2)}) async-start(bf16[16,128,128]{1,2,0:T(8,128)(2,1)} %broadcast_select_fusion.2), calls=%async_computation.2 | async-start | bytes 1048576 | tf_op jit(solution)/shard_map/all_to_all | solution.py:54
  246.2 123.3 %all-reduce.9.cloned.1.call-start = ((), (), s32[]{:S(2)}) async-start(), calls=%async_computation.7 | async-start | bytes 262144 | tf_op jit(solution)/shard_map/psum | solution.py:9
  246.2 41.5 %collective-permute-start.1 = (f32[512,128]{1,0:T(8,128)}, f32[512,128]{1,0:T(8,128)}, u32[]{:S(2)}, u32[]{:S(2)}) collective-permute-start(f32[512,128]{1,0:T(8,128)} %get-tuple-element.9), channel_id=1, source_target_pairs={{1,0},{2,1},{3,2},{4,3},{5,4},{6,5},{7,6},{8,7},{9,8},{10,9},{11,1... | collective-permute-start | bytes 786440 | tf_op jit(solution)/shard_map/ppermute | solution.py:15
  272.3 6.9 %copy-start.1 = (bf16[96,128,128]{2,0,1:T(8,128)(2,1)S(1)}, bf16[96,128,128]{2,0,1:T(8,128)(2,1)}, u32[]{:S(2)}) copy-start(bf16[96,128,128]{2,0,1:T(8,128)(2,1)} %copy.53) | copy-start | bytes 9437188
  373.8 16.4 %all-to-all-start.3 = ((bf16[16,128,128]{1,2,0:T(8,128)(2,1)}), bf16[16,128,128]{1,2,0:T(8,128)(2,1)}, u32[]{:S(2)}, u32[]{:S(2)}) async-start(bf16[16,128,128]{1,2,0:T(8,128)(2,1)} %broadcast_select_fusion.1), calls=%async_computation.3 | async-start | bytes 1048576 | tf_op jit(solution)/shard_map/all_to_all | solution.py:54
  380.8 123.4 %all-reduce.11.cloned.1.call-start = ((), (), s32[]{:S(2)}) async-start(), calls=%async_computation.8 | async-start | bytes 262144 | tf_op jit(solution)/shard_map/psum | solution.py:9
  380.8 41.5 %collective-permute-start.2 = (f32[512,128]{1,0:T(8,128)}, f32[512,128]{1,0:T(8,128)}, u32[]{:S(2)}, u32[]{:S(2)}) collective-permute-start(f32[512,128]{1,0:T(8,128)} %get-tuple-element.7), channel_id=1, source_target_pairs={{1,0},{2,1},{3,2},{4,3},{5,4},{6,5},{7,6},{8,7},{9,8},{10,9},{11,1... | collective-permute-start | bytes 786440 | tf_op jit(solution)/shard_map/ppermute | solution.py:15
  406.8 6.9 %copy-start.2 = (bf16[96,128,128]{2,0,1:T(8,128)(2,1)S(1)}, bf16[96,128,128]{2,0,1:T(8,128)(2,1)}, u32[]{:S(2)}) copy-start(bf16[96,128,128]{2,0,1:T(8,128)(2,1)} %copy.58) | copy-start | bytes 9437188
  422.2 93.3 %copy-start.6 = (bf16[4,128,128]{1,2,0:T(8,128)(2,1)S(1)}, bf16[4,128,128]{1,2,0:T(8,128)(2,1)}, u32[]{:S(2)}) copy-start(bf16[4,128,128]{1,2,0:T(8,128)(2,1)} %all-reduce.5.cloned.1.call-done) | copy-start | bytes 393220
  504.2 17.5 %copy-start.7 = (bf16[4,128,128]{1,2,0:T(8,128)(2,1)S(1)}, bf16[4,128,128]{1,2,0:T(8,128)(2,1)}, u32[]{:S(2)}) copy-start(bf16[4,128,128]{1,2,0:T(8,128)(2,1)} %all-reduce.11.cloned.1.call-done) | copy-start | bytes 393220
  508.6 16.4 %all-to-all-start.4 = ((bf16[16,128,128]{1,2,0:T(8,128)(2,1)}), bf16[16,128,128]{1,2,0:T(8,128)(2,1)}, u32[]{:S(2)}, u32[]{:S(2)}) async-start(bf16[16,128,128]{1,2,0:T(8,128)(2,1)} %broadcast_select_fusion), calls=%async_computation.4 | async-start | bytes 1048576 | tf_op jit(solution)/shard_map/all_to_all | solution.py:54
  518.4 37.9 %collective-permute-start.3 = (f32[512,128]{1,0:T(8,128)}, f32[512,128]{1,0:T(8,128)}, u32[]{:S(2)}, u32[]{:S(2)}) collective-permute-start(f32[512,128]{1,0:T(8,128)} %get-tuple-element.5), channel_id=1, source_target_pairs={{1,0},{2,1},{3,2},{4,3},{5,4},{6,5},{7,6},{8,7},{9,8},{10,9},{11,1... | collective-permute-start | bytes 786440 | tf_op jit(solution)/shard_map/ppermute | solution.py:15
  541.6 6.9 %copy-start.3 = (bf16[96,128,128]{2,0,1:T(8,128)(2,1)S(1)}, bf16[96,128,128]{2,0,1:T(8,128)(2,1)}, u32[]{:S(2)}) copy-start(bf16[96,128,128]{2,0,1:T(8,128)(2,1)} %copy.63) | copy-start | bytes 9437188
Sparse Core Ops, SparseCore 0:
  19.3 81.5 all-reduce.4
  156.3 78.6 all-reduce.6
  290.9 78.6 all-reduce.8
  425.5 78.6 all-reduce.10
where the time goes:
time: 568 us; the launch traced here: 564 us
  waiting for transfers between devices  335 us (59%)
  local copies, waits for them, and re-layouts  69.8 us (12%)
  matrix products  50.7 us (9%)
  starting transfers between devices  48.1 us (8%)
  other arithmetic  45.7 us (8%)
  between operations  14.6 us (3%)
    psum x4, waiting for transfers between devices, from_root(): return lax.psum(block, axis)  313 us
    dot_general x4, matrix products, per_device(): jnp.einsum('kij,kje->kie', interaction, picked, preferred_element_type=jn...  31.5 us
    all_to_all x4, starting transfers between devices, per_device(): lax.all_to_all(outgoing, 'rows', split_axis=0, concat_axis=0, tiled=True)  27.8 us
    convert_element_type x4, other arithmetic, place_rows(): low_part = (products - high_part.astype(jnp.float32)).astype(jnp.bfloat16)  27.3 us
    all_to_all x4, waiting for transfers between devices, per_device(): lax.all_to_all(outgoing, 'rows', split_axis=0, concat_axis=0, tiled=True)  21.9 us
    convert_element_type x4, local copies, waits for them, and re-layouts, place_rows(): low_part = (products - high_part.astype(jnp.float32)).astype(jnp.bfloat16)  19.7 us
    optimization_barrier x4, local copies, waits for them, and re-layouts, place_rows(): high_part = lax.optimization_barrier(products.astype(jnp.bfloat16))  19.6 us
    gather x4, local copies, waits for them, and re-layouts, per_device(): picked = jnp.take(arrived, source, axis=0)  15.1 us
  transfers between devices with their start and end apart: 13, of which 8 were waited for; matrix products, arithmetic and copies ran while one was open for 25% of the time, Pallas kernels for 0%

commit v1 on v0

v1 whole, which is shorter than its diff:
```python
import jax
import jax.numpy as jnp
from jax import lax
from jax.experimental import pallas as pl
from jax.experimental.pallas import tpu as pltpu
from jax.sharding import PartitionSpec as P

UNROLL = 8


def accumulate(meta, blocks, pieces, base, gathered, sums):
    rows = base.shape[0]
    for place, piece in enumerate(pieces):
        gathered[pl.ds(place * rows, rows)] = piece[...]
    sums[pl.ds(0, rows)] = base[...]
    slots = blocks.shape[0]

    def group(at, carry):
        for offset in range(UNROLL):
            slot = at * UNROLL + offset
            word = meta[slot]
            column = word >> 3
            row = word & 7
            sums[row] += jnp.dot(
                blocks[slot], gathered[column], preferred_element_type=jnp.float32
            )
        return carry

    lax.fori_loop(0, (meta[slots] + UNROLL - 1) // UNROLL, group, 0)


def solve_rows(inverse, right_side):
    return jnp.dot(
        inverse, right_side, precision=lax.Precision.HIGHEST, preferred_element_type=jnp.float32
    ).astype(jnp.bfloat16)


def first_kernel(excitation, base, inverse, solved):
    for b in range(base.shape[0]):
        solved[b] = solve_rows(inverse[b], excitation[b].astype(jnp.float32) - base[b])


def step_kernel(meta, blocks, *refs):
    *pieces, base, excitation, inverse, total, solved, gathered, sums = refs
    accumulate(meta, blocks, pieces, base, gathered, sums)
    for b in range(base.shape[0]):
        total[b] = sums[b]
        solved[b] = solve_rows(inverse[b], excitation[b].astype(jnp.float32) - sums[b])


def last_kernel(meta, blocks, *refs):
    *pieces, base, total, gathered, sums = refs
    accumulate(meta, blocks, pieces, base, gathered, sums)
    total[...] = sums[pl.ds(0, base.shape[0])]


def scratch(pieces, base):
    rows, size, width = base.shape
    return [
        pltpu.VMEM((len(pieces) * rows, size, width), jnp.bfloat16),
        pltpu.VMEM((8, size, width), jnp.float32),
    ]


SMEM = pl.BlockSpec(memory_space=pltpu.SMEM)
VMEM = pl.BlockSpec(memory_space=pltpu.VMEM)


def first_solve(excitation, base, inverse):
    return pl.pallas_call(
        first_kernel,
        out_shape=jax.ShapeDtypeStruct(base.shape, jnp.bfloat16),
        in_specs=[VMEM] * 3,
        out_specs=VMEM,
    )(excitation, base, inverse)


def step(meta, blocks, pieces, base, excitation, inverse):
    return pl.pallas_call(
        step_kernel,
        out_shape=(
            jax.ShapeDtypeStruct(base.shape, jnp.float32),
            jax.ShapeDtypeStruct(base.shape, jnp.bfloat16),
        ),
        in_specs=[SMEM] + [VMEM] * (len(pieces) + 4),
        out_specs=(VMEM, VMEM),
        scratch_shapes=scratch(pieces, base),
    )(meta, blocks, *pieces, base, excitation, inverse)


def product(meta, blocks, pieces, base):
    return pl.pallas_call(
        last_kernel,
        out_shape=jax.ShapeDtypeStruct(base.shape, jnp.float32),
        in_specs=[SMEM] + [VMEM] * (len(pieces) + 2),
        out_specs=VMEM,
        scratch_shapes=scratch(pieces, base),
    )(meta, blocks, *pieces, base)


def over_rows(value, flip):
    count = lax.axis_size("rows")
    return lax.ppermute(value, "rows", [(r, r ^ flip) for r in range(count)])


def exchange(own):
    half = lax.axis_size("rows") // 2
    near = [own] + [over_rows(own, 2 * z) for z in range(1, half)]
    return near + [over_rows(piece, 1) for piece in near]


LAG_ROUNDS = (
    [(0, 1)],
    [(0, 3), (1, 2)],
    [(x, x + 4) for x in range(4)],
    [(x, x + 12) for x in range(4)] + [(x + 4, x + 8) for x in range(4)],
)


def spread(value):
    lag = lax.axis_index("lag")
    for pairs in LAG_ROUNDS:
        arrived = lax.ppermute(value, "lag", pairs)
        takes = jnp.zeros((), jnp.bool_)
        for _, target in pairs:
            takes = takes | (lag == target)
        value = jnp.where(takes, arrived, value)
    return value


def from_behind(value):
    count = lax.axis_size("lag")
    return lax.ppermute(value, "lag", [(g + 1, g) for g in range(count - 1)])


def slot_words(slot_row, slot_owner, slot_pos, needed, count):
    slots = slot_row.shape[0]
    table = needed.reshape(-1)
    entry = slot_owner * needed.shape[-1] + slot_pos
    local = jnp.sum(
        jnp.where(entry[:, None] == jnp.arange(table.shape[0], dtype=jnp.int32)[None, :], table[None, :], 0),
        axis=1,
    )
    apart = slot_owner ^ lax.axis_index("rows")
    column = ((apart & 1) * 4 + (apart >> 1)) * 4 + local
    row = jnp.where(jnp.arange(slots, dtype=jnp.int32) < count, slot_row, 4)
    return jnp.concatenate([column * 8 + row, jnp.full((32,), count, jnp.int32)])


def per_device(
    excitation, pending, inverse, interaction, slot_row, slot_owner, slot_pos, needed, block_count
):
    row_blocks, block_size, _ = inverse.shape
    steps, rows, width = excitation.shape
    excitation_blocks = excitation.reshape(steps, row_blocks, block_size, width)
    meta = slot_words(slot_row, slot_owner, slot_pos, needed[0], block_count[0, 0])
    total = pending[0].reshape(row_blocks, block_size, width)
    solved = first_solve(excitation_blocks[0], total, inverse)
    outputs = []
    for t in range(steps):
        base = from_behind(total)
        solved = spread(solved)
        outputs.append(solved)
        pieces = exchange(solved)
        if t + 1 < steps:
            total, solved = step(meta, interaction, pieces, base, excitation_blocks[t + 1], inverse)
        else:
            total = product(meta, interaction, pieces, base)
    return (jnp.stack(outputs).reshape(steps, rows, width), total.reshape(1, rows, width))


def solution(mesh):
    in_specs = (
        P(None, "rows", None),
        P("lag", "rows", None),
        P("rows", None, None),
        P(("rows", "lag"), None, None),
        P(("rows", "lag")),
        P(("rows", "lag")),
        P(("rows", "lag")),
        P(("rows", "lag"), None, None),
        P("rows", "lag"),
    )
    out_specs = (P(None, "rows", None), P("lag", "rows", None))
    return jax.shard_map(
        per_device, mesh=mesh, in_specs=in_specs, out_specs=out_specs, check_vma=False
    )
```

time: 568 us -> 167 us (0.29)
  waiting for transfers between devices: 335 us -> 34.8 us
  local copies, waits for them, and re-layouts: 69.8 us -> 5.87 us
  matrix products: 50.7 us -> 0 us
  starting transfers between devices: 48.1 us -> 95 us
  other arithmetic: 45.7 us -> 5.78 us
  Pallas kernels: 0 us -> 24.1 us
  between operations: 14.6 us -> 2.12 us
    psum x4 -> x0, waiting for transfers between devices: 313 us -> none  [from_root(): return lax.psum(block, axis)]
    ppermute x4 -> x48, starting transfers between devices: 14.3 us -> 95 us  [the longest x28 57.4 us: over_rows(): return lax.ppermute(value, 'rows', [(r, r ^ flip) for r in range(count)])]
    dot_general x16 -> x0, matrix products: 50.7 us -> none  [the longest x4 31.5 us: per_device(): jnp.einsum('kij,kje->kie', interaction, picked, preferred_element_type=jn...]
    ppermute x4 -> x48, waiting for transfers between devices: 0.01 us -> 34.8 us  [the longest x16 32 us: spread(): arrived = lax.ppermute(value, 'lag', pairs)]
    all_to_all x5 -> x0, starting transfers between devices: 33.8 us -> none  [the longest x4 27.8 us: per_device(): lax.all_to_all(outgoing, 'rows', split_axis=0, concat_axis=0, tiled=True)]
    convert_element_type x4 -> x0, other arithmetic: 27.3 us -> none  [place_rows(): low_part = (products - high_part.astype(jnp.float32)).astype(jnp.bfloat16)]
    gather x8 -> x0, local copies, waits for them, and re-layouts: 24.4 us -> none  [the longest x4 15.1 us: per_device(): picked = jnp.take(arrived, source, axis=0)]
    pallas_call x0 -> x5, Pallas kernels: none -> 24.1 us  [the longest x3 16.8 us: step(): pl.pallas_call(step_kernel, out_shape=(jax.ShapeDtypeStruct(base.shape, j...]
  transfers between devices with their start and end apart: 13 -> 48, of which waited for: 8 -> 9; matrix products, arithmetic and copies ran while one was open for 25% -> 2% of each run, Pallas kernels for 0% -> 0%
where the time goes in v1:
time: 167 us; the launch traced here: 168 us
  starting transfers between devices  95 us (57%)
  waiting for transfers between devices  34.8 us (21%)
  Pallas kernels  24.1 us (14%)
  local copies, waits for them, and re-layouts  5.87 us (4%)
  other arithmetic  5.78 us (3%)
  between operations  2.12 us (1%)
    ppermute x28, starting transfers between devices, over_rows(): return lax.ppermute(value, 'rows', [(r, r ^ flip) for r in range(count)])  57.4 us
    ppermute x16, waiting for transfers between devices, spread(): arrived = lax.ppermute(value, 'lag', pairs)  32 us
    ppermute x4, starting transfers between devices, from_behind(): return lax.ppermute(value, 'lag', [(g + 1, g) for g in range(count - 1)])  24.4 us
    pallas_call x3, Pallas kernels, step(): pl.pallas_call(step_kernel, out_shape=(jax.ShapeDtypeStruct(base.shape, j...  16.8 us
    ppermute x16, starting transfers between devices, spread(): arrived = lax.ppermute(value, 'lag', pairs)  13.1 us
    pallas_call x1, Pallas kernels, product(): pl.pallas_call(last_kernel, out_shape=jax.ShapeDtypeStruct(base.shape, jn...  5.16 us
    select_n x16, other arithmetic, spread(): value = jnp.where(takes, arrived, value)  3.91 us
    unnamed x85, local copies, waits for them, and re-layouts  3.4 us
  transfers between devices with their start and end apart: 48, of which 9 were waited for; matrix products, arithmetic and copies ran while one was open for 2% of the time, Pallas kernels for 0%

profile of v1, /device:TPU:25, one launch (start us, length us, event | category | flops | bytes accessed | tf_op | source)
XLA Modules:
  0.0 167.6 jit_solution(6302091902221355710)
XLA Ops:
  0.7 1.9 %fusion.1 = (bf16[1,512,128]{2,1,0:T(8,128)(2,1)}, bf16[1,512,128]{2,1,0:T(8,128)(2,1)}, bf16[1,512,128]{2,1,0:T(8,128)(2,1)}, bf16[1,512,128]{2,1,0:T(8,128)(2,1)}) fusion(bf16[4,512,128]{2,1,0:T(8,128)(2,1)} %param.9), kind=kLoop, calls=%fused_computation.22 | loop fusion | bytes 1048576 | tf_op jit(solution)/shard_map/slice | solution.py:166
  2.6 2.1 %shard_map.104 = bf16[4,128,128]{2,1,0:T(8,128)(2,1)} custom-call(bf16[4,128,128]{2,1,0:T(8,128)(2,1)} %bitcast.20, f32[4,128,128]{2,1,0:T(8,128)} %bitcast.21, f32[4,128,128]{2,1,0:T(8,128)} %refs_10_.5), custom_call_target="tpu_custom_call" | custom-call | tf_op jit(solution)/shard_map/pallas_call | solution.py:70
  4.7 0.7 collective-permute-start
  5.4 0.9 broadcast_select_fusion.3
  6.3 0.7 collective-permute-start.1
  7.0 0.7 collective-permute-start.2
  7.8 1.3 collective-permute-start.3
  9.1 4.6 %collective-permute-start.11 = (f32[4,128,128]{2,1,0:T(8,128)}, f32[4,128,128]{2,1,0:T(8,128)S(1)}, u32[]{:S(2)}, u32[]{:S(2)}) collective-permute-start(f32[4,128,128]{2,1,0:T(8,128)} %bitcast.22), channel_id=1, source_target_pairs={{1,0},{2,1},{3,2},{4,3},{5,4},{6,5},{7,6},{8,7},{9,8},{10,9},{11,1... | collective-permute-start | bytes 786440 | tf_op jit(solution)/shard_map/ppermute | solution.py:133
  13.7 7.6 %collective-permute-done.3 = bf16[4,128,128]{2,1,0:T(8,128)(2,1)S(1)} collective-permute-done((bf16[4,128,128]{2,1,0:T(8,128)(2,1)S(1)}, bf16[4,128,128]{2,1,0:T(8,128)(2,1)S(1)}, u32[]{:S(2)}, u32[]{:S(2)}) %collective-permute-start.3) | collective-permute-done | bytes 131104 | tf_op jit(solution)/shard_map/ppermute | solution.py:123
  21.3 3.8 %collective-permute-start.6 = (bf16[4,128,128]{2,1,0:T(8,128)(2,1)S(1)}, bf16[4,128,128]{2,1,0:T(8,128)(2,1)S(1)}, u32[]{:S(2)}, u32[]{:S(2)}) collective-permute-start(bf16[4,128,128]{2,1,0:T(8,128)(2,1)S(1)} %broadcast_select_fusion.15.refs_0_), channel_id=1, source_target_pairs={{0,96},{16,112},{32,64},{48,80},{64,32},{80,48},{96,0},{112,16},{1... | collective-permute-start | bytes 393224 | tf_op jit(solution)/shard_map/ppermute | solution.py:103
  25.2 1.3 collective-permute-start.5
  27.4 4.2 %collective-permute-start.7 = (bf16[4,128,128]{2,1,0:T(8,128)(2,1)S(1)}, bf16[4,128,128]{2,1,0:T(8,128)(2,1)S(1)}, u32[]{:S(2)}, u32[]{:S(2)}) collective-permute-start(bf16[4,128,128]{2,1,0:T(8,128)(2,1)S(1)} %broadcast_select_fusion.15.refs_0_), channel_id=1, source_target_pairs={{0,16},{16,0},{32,48},{48,32},{64,80},{80,64},{96,112},{112,96},{1... | collective-permute-start | bytes 393224 | tf_op jit(solution)/shard_map/ppermute | solution.py:103
  31.5 1.0 collective-permute-start.10
  32.6 1.4 collective-permute-start.8
  33.9 1.5 collective-permute-start.9
  35.5 0.5 concatenate.4.meta
  37.1 5.6 %shard_map.105 = (f32[4,128,128]{2,1,0:T(8,128)}, bf16[4,128,128]{2,1,0:T(8,128)(2,1)}) custom-call(s32[128]{0:T(128)} %concatenate.4.meta, bf16[96,128,128]{2,1,0:T(8,128)(2,1)} %blocks.7, bf16[4,128,128]{2,1,0:T(8,128)(2,1)} %copy-done, bf16[4,128,128]{2,1,0:T(8,128)(2,1)} %copy-done.11, bf16[4,128,128]{2,1,0:T(8,128)(2,1)} %copy-done.12, ...), custom_call_target="tpu_custom_call" | custom-call | tf_op jit(solution)/shard_map/pallas_call | solution.py:79
  42.7 0.7 collective-permute-start.12
  43.3 0.9 broadcast_select_fusion.2
  44.3 0.7 collective-permute-start.13
  45.0 0.7 collective-permute-start.14
  45.7 1.3 collective-permute-start.15
  47.0 11.1 %collective-permute-done.15 = bf16[4,128,128]{2,1,0:T(8,128)(2,1)S(1)} collective-permute-done((bf16[4,128,128]{2,1,0:T(8,128)(2,1)S(1)}, bf16[4,128,128]{2,1,0:T(8,128)(2,1)S(1)}, u32[]{:S(2)}, u32[]{:S(2)}) %collective-permute-start.15) | collective-permute-done | bytes 131104 | tf_op jit(solution)/shard_map/ppermute | solution.py:123
  58.1 5.1 %collective-permute-start.16 = (bf16[4,128,128]{2,1,0:T(8,128)(2,1)S(1)}, bf16[4,128,128]{2,1,0:T(8,128)(2,1)S(1)}, u32[]{:S(2)}, u32[]{:S(2)}) collective-permute-start(bf16[4,128,128]{2,1,0:T(8,128)(2,1)S(1)} %broadcast_select_fusion.14.refs_0_), channel_id=1, source_target_pairs={{0,32},{16,48},{32,0},{48,16},{64,96},{80,112},{96,64},{112,80},{1... | collective-permute-start | bytes 393224 | tf_op jit(solution)/shard_map/ppermute | solution.py:103
  63.2 6.6 %collective-permute-start.23 = (f32[4,128,128]{2,1,0:T(8,128)}, f32[4,128,128]{2,1,0:T(8,128)S(1)}, u32[]{:S(2)}, u32[]{:S(2)}) collective-permute-start(f32[4,128,128]{2,1,0:T(8,128)} %get-tuple-element.9), channel_id=1, source_target_pairs={{1,0},{2,1},{3,2},{4,3},{5,4},{6,5},{7,6},{8,7},{9,8},{10,9},{11,1... | collective-permute-start | bytes 786440 | tf_op jit(solution)/shard_map/ppermute | solution.py:133
  69.8 1.4 collective-permute-start.17
  71.2 1.1 collective-permute-start.18
  72.3 2.6 %collective-permute-start.19 = (bf16[4,128,128]{2,1,0:T(8,128)(2,1)S(1)}, bf16[4,128,128]{2,1,0:T(8,128)(2,1)S(1)}, u32[]{:S(2)}, u32[]{:S(2)}) collective-permute-start(bf16[4,128,128]{2,1,0:T(8,128)(2,1)S(1)} %broadcast_select_fusion.14.refs_0_), channel_id=1, source_target_pairs={{0,16},{16,0},{32,48},{48,32},{64,80},{80,64},{96,112},{112,96},{1... | collective-permute-start | bytes 393224 | tf_op jit(solution)/shard_map/ppermute | solution.py:103
  75.3 3.5 %collective-permute-start.21 = (bf16[4,128,128]{2,1,0:T(8,128)(2,1)S(1)}, bf16[4,128,128]{2,1,0:T(8,128)(2,1)S(1)}, u32[]{:S(2)}, u32[]{:S(2)}) collective-permute-start(bf16[4,128,128]{2,1,0:T(8,128)(2,1)S(1)} %collective-permute-done.17.refs_2_), channel_id=1, source_target_pairs={{0,16},{16,0},{32,48},{48,32},{64,80},{80,64},{96,112},{112,96},{1... | collective-permute-start | bytes 393224 | tf_op jit(solution)/shard_map/ppermute | solution.py:103
  78.7 1.8 %collective-permute-start.22 = (bf16[4,128,128]{2,1,0:T(8,128)(2,1)S(1)}, bf16[4,128,128]{2,1,0:T(8,128)(2,1)S(1)}, u32[]{:S(2)}, u32[]{:S(2)}) collective-permute-start(bf16[4,128,128]{2,1,0:T(8,128)(2,1)S(1)} %collective-permute-done.18.refs_3_), channel_id=1, source_target_pairs={{0,16},{16,0},{32,48},{48,32},{64,80},{80,64},{96,112},{112,96},{1... | collective-permute-start | bytes 393224 | tf_op jit(solution)/shard_map/ppermute | solution.py:103
  80.6 0.9 collective-permute-done.22.refs_7_
  81.6 0.6 copy-done.37
  82.2 5.6 %shard_map.106 = (f32[4,128,128]{2,1,0:T(8,128)}, bf16[4,128,128]{2,1,0:T(8,128)(2,1)}) custom-call(s32[128]{0:T(128)} %concatenate.4.meta, bf16[96,128,128]{2,1,0:T(8,128)(2,1)} %blocks.7, bf16[4,128,128]{2,1,0:T(8,128)(2,1)} %copy-done.2, bf16[4,128,128]{2,1,0:T(8,128)(2,1)} %copy-done.15, bf16[4,128,128]{2,1,0:T(8,128)(2,1)} %copy-done.18, ...), custom_call_target="tpu_custom_call" | custom-call | tf_op jit(solution)/shard_map/pallas_call | solution.py:79
  87.8 0.7 collective-permute-start.24
  88.5 0.9 broadcast_select_fusion.1
  89.4 0.7 collective-permute-start.25
  90.1 0.7 collective-permute-start.26
  90.8 1.3 collective-permute-start.27
  92.1 6.6 %collective-permute-done.27 = bf16[4,128,128]{2,1,0:T(8,128)(2,1)S(1)} collective-permute-done((bf16[4,128,128]{2,1,0:T(8,128)(2,1)S(1)}, bf16[4,128,128]{2,1,0:T(8,128)(2,1)S(1)}, u32[]{:S(2)}, u32[]{:S(2)}) %collective-permute-start.27) | collective-permute-done | bytes 131104 | tf_op jit(solution)/shard_map/ppermute | solution.py:123
  98.8 1.3 collective-permute-start.28
  100.0 6.6 %collective-permute-start.35 = (f32[4,128,128]{2,1,0:T(8,128)}, f32[4,128,128]{2,1,0:T(8,128)S(1)}, u32[]{:S(2)}, u32[]{:S(2)}) collective-permute-start(f32[4,128,128]{2,1,0:T(8,128)} %get-tuple-element.11), channel_id=1, source_target_pairs={{1,0},{2,1},{3,2},{4,3},{5,4},{6,5},{7,6},{8,7},{9,8},{10,9},{11,1... | collective-permute-start | bytes 786440 | tf_op jit(solution)/shard_map/ppermute | solution.py:133
  106.7 3.1 %collective-permute-start.29 = (bf16[4,128,128]{2,1,0:T(8,128)(2,1)S(1)}, bf16[4,128,128]{2,1,0:T(8,128)(2,1)S(1)}, u32[]{:S(2)}, u32[]{:S(2)}) collective-permute-start(bf16[4,128,128]{2,1,0:T(8,128)(2,1)S(1)} %broadcast_select_fusion.13.refs_0_), channel_id=1, source_target_pairs={{0,64},{16,80},{32,96},{48,112},{64,0},{80,16},{96,32},{112,48},{1... | collective-permute-start | bytes 393224 | tf_op jit(solution)/shard_map/ppermute | solution.py:103
  109.8 5.1 %collective-permute-start.31 = (bf16[4,128,128]{2,1,0:T(8,128)(2,1)S(1)}, bf16[4,128,128]{2,1,0:T(8,128)(2,1)S(1)}, u32[]{:S(2)}, u32[]{:S(2)}) collective-permute-start(bf16[4,128,128]{2,1,0:T(8,128)(2,1)S(1)} %broadcast_select_fusion.13.refs_0_), channel_id=1, source_target_pairs={{0,16},{16,0},{32,48},{48,32},{64,80},{80,64},{96,112},{112,96},{1... | collective-permute-start | bytes 393224 | tf_op jit(solution)/shard_map/ppermute | solution.py:103
  114.9 1.8 %collective-permute-start.33 = (bf16[4,128,128]{2,1,0:T(8,128)(2,1)S(1)}, bf16[4,128,128]{2,1,0:T(8,128)(2,1)S(1)}, u32[]{:S(2)}, u32[]{:S(2)}) collective-permute-start(bf16[4,128,128]{2,1,0:T(8,128)(2,1)S(1)} %collective-permute-done.29.refs_2_), channel_id=1, source_target_pairs={{0,16},{16,0},{32,48},{48,32},{64,80},{80,64},{96,112},{112,96},{1... | collective-permute-start | bytes 393224 | tf_op jit(solution)/shard_map/ppermute | solution.py:103
  116.7 2.4 %collective-permute-start.34 = (bf16[4,128,128]{2,1,0:T(8,128)(2,1)S(1)}, bf16[4,128,128]{2,1,0:T(8,128)(2,1)S(1)}, u32[]{:S(2)}, u32[]{:S(2)}) collective-permute-start(bf16[4,128,128]{2,1,0:T(8,128)(2,1)S(1)} %collective-permute-done.30.refs_3_), channel_id=1, source_target_pairs={{0,16},{16,0},{32,48},{48,32},{64,80},{80,64},{96,112},{112,96},{1... | collective-permute-start | bytes 393224 | tf_op jit(solution)/shard_map/ppermute | solution.py:103
  119.2 0.9 collective-permute-done.34.refs_7_
  120.2 0.6 copy-done.36
  120.8 5.6 %shard_map.107 = (f32[4,128,128]{2,1,0:T(8,128)}, bf16[4,128,128]{2,1,0:T(8,128)(2,1)}) custom-call(s32[128]{0:T(128)} %concatenate.4.meta, bf16[96,128,128]{2,1,0:T(8,128)(2,1)} %blocks.7, bf16[4,128,128]{2,1,0:T(8,128)(2,1)} %copy-done.4, bf16[4,128,128]{2,1,0:T(8,128)(2,1)} %copy-done.14, bf16[4,128,128]{2,1,0:T(8,128)(2,1)} %copy-done.17, ...), custom_call_target="tpu_custom_call" | custom-call | tf_op jit(solution)/shard_map/pallas_call | solution.py:79
  126.4 0.7 collective-permute-start.36
  127.1 0.9 broadcast_select_fusion
  128.0 0.7 collective-permute-start.37
  128.7 0.7 collective-permute-start.38
  129.4 1.3 collective-permute-start.39
  130.7 6.6 %collective-permute-done.39 = bf16[4,128,128]{2,1,0:T(8,128)(2,1)S(1)} collective-permute-done((bf16[4,128,128]{2,1,0:T(8,128)(2,1)S(1)}, bf16[4,128,128]{2,1,0:T(8,128)(2,1)S(1)}, u32[]{:S(2)}, u32[]{:S(2)}) %collective-permute-start.39) | collective-permute-done | bytes 131104 | tf_op jit(solution)/shard_map/ppermute | solution.py:123
  137.4 3.0 %collective-permute-start.40 = (bf16[4,128,128]{2,1,0:T(8,128)(2,1)S(1)}, bf16[4,128,128]{2,1,0:T(8,128)(2,1)S(1)}, u32[]{:S(2)}, u32[]{:S(2)}) collective-permute-start(bf16[4,128,128]{2,1,0:T(8,128)(2,1)S(1)} %broadcast_select_fusion.12.refs_0_), channel_id=1, source_target_pairs={{0,32},{16,48},{32,0},{48,16},{64,96},{80,112},{96,64},{112,80},{1... | collective-permute-start | bytes 393224 | tf_op jit(solution)/shard_map/ppermute | solution.py:103
  140.4 6.6 %collective-permute-start.47 = (f32[4,128,128]{2,1,0:T(8,128)}, f32[4,128,128]{2,1,0:T(8,128)S(1)}, u32[]{:S(2)}, u32[]{:S(2)}) collective-permute-start(f32[4,128,128]{2,1,0:T(8,128)} %get-tuple-element.13), channel_id=1, source_target_pairs={{1,0},{2,1},{3,2},{4,3},{5,4},{6,5},{7,6},{8,7},{9,8},{10,9},{11,1... | collective-permute-start | bytes 786440 | tf_op jit(solution)/shard_map/ppermute | solution.py:133
  147.0 2.8 %collective-permute-start.41 = (bf16[4,128,128]{2,1,0:T(8,128)(2,1)S(1)}, bf16[4,128,128]{2,1,0:T(8,128)(2,1)S(1)}, u32[]{:S(2)}, u32[]{:S(2)}) collective-permute-start(bf16[4,128,128]{2,1,0:T(8,128)(2,1)S(1)} %broadcast_select_fusion.12.refs_0_), channel_id=1, source_target_pairs={{0,64},{16,80},{32,96},{48,112},{64,0},{80,16},{96,32},{112,48},{1... | collective-permute-start | bytes 393224 | tf_op jit(solution)/shard_map/ppermute | solution.py:103
  149.8 3.6 %collective-permute-start.43 = (bf16[4,128,128]{2,1,0:T(8,128)(2,1)S(1)}, bf16[4,128,128]{2,1,0:T(8,128)(2,1)S(1)}, u32[]{:S(2)}, u32[]{:S(2)}) collective-permute-start(bf16[4,128,128]{2,1,0:T(8,128)(2,1)S(1)} %broadcast_select_fusion.12.refs_0_), channel_id=1, source_target_pairs={{0,16},{16,0},{32,48},{48,32},{64,80},{80,64},{96,112},{112,96},{1... | collective-permute-start | bytes 393224 | tf_op jit(solution)/shard_map/ppermute | solution.py:103
  153.5 2.5 %collective-permute-start.45 = (bf16[4,128,128]{2,1,0:T(8,128)(2,1)S(1)}, bf16[4,128,128]{2,1,0:T(8,128)(2,1)S(1)}, u32[]{:S(2)}, u32[]{:S(2)}) collective-permute-start(bf16[4,128,128]{2,1,0:T(8,128)(2,1)S(1)} %collective-permute-done.41.refs_2_), channel_id=1, source_target_pairs={{0,16},{16,0},{32,48},{48,32},{64,80},{80,64},{96,112},{112,96},{1... | collective-permute-start | bytes 393224 | tf_op jit(solution)/shard_map/ppermute | solution.py:103
  156.3 2.9 %collective-permute-start.46 = (bf16[4,128,128]{2,1,0:T(8,128)(2,1)S(1)}, bf16[4,128,128]{2,1,0:T(8,128)(2,1)S(1)}, u32[]{:S(2)}, u32[]{:S(2)}) collective-permute-start(bf16[4,128,128]{2,1,0:T(8,128)(2,1)S(1)} %collective-permute-done.42.refs_3_), channel_id=1, source_target_pairs={{0,16},{16,0},{32,48},{48,32},{64,80},{80,64},{96,112},{112,96},{1... | collective-permute-start | bytes 393224 | tf_op jit(solution)/shard_map/ppermute | solution.py:103
  159.2 1.8 %pad_maximum_fusion = bf16[4,512,128]{2,1,0:T(8,128)(2,1)} fusion(bf16[1,512,128]{2,1,0:T(8,128)(2,1)S(1)} %bitcast.16, bf16[1,512,128]{2,1,0:T(8,128)(2,1)} %bitcast.15, bf16[1,512,128]{2,1,0:T(8,128)(2,1)S(1)} %bitcast.14, bf16[1,512,128]{2,1,0:T(8,128)(2,1)S(1)} %bitcast.13), kind=kLoop, calls=%fused_computation | loop fusion | flops 786432 | bytes 1048576 | tf_op jit(solution)/shard_map/stack | solution.py:169
  161.1 0.6 copy-done.7
  161.8 0.6 copy-done.35
  162.5 5.2 %shard_map.108 = f32[4,128,128]{2,1,0:T(8,128)} custom-call(s32[128]{0:T(128)} %concatenate.4.meta, bf16[96,128,128]{2,1,0:T(8,128)(2,1)} %blocks.7, bf16[4,128,128]{2,1,0:T(8,128)(2,1)} %copy-done.5, bf16[4,128,128]{2,1,0:T(8,128)(2,1)} %copy-done.13, bf16[4,128,128]{2,1,0:T(8,128)(2,1)} %copy-done.16, bf16[4,128,128]{2,1,0:T(8,128)(2,1)} %copy-done.19, ...), custom_call_target="tpu_custom_call" | custom-call | tf_op jit(solution)/shard_map/pallas_call | solution.py:92
  (145 shorter events, 2.7 us)
Async XLA Ops:
  0.6 25.8 %copy-start.40 = (s32[96]{0:T(128)S(1)}, s32[96]{0:T(128)}, u32[]{:S(2)}) copy-start(s32[96]{0:T(128)} %param.14) | copy-start | bytes 1156
  0.6 25.8 %copy-start.41 = (s32[96]{0:T(128)S(1)}, s32[96]{0:T(128)}, u32[]{:S(2)}) copy-start(s32[96]{0:T(128)} %param.15) | copy-start | bytes 1156
  0.7 25.8 %copy-start.38 = (s32[1,8,2]{1,2,0:T(2,128)S(1)}, s32[1,8,2]{1,2,0:T(2,128)}, u32[]{:S(2)}) copy-start(s32[1,8,2]{1,2,0:T(2,128)} %param.16) | copy-start | bytes 196
  0.7 34.8 %copy-start.39 = (s32[96]{0:T(128)S(1)}, s32[96]{0:T(128)}, u32[]{:S(2)}) copy-start(s32[96]{0:T(128)} %param.13) | copy-start | bytes 1156
  4.7 0.7 collective-permute-start
  6.3 0.7 collective-permute-start.1
  7.0 0.7 collective-permute-start.2
  7.8 13.5 %collective-permute-start.3 = (bf16[4,128,128]{2,1,0:T(8,128)(2,1)S(1)}, bf16[4,128,128]{2,1,0:T(8,128)(2,1)S(1)}, u32[]{:S(2)}, u32[]{:S(2)}) collective-permute-start(bf16[4,128,128]{2,1,0:T(8,128)(2,1)S(1)} %broadcast_select_fusion.11), channel_id=1, source_target_pairs={{0,12},{1,13},{2,14},{3,15},{4,8},{5,9},{6,10},{7,11},{16,28},{17,... | collective-permute-start | bytes 393224 | tf_op jit(solution)/shard_map/ppermute | solution.py:123
  9.1 26.9 %collective-permute-start.11 = (f32[4,128,128]{2,1,0:T(8,128)}, f32[4,128,128]{2,1,0:T(8,128)S(1)}, u32[]{:S(2)}, u32[]{:S(2)}) collective-permute-start(f32[4,128,128]{2,1,0:T(8,128)} %bitcast.22), channel_id=1, source_target_pairs={{1,0},{2,1},{3,2},{4,3},{5,4},{6,5},{7,6},{8,7},{9,8},{10,9},{11,1... | collective-permute-start | bytes 786440 | tf_op jit(solution)/shard_map/ppermute | solution.py:133
  21.3 15.1 %copy-start = (bf16[4,128,128]{2,1,0:T(8,128)(2,1)}, bf16[4,128,128]{2,1,0:T(8,128)(2,1)S(1)}, u32[]{:S(2)}) copy-start(bf16[4,128,128]{2,1,0:T(8,128)(2,1)S(1)} %broadcast_select_fusion.15.refs_0_) | copy-start | bytes 393220
  21.3 10.2 %collective-permute-start.6 = (bf16[4,128,128]{2,1,0:T(8,128)(2,1)S(1)}, bf16[4,128,128]{2,1,0:T(8,128)(2,1)S(1)}, u32[]{:S(2)}, u32[]{:S(2)}) collective-permute-start(bf16[4,128,128]{2,1,0:T(8,128)(2,1)S(1)} %broadcast_select_fusion.15.refs_0_), channel_id=1, source_target_pairs={{0,96},{16,112},{32,64},{48,80},{64,32},{80,48},{96,0},{112,16},{1... | collective-permute-start | bytes 393224 | tf_op jit(solution)/shard_map/ppermute | solution.py:103
  25.1 7.4 %collective-permute-start.4 = (bf16[4,128,128]{2,1,0:T(8,128)(2,1)S(1)}, bf16[4,128,128]{2,1,0:T(8,128)(2,1)S(1)}, u32[]{:S(2)}, u32[]{:S(2)}) collective-permute-start(bf16[4,128,128]{2,1,0:T(8,128)(2,1)S(1)} %broadcast_select_fusion.15.refs_0_), channel_id=1, source_target_pairs={{0,32},{16,48},{32,0},{48,16},{64,96},{80,112},{96,64},{112,80},{1... | collective-permute-start | bytes 393224 | tf_op jit(solution)/shard_map/ppermute | solution.py:103
  25.2 8.8 %collective-permute-start.5 = (bf16[4,128,128]{2,1,0:T(8,128)(2,1)S(1)}, bf16[4,128,128]{2,1,0:T(8,128)(2,1)S(1)}, u32[]{:S(2)}, u32[]{:S(2)}) collective-permute-start(bf16[4,128,128]{2,1,0:T(8,128)(2,1)S(1)} %broadcast_select_fusion.15.refs_0_), channel_id=1, source_target_pairs={{0,64},{16,80},{32,96},{48,112},{64,0},{80,16},{96,32},{112,48},{1... | collective-permute-start | bytes 393224 | tf_op jit(solution)/shard_map/ppermute | solution.py:103
  27.4 8.6 %collective-permute-start.7 = (bf16[4,128,128]{2,1,0:T(8,128)(2,1)S(1)}, bf16[4,128,128]{2,1,0:T(8,128)(2,1)S(1)}, u32[]{:S(2)}, u32[]{:S(2)}) collective-permute-start(bf16[4,128,128]{2,1,0:T(8,128)(2,1)S(1)} %broadcast_select_fusion.15.refs_0_), channel_id=1, source_target_pairs={{0,16},{16,0},{32,48},{48,32},{64,80},{80,64},{96,112},{112,96},{1... | collective-permute-start | bytes 393224 | tf_op jit(solution)/shard_map/ppermute | solution.py:103
  31.5 4.4 %collective-permute-start.10 = (bf16[4,128,128]{2,1,0:T(8,128)(2,1)S(1)}, bf16[4,128,128]{2,1,0:T(8,128)(2,1)S(1)}, u32[]{:S(2)}, u32[]{:S(2)}) collective-permute-start(bf16[4,128,128]{2,1,0:T(8,128)(2,1)S(1)} %collective-permute-done.6.refs_3_), channel_id=1, source_target_pairs={{0,16},{16,0},{32,48},{48,32},{64,80},{80,64},{96,112},{112,96},{1... | collective-permute-start | bytes 393224 | tf_op jit(solution)/shard_map/ppermute | solution.py:103
  32.6 3.4 %collective-permute-start.8 = (bf16[4,128,128]{2,1,0:T(8,128)(2,1)S(1)}, bf16[4,128,128]{2,1,0:T(8,128)(2,1)S(1)}, u32[]{:S(2)}, u32[]{:S(2)}) collective-permute-start(bf16[4,128,128]{2,1,0:T(8,128)(2,1)S(1)} %collective-permute-done.4.refs_1_), channel_id=1, source_target_pairs={{0,16},{16,0},{32,48},{48,32},{64,80},{80,64},{96,112},{112,96},{1... | collective-permute-start | bytes 393224 | tf_op jit(solution)/shard_map/ppermute | solution.py:103
  33.9 2.5 %collective-permute-start.9 = (bf16[4,128,128]{2,1,0:T(8,128)(2,1)S(1)}, bf16[4,128,128]{2,1,0:T(8,128)(2,1)S(1)}, u32[]{:S(2)}, u32[]{:S(2)}) collective-permute-start(bf16[4,128,128]{2,1,0:T(8,128)(2,1)S(1)} %collective-permute-done.5.refs_2_), channel_id=1, source_target_pairs={{0,16},{16,0},{32,48},{48,32},{64,80},{80,64},{96,112},{112,96},{1... | collective-permute-start | bytes 393224 | tf_op jit(solution)/shard_map/ppermute | solution.py:103
  42.7 0.7 collective-permute-start.12
  44.3 0.7 collective-permute-start.13
  45.0 0.7 collective-permute-start.14
  45.7 12.4 %collective-permute-start.15 = (bf16[4,128,128]{2,1,0:T(8,128)(2,1)S(1)}, bf16[4,128,128]{2,1,0:T(8,128)(2,1)S(1)}, u32[]{:S(2)}, u32[]{:S(2)}) collective-permute-start(bf16[4,128,128]{2,1,0:T(8,128)(2,1)S(1)} %broadcast_select_fusion.10), channel_id=1, source_target_pairs={{0,12},{1,13},{2,14},{3,15},{4,8},{5,9},{6,10},{7,11},{16,28},{17,... | collective-permute-start | bytes 393224 | tf_op jit(solution)/shard_map/ppermute | solution.py:123
  58.1 23.4 %copy-start.2 = (bf16[4,128,128]{2,1,0:T(8,128)(2,1)}, bf16[4,128,128]{2,1,0:T(8,128)(2,1)S(1)}, u32[]{:S(2)}) copy-start(bf16[4,128,128]{2,1,0:T(8,128)(2,1)S(1)} %broadcast_select_fusion.14.refs_0_) | copy-start | bytes 393220
  58.1 16.8 %collective-permute-start.16 = (bf16[4,128,128]{2,1,0:T(8,128)(2,1)S(1)}, bf16[4,128,128]{2,1,0:T(8,128)(2,1)S(1)}, u32[]{:S(2)}, u32[]{:S(2)}) collective-permute-start(bf16[4,128,128]{2,1,0:T(8,128)(2,1)S(1)} %broadcast_select_fusion.14.refs_0_), channel_id=1, source_target_pairs={{0,32},{16,48},{32,0},{48,16},{64,96},{80,112},{96,64},{112,80},{1... | collective-permute-start | bytes 393224 | tf_op jit(solution)/shard_map/ppermute | solution.py:103
  63.2 17.4 %collective-permute-start.23 = (f32[4,128,128]{2,1,0:T(8,128)}, f32[4,128,128]{2,1,0:T(8,128)S(1)}, u32[]{:S(2)}, u32[]{:S(2)}) collective-permute-start(f32[4,128,128]{2,1,0:T(8,128)} %get-tuple-element.9), channel_id=1, source_target_pairs={{1,0},{2,1},{3,2},{4,3},{5,4},{6,5},{7,6},{8,7},{9,8},{10,9},{11,1... | collective-permute-start | bytes 786440 | tf_op jit(solution)/shard_map/ppermute | solution.py:133
  69.8 5.4 %collective-permute-start.17 = (bf16[4,128,128]{2,1,0:T(8,128)(2,1)S(1)}, bf16[4,128,128]{2,1,0:T(8,128)(2,1)S(1)}, u32[]{:S(2)}, u32[]{:S(2)}) collective-permute-start(bf16[4,128,128]{2,1,0:T(8,128)(2,1)S(1)} %broadcast_select_fusion.14.refs_0_), channel_id=1, source_target_pairs={{0,64},{16,80},{32,96},{48,112},{64,0},{80,16},{96,32},{112,48},{1... | collective-permute-start | bytes 393224 | tf_op jit(solution)/shard_map/ppermute | solution.py:103
  71.2 7.5 %collective-permute-start.18 = (bf16[4,128,128]{2,1,0:T(8,128)(2,1)S(1)}, bf16[4,128,128]{2,1,0:T(8,128)(2,1)S(1)}, u32[]{:S(2)}, u32[]{:S(2)}) collective-permute-start(bf16[4,128,128]{2,1,0:T(8,128)(2,1)S(1)} %broadcast_select_fusion.14.refs_0_), channel_id=1, source_target_pairs={{0,96},{16,112},{32,64},{48,80},{64,32},{80,48},{96,0},{112,16},{1... | collective-permute-start | bytes 393224 | tf_op jit(solution)/shard_map/ppermute | solution.py:103
  72.3 8.3 %collective-permute-start.19 = (bf16[4,128,128]{2,1,0:T(8,128)(2,1)S(1)}, bf16[4,128,128]{2,1,0:T(8,128)(2,1)S(1)}, u32[]{:S(2)}, u32[]{:S(2)}) collective-permute-start(bf16[4,128,128]{2,1,0:T(8,128)(2,1)S(1)} %broadcast_select_fusion.14.refs_0_), channel_id=1, source_target_pairs={{0,16},{16,0},{32,48},{48,32},{64,80},{80,64},{96,112},{112,96},{1... | collective-permute-start | bytes 393224 | tf_op jit(solution)/shard_map/ppermute | solution.py:103
  74.9 6.7 %copy-start.15 = (bf16[4,128,128]{2,1,0:T(8,128)(2,1)}, bf16[4,128,128]{2,1,0:T(8,128)(2,1)S(1)}, u32[]{:S(2)}) copy-start(bf16[4,128,128]{2,1,0:T(8,128)(2,1)S(1)} %collective-permute-done.16.refs_1_) | copy-start | bytes 393220
  74.9 5.7 %collective-permute-start.20 = (bf16[4,128,128]{2,1,0:T(8,128)(2,1)S(1)}, bf16[4,128,128]{2,1,0:T(8,128)(2,1)S(1)}, u32[]{:S(2)}, u32[]{:S(2)}) collective-permute-start(bf16[4,128,128]{2,1,0:T(8,128)(2,1)S(1)} %collective-permute-done.16.refs_1_), channel_id=1, source_target_pairs={{0,16},{16,0},{32,48},{48,32},{64,80},{80,64},{96,112},{112,96},{1... | collective-permute-start | bytes 393224 | tf_op jit(solution)/shard_map/ppermute | solution.py:103
  75.2 6.3 %copy-start.18 = (bf16[4,128,128]{2,1,0:T(8,128)(2,1)}, bf16[4,128,128]{2,1,0:T(8,128)(2,1)S(1)}, u32[]{:S(2)}) copy-start(bf16[4,128,128]{2,1,0:T(8,128)(2,1)S(1)} %collective-permute-done.17.refs_2_) | copy-start | bytes 393220
  75.3 5.3 %collective-permute-start.21 = (bf16[4,128,128]{2,1,0:T(8,128)(2,1)S(1)}, bf16[4,128,128]{2,1,0:T(8,128)(2,1)S(1)}, u32[]{:S(2)}, u32[]{:S(2)}) collective-permute-start(bf16[4,128,128]{2,1,0:T(8,128)(2,1)S(1)} %collective-permute-done.17.refs_2_), channel_id=1, source_target_pairs={{0,16},{16,0},{32,48},{48,32},{64,80},{80,64},{96,112},{112,96},{1... | collective-permute-start | bytes 393224 | tf_op jit(solution)/shard_map/ppermute | solution.py:103
  78.7 2.8 %collective-permute-start.22 = (bf16[4,128,128]{2,1,0:T(8,128)(2,1)S(1)}, bf16[4,128,128]{2,1,0:T(8,128)(2,1)S(1)}, u32[]{:S(2)}, u32[]{:S(2)}) collective-permute-start(bf16[4,128,128]{2,1,0:T(8,128)(2,1)S(1)} %collective-permute-done.18.refs_3_), channel_id=1, source_target_pairs={{0,16},{16,0},{32,48},{48,32},{64,80},{80,64},{96,112},{112,96},{1... | collective-permute-start | bytes 393224 | tf_op jit(solution)/shard_map/ppermute | solution.py:103
  87.8 0.7 collective-permute-start.24
  89.4 0.7 collective-permute-start.25
  90.1 0.7 collective-permute-start.26
  90.8 7.9 %collective-permute-start.27 = (bf16[4,128,128]{2,1,0:T(8,128)(2,1)S(1)}, bf16[4,128,128]{2,1,0:T(8,128)(2,1)S(1)}, u32[]{:S(2)}, u32[]{:S(2)}) collective-permute-start(bf16[4,128,128]{2,1,0:T(8,128)(2,1)S(1)} %broadcast_select_fusion.9), channel_id=1, source_target_pairs={{0,12},{1,13},{2,14},{3,15},{4,8},{5,9},{6,10},{7,11},{16,28},{17,... | collective-permute-start | bytes 393224 | tf_op jit(solution)/shard_map/ppermute | solution.py:123
  98.7 21.4 %copy-start.4 = (bf16[4,128,128]{2,1,0:T(8,128)(2,1)}, bf16[4,128,128]{2,1,0:T(8,128)(2,1)S(1)}, u32[]{:S(2)}) copy-start(bf16[4,128,128]{2,1,0:T(8,128)(2,1)S(1)} %broadcast_select_fusion.13.refs_0_) | copy-start | bytes 393220
  98.8 16.1 %collective-permute-start.28 = (bf16[4,128,128]{2,1,0:T(8,128)(2,1)S(1)}, bf16[4,128,128]{2,1,0:T(8,128)(2,1)S(1)}, u32[]{:S(2)}, u32[]{:S(2)}) collective-permute-start(bf16[4,128,128]{2,1,0:T(8,128)(2,1)S(1)} %broadcast_select_fusion.13.refs_0_), channel_id=1, source_target_pairs={{0,32},{16,48},{32,0},{48,16},{64,96},{80,112},{96,64},{112,80},{1... | collective-permute-start | bytes 393224 | tf_op jit(solution)/shard_map/ppermute | solution.py:103
  100.0 19.1 %collective-permute-start.35 = (f32[4,128,128]{2,1,0:T(8,128)}, f32[4,128,128]{2,1,0:T(8,128)S(1)}, u32[]{:S(2)}, u32[]{:S(2)}) collective-permute-start(f32[4,128,128]{2,1,0:T(8,128)} %get-tuple-element.11), channel_id=1, source_target_pairs={{1,0},{2,1},{3,2},{4,3},{5,4},{6,5},{7,6},{8,7},{9,8},{10,9},{11,1... | collective-permute-start | bytes 786440 | tf_op jit(solution)/shard_map/ppermute | solution.py:133
  106.7 8.3 %collective-permute-start.29 = (bf16[4,128,128]{2,1,0:T(8,128)(2,1)S(1)}, bf16[4,128,128]{2,1,0:T(8,128)(2,1)S(1)}, u32[]{:S(2)}, u32[]{:S(2)}) collective-permute-start(bf16[4,128,128]{2,1,0:T(8,128)(2,1)S(1)} %broadcast_select_fusion.13.refs_0_), channel_id=1, source_target_pairs={{0,64},{16,80},{32,96},{48,112},{64,0},{80,16},{96,32},{112,48},{1... | collective-permute-start | bytes 393224 | tf_op jit(solution)/shard_map/ppermute | solution.py:103
  109.8 7.0 %collective-permute-start.30 = (bf16[4,128,128]{2,1,0:T(8,128)(2,1)S(1)}, bf16[4,128,128]{2,1,0:T(8,128)(2,1)S(1)}, u32[]{:S(2)}, u32[]{:S(2)}) collective-permute-start(bf16[4,128,128]{2,1,0:T(8,128)(2,1)S(1)} %broadcast_select_fusion.13.refs_0_), channel_id=1, source_target_pairs={{0,96},{16,112},{32,64},{48,80},{64,32},{80,48},{96,0},{112,16},{1... | collective-permute-start | bytes 393224 | tf_op jit(solution)/shard_map/ppermute | solution.py:103
  109.8 9.4 %collective-permute-start.31 = (bf16[4,128,128]{2,1,0:T(8,128)(2,1)S(1)}, bf16[4,128,128]{2,1,0:T(8,128)(2,1)S(1)}, u32[]{:S(2)}, u32[]{:S(2)}) collective-permute-start(bf16[4,128,128]{2,1,0:T(8,128)(2,1)S(1)} %broadcast_select_fusion.13.refs_0_), channel_id=1, source_target_pairs={{0,16},{16,0},{32,48},{48,32},{64,80},{80,64},{96,112},{112,96},{1... | collective-permute-start | bytes 393224 | tf_op jit(solution)/shard_map/ppermute | solution.py:103
  114.8 5.3 %copy-start.14 = (bf16[4,128,128]{2,1,0:T(8,128)(2,1)}, bf16[4,128,128]{2,1,0:T(8,128)(2,1)S(1)}, u32[]{:S(2)}) copy-start(bf16[4,128,128]{2,1,0:T(8,128)(2,1)S(1)} %collective-permute-done.28.refs_1_) | copy-start | bytes 393220
  114.8 4.3 %collective-permute-start.32 = (bf16[4,128,128]{2,1,0:T(8,128)(2,1)S(1)}, bf16[4,128,128]{2,1,0:T(8,128)(2,1)S(1)}, u32[]{:S(2)}, u32[]{:S(2)}) collective-permute-start(bf16[4,128,128]{2,1,0:T(8,128)(2,1)S(1)} %collective-permute-done.28.refs_1_), channel_id=1, source_target_pairs={{0,16},{16,0},{32,48},{48,32},{64,80},{80,64},{96,112},{112,96},{1... | collective-permute-start | bytes 393224 | tf_op jit(solution)/shard_map/ppermute | solution.py:103
  114.9 5.2 %copy-start.17 = (bf16[4,128,128]{2,1,0:T(8,128)(2,1)}, bf16[4,128,128]{2,1,0:T(8,128)(2,1)S(1)}, u32[]{:S(2)}) copy-start(bf16[4,128,128]{2,1,0:T(8,128)(2,1)S(1)} %collective-permute-done.29.refs_2_) | copy-start | bytes 393220
  114.9 4.2 %collective-permute-start.33 = (bf16[4,128,128]{2,1,0:T(8,128)(2,1)S(1)}, bf16[4,128,128]{2,1,0:T(8,128)(2,1)S(1)}, u32[]{:S(2)}, u32[]{:S(2)}) collective-permute-start(bf16[4,128,128]{2,1,0:T(8,128)(2,1)S(1)} %collective-permute-done.29.refs_2_), channel_id=1, source_target_pairs={{0,16},{16,0},{32,48},{48,32},{64,80},{80,64},{96,112},{112,96},{1... | collective-permute-start | bytes 393224 | tf_op jit(solution)/shard_map/ppermute | solution.py:103
  116.7 3.4 %collective-permute-start.34 = (bf16[4,128,128]{2,1,0:T(8,128)(2,1)S(1)}, bf16[4,128,128]{2,1,0:T(8,128)(2,1)S(1)}, u32[]{:S(2)}, u32[]{:S(2)}) collective-permute-start(bf16[4,128,128]{2,1,0:T(8,128)(2,1)S(1)} %collective-permute-done.30.refs_3_), channel_id=1, source_target_pairs={{0,16},{16,0},{32,48},{48,32},{64,80},{80,64},{96,112},{112,96},{1... | collective-permute-start | bytes 393224 | tf_op jit(solution)/shard_map/ppermute | solution.py:103
  120.8 38.4 %copy-start.1 = (bf16[4,128,128]{2,1,0:T(8,128)(2,1)S(1)}, bf16[4,128,128]{2,1,0:T(8,128)(2,1)}, u32[]{:S(2)}) copy-start(bf16[4,128,128]{2,1,0:T(8,128)(2,1)} %copy-done) | copy-start | bytes 393220
  120.8 38.4 %copy-start.3 = (bf16[4,128,128]{2,1,0:T(8,128)(2,1)S(1)}, bf16[4,128,128]{2,1,0:T(8,128)(2,1)}, u32[]{:S(2)}) copy-start(bf16[4,128,128]{2,1,0:T(8,128)(2,1)} %copy-done.2) | copy-start | bytes 393220
  126.4 0.7 collective-permute-start.36
  128.0 0.7 collective-permute-start.37
  128.7 0.7 collective-permute-start.38
  129.4 7.9 %collective-permute-start.39 = (bf16[4,128,128]{2,1,0:T(8,128)(2,1)S(1)}, bf16[4,128,128]{2,1,0:T(8,128)(2,1)S(1)}, u32[]{:S(2)}, u32[]{:S(2)}) collective-permute-start(bf16[4,128,128]{2,1,0:T(8,128)(2,1)S(1)} %broadcast_select_fusion.8), channel_id=1, source_target_pairs={{0,12},{1,13},{2,14},{3,15},{4,8},{5,9},{6,10},{7,11},{16,28},{17,... | collective-permute-start | bytes 393224 | tf_op jit(solution)/shard_map/ppermute | solution.py:123
  137.4 23.7 %copy-start.5 = (bf16[4,128,128]{2,1,0:T(8,128)(2,1)}, bf16[4,128,128]{2,1,0:T(8,128)(2,1)S(1)}, u32[]{:S(2)}) copy-start(bf16[4,128,128]{2,1,0:T(8,128)(2,1)S(1)} %broadcast_select_fusion.12.refs_0_) | copy-start | bytes 393220
  137.4 16.1 %collective-permute-start.40 = (bf16[4,128,128]{2,1,0:T(8,128)(2,1)S(1)}, bf16[4,128,128]{2,1,0:T(8,128)(2,1)S(1)}, u32[]{:S(2)}, u32[]{:S(2)}) collective-permute-start(bf16[4,128,128]{2,1,0:T(8,128)(2,1)S(1)} %broadcast_select_fusion.12.refs_0_), channel_id=1, source_target_pairs={{0,32},{16,48},{32,0},{48,16},{64,96},{80,112},{96,64},{112,80},{1... | collective-permute-start | bytes 393224 | tf_op jit(solution)/shard_map/ppermute | solution.py:103
  140.4 20.6 %collective-permute-start.47 = (f32[4,128,128]{2,1,0:T(8,128)}, f32[4,128,128]{2,1,0:T(8,128)S(1)}, u32[]{:S(2)}, u32[]{:S(2)}) collective-permute-start(f32[4,128,128]{2,1,0:T(8,128)} %get-tuple-element.13), channel_id=1, source_target_pairs={{1,0},{2,1},{3,2},{4,3},{5,4},{6,5},{7,6},{8,7},{9,8},{10,9},{11,1... | collective-permute-start | bytes 786440 | tf_op jit(solution)/shard_map/ppermute | solution.py:133
  147.0 6.5 %collective-permute-start.41 = (bf16[4,128,128]{2,1,0:T(8,128)(2,1)S(1)}, bf16[4,128,128]{2,1,0:T(8,128)(2,1)S(1)}, u32[]{:S(2)}, u32[]{:S(2)}) collective-permute-start(bf16[4,128,128]{2,1,0:T(8,128)(2,1)S(1)} %broadcast_select_fusion.12.refs_0_), channel_id=1, source_target_pairs={{0,64},{16,80},{32,96},{48,112},{64,0},{80,16},{96,32},{112,48},{1... | collective-permute-start | bytes 393224 | tf_op jit(solution)/shard_map/ppermute | solution.py:103
  149.8 6.4 %collective-permute-start.42 = (bf16[4,128,128]{2,1,0:T(8,128)(2,1)S(1)}, bf16[4,128,128]{2,1,0:T(8,128)(2,1)S(1)}, u32[]{:S(2)}, u32[]{:S(2)}) collective-permute-start(bf16[4,128,128]{2,1,0:T(8,128)(2,1)S(1)} %broadcast_select_fusion.12.refs_0_), channel_id=1, source_target_pairs={{0,96},{16,112},{32,64},{48,80},{64,32},{80,48},{96,0},{112,16},{1... | collective-permute-start | bytes 393224 | tf_op jit(solution)/shard_map/ppermute | solution.py:103
  149.8 11.1 %collective-permute-start.43 = (bf16[4,128,128]{2,1,0:T(8,128)(2,1)S(1)}, bf16[4,128,128]{2,1,0:T(8,128)(2,1)S(1)}, u32[]{:S(2)}, u32[]{:S(2)}) collective-permute-start(bf16[4,128,128]{2,1,0:T(8,128)(2,1)S(1)} %broadcast_select_fusion.12.refs_0_), channel_id=1, source_target_pairs={{0,16},{16,0},{32,48},{48,32},{64,80},{80,64},{96,112},{112,96},{1... | collective-permute-start | bytes 393224 | tf_op jit(solution)/shard_map/ppermute | solution.py:103
  153.5 7.6 %copy-start.13 = (bf16[4,128,128]{2,1,0:T(8,128)(2,1)}, bf16[4,128,128]{2,1,0:T(8,128)(2,1)S(1)}, u32[]{:S(2)}) copy-start(bf16[4,128,128]{2,1,0:T(8,128)(2,1)S(1)} %collective-permute-done.40.refs_1_) | copy-start | bytes 393220
  153.5 7.5 %collective-permute-start.44 = (bf16[4,128,128]{2,1,0:T(8,128)(2,1)S(1)}, bf16[4,128,128]{2,1,0:T(8,128)(2,1)S(1)}, u32[]{:S(2)}, u32[]{:S(2)}) collective-permute-start(bf16[4,128,128]{2,1,0:T(8,128)(2,1)S(1)} %collective-permute-done.40.refs_1_), channel_id=1, source_target_pairs={{0,16},{16,0},{32,48},{48,32},{64,80},{80,64},{96,112},{112,96},{1... | collective-permute-start | bytes 393224 | tf_op jit(solution)/shard_map/ppermute | solution.py:103
  153.5 7.5 %copy-start.16 = (bf16[4,128,128]{2,1,0:T(8,128)(2,1)}, bf16[4,128,128]{2,1,0:T(8,128)(2,1)S(1)}, u32[]{:S(2)}) copy-start(bf16[4,128,128]{2,1,0:T(8,128)(2,1)S(1)} %collective-permute-done.41.refs_2_) | copy-start | bytes 393220
  153.5 7.5 %collective-permute-start.45 = (bf16[4,128,128]{2,1,0:T(8,128)(2,1)S(1)}, bf16[4,128,128]{2,1,0:T(8,128)(2,1)S(1)}, u32[]{:S(2)}, u32[]{:S(2)}) collective-permute-start(bf16[4,128,128]{2,1,0:T(8,128)(2,1)S(1)} %collective-permute-done.41.refs_2_), channel_id=1, source_target_pairs={{0,16},{16,0},{32,48},{48,32},{64,80},{80,64},{96,112},{112,96},{1... | collective-permute-start | bytes 393224 | tf_op jit(solution)/shard_map/ppermute | solution.py:103
  156.3 4.8 %collective-permute-start.46 = (bf16[4,128,128]{2,1,0:T(8,128)(2,1)S(1)}, bf16[4,128,128]{2,1,0:T(8,128)(2,1)S(1)}, u32[]{:S(2)}, u32[]{:S(2)}) collective-permute-start(bf16[4,128,128]{2,1,0:T(8,128)(2,1)S(1)} %collective-permute-done.42.refs_3_), channel_id=1, source_target_pairs={{0,16},{16,0},{32,48},{48,32},{64,80},{80,64},{96,112},{112,96},{1... | collective-permute-start | bytes 393224 | tf_op jit(solution)/shard_map/ppermute | solution.py:103
  (26 other events, 38.8 us)

commit v2 on v1

v2 whole, which is shorter than its diff:
```python
import jax
import jax.numpy as jnp
from jax import lax
from jax.experimental import pallas as pl
from jax.experimental.pallas import tpu as pltpu
from jax.sharding import PartitionSpec as P


GROUP = 4
UNROLL = 4
PLACES = 112
ZERO_COLUMN = 32
COUNT_WORD = 144
PIECES = 8


def accumulate(meta, blocks, pieces, base, gathered, sums, arrivals):
    rows = base.shape[0]
    copies = [
        pltpu.make_async_copy(piece, gathered.at[pl.ds(place * rows, rows)], arrivals.at[place])
        for place, piece in enumerate(pieces)
    ]
    for copy in copies:
        copy.start()
    gathered[ZERO_COLUMN] = jnp.zeros(gathered.shape[1:], gathered.dtype)
    sums[...] = base[...]
    for copy in copies:
        copy.wait()

    def several(at, carry):
        for offset in range(UNROLL):
            group = at * UNROLL + offset
            words = [meta[group * GROUP + member] for member in range(GROUP)]
            left = jnp.concatenate([blocks[word >> 6] for word in words], axis=1)
            right = jnp.concatenate([gathered[word & 63] for word in words], axis=0)
            sums[meta[PLACES + group]] += jnp.dot(left, right, preferred_element_type=jnp.float32)
        return carry

    lax.fori_loop(0, (meta[COUNT_WORD] + UNROLL - 1) // UNROLL, several, 0)


def solve(inverse, excitation, field, solved):
    for b in range(inverse.shape[0]):
        solved[b] = jnp.dot(
            inverse[b],
            excitation[b].astype(jnp.float32) - field[b],
            precision=lax.Precision.HIGHEST,
            preferred_element_type=jnp.float32,
        ).astype(solved.dtype)


def first_kernel(lag, excitation, base, inverse, solved):
    @pl.when(lag[0] == 0)
    def _():
        solve(inverse, excitation, base, solved)

    @pl.when(lag[0] != 0)
    def _():
        solved[...] = jnp.zeros(solved.shape, solved.dtype)


def chain_kernel(lag, meta, blocks, *refs):
    pieces, (base, excitation, inverse, solved, gathered, sums, arrivals) = refs[:PIECES], refs[PIECES:]

    @pl.when(lag[0] == 0)
    def _():
        accumulate(meta, blocks, pieces, base, gathered, sums, arrivals)
        solve(inverse, excitation, sums, solved)

    @pl.when(lag[0] != 0)
    def _():
        solved[...] = jnp.zeros(solved.shape, solved.dtype)


def others_kernel(lag, meta, blocks, *refs):
    pieces, (base, total, gathered, arrivals) = refs[:PIECES], refs[PIECES:]

    @pl.when(lag[0] != 0)
    def _():
        accumulate(meta, blocks, pieces, base, gathered, total, arrivals)

    @pl.when(lag[0] == 0)
    def _():
        total[...] = jnp.zeros(total.shape, total.dtype)


def last_kernel(meta, blocks, *refs):
    pieces, solved, (base, total, kept, gathered, arrivals, placed) = refs[:PIECES], refs[PIECES:-6], refs[-6:]
    copies = [
        pltpu.make_async_copy(each, kept.at[t], placed.at[t]) for t, each in enumerate(solved)
    ]
    for copy in copies:
        copy.start()
    accumulate(meta, blocks, pieces, base, gathered, total, arrivals)
    for copy in copies:
        copy.wait()


PARAMS = pltpu.CompilerParams(vmem_limit_bytes=24 * 1024 * 1024)
SMEM = pl.BlockSpec(memory_space=pltpu.SMEM)
VMEM = pl.BlockSpec(memory_space=pltpu.VMEM)
ANY = pl.BlockSpec(memory_space=pl.ANY)


def held(arrays):
    return [pltpu.with_memory_space_constraint(array, pltpu.VMEM) for array in arrays]


def gathering(base):
    return [
        pltpu.VMEM((ZERO_COLUMN + 1,) + base.shape[1:], jnp.bfloat16),
        pltpu.SemaphoreType.DMA((PIECES,)),
    ]


def first_solve(lag, excitation, base, inverse):
    return pl.pallas_call(
        first_kernel,
        out_shape=jax.ShapeDtypeStruct(base.shape, jnp.bfloat16),
        in_specs=[SMEM, VMEM, VMEM, VMEM],
        compiler_params=PARAMS,
        out_specs=VMEM,
    )(lag, excitation, base, inverse)


def chain_step(lag, meta, blocks, pieces, base, excitation, inverse):
    gathered, arrivals = gathering(base)
    return pl.pallas_call(
        chain_kernel,
        out_shape=jax.ShapeDtypeStruct(base.shape, jnp.bfloat16),
        in_specs=[SMEM, SMEM, VMEM] + [VMEM] * PIECES + [VMEM] * 3,
        compiler_params=PARAMS,
        out_specs=VMEM,
        scratch_shapes=[gathered, pltpu.VMEM(base.shape, jnp.float32), arrivals],
    )(lag, meta, blocks, *held(pieces), base, excitation, inverse)


def others_step(lag, meta, blocks, pieces, base):
    return pl.pallas_call(
        others_kernel,
        out_shape=jax.ShapeDtypeStruct(base.shape, jnp.float32),
        in_specs=[SMEM, SMEM, VMEM] + [VMEM] * PIECES + [VMEM],
        compiler_params=PARAMS,
        out_specs=VMEM,
        scratch_shapes=gathering(base),
    )(lag, meta, blocks, *held(pieces), base)


def last_step(meta, blocks, pieces, solved, base):
    return pl.pallas_call(
        last_kernel,
        out_shape=(
            jax.ShapeDtypeStruct(base.shape, jnp.float32),
            jax.ShapeDtypeStruct((len(solved),) + base.shape, jnp.bfloat16),
        ),
        in_specs=[SMEM, VMEM] + [VMEM] * PIECES + [ANY] * len(solved) + [VMEM],
        compiler_params=PARAMS,
        out_specs=(VMEM, ANY),
        scratch_shapes=gathering(base) + [pltpu.SemaphoreType.DMA((len(solved),))],
    )(meta, blocks, *held(pieces), *solved, base)


def over_rows(value, flip):
    count = lax.axis_size("rows")
    return lax.ppermute(value, "rows", [(r, r ^ flip) for r in range(count)])


def exchange(own):
    half = lax.axis_size("rows") // 2
    near = [own]
    for z in range(1, half):
        near.append(over_rows(own, 2 * z))
    pieces = list(near)
    for z in range(half):
        pieces.append(over_rows(near[z], 1))
    return pieces


LAG_ROUNDS = (
    [(0, 1)],
    [(0, 3), (1, 2)],
    [(x, x + 4) for x in range(4)],
    [(x, x + 12) for x in range(4)] + [(x + 4, x + 8) for x in range(4)],
)


def spread(value):
    lag = lax.axis_index("lag")
    for pairs in LAG_ROUNDS:
        arrived = lax.ppermute(value, "lag", pairs)
        takes = jnp.zeros((), jnp.bool_)
        for _, target in pairs:
            takes = takes | (lag == target)
        value = jnp.where(takes, arrived, value)
    return value


def from_behind(value):
    count = lax.axis_size("lag")
    return lax.ppermute(value, "lag", [(g + 1, g) for g in range(count - 1)])


def slot_words(slot_row, slot_owner, slot_pos, needed, count, row_blocks):
    slots = slot_row.shape[0]
    at = jnp.arange(slots, dtype=jnp.int32)
    live = at < count
    table = needed.reshape(-1)
    entry = slot_owner * needed.shape[-1] + slot_pos
    entries = jnp.arange(table.shape[0], dtype=jnp.int32)
    local = jnp.sum(jnp.where(entry[:, None] == entries[None, :], table[None, :], 0), axis=1)
    apart = slot_owner ^ lax.axis_index("rows")
    column = ((apart & 1) * 4 + (apart >> 1)) * row_blocks + local
    word = at * 64 + column
    earlier = (slot_row[None, :] == slot_row[:, None]) & (at[None, :] < at[:, None])
    rank = jnp.sum(earlier.astype(jnp.int32), axis=1)
    row_at = jnp.arange(row_blocks, dtype=jnp.int32)
    in_row = (slot_row[None, :] == row_at[:, None]) & live[None, :]
    groups = (jnp.sum(in_row.astype(jnp.int32), axis=1) + GROUP - 1) // GROUP
    first = jnp.sum(jnp.where(row_at[None, :] < row_at[:, None], groups[None, :], 0), axis=1)
    start = jnp.sum(jnp.where(slot_row[:, None] == row_at[None, :], first[None, :], 0), axis=1)
    place = jnp.where(live, start * GROUP + rank, -1)
    taken = place[None, :] == jnp.arange(PLACES, dtype=jnp.int32)[:, None]
    words = ZERO_COLUMN + jnp.sum(jnp.where(taken, word[None, :] - ZERO_COLUMN, 0), axis=1)
    group_at = jnp.arange(COUNT_WORD - PLACES, dtype=jnp.int32)
    group_row = jnp.sum((group_at[:, None] >= first[None, :]).astype(jnp.int32), axis=1) - 1
    return jnp.concatenate([words, group_row, jnp.sum(groups)[None]])


def per_device(
    excitation, pending, inverse, interaction, slot_row, slot_owner, slot_pos, needed, block_count
):
    row_blocks, block_size, _ = inverse.shape
    steps, rows, width = excitation.shape
    excitation_blocks = excitation.reshape(steps, row_blocks, block_size, width)
    lag = jnp.full((1,), lax.axis_index("lag"), jnp.int32)
    total = pending[0].reshape(row_blocks, block_size, width)
    solved = first_solve(lag, excitation_blocks[0], total, inverse)
    slot_row, solved = lax.optimization_barrier((slot_row, solved))
    meta = slot_words(slot_row, slot_owner, slot_pos, needed[0], block_count[0, 0], row_blocks)
    outputs = []
    (interaction,) = held((interaction,))
    for t in range(steps):
        solved = spread(solved)
        outputs.append(solved)
        if t > 0:
            total = others_step(lag, meta, interaction, pieces, base)
        base = from_behind(total)
        pieces = exchange(solved)
        if t + 1 < steps:
            solved = chain_step(lag, meta, interaction, pieces, base, excitation_blocks[t + 1], inverse)
        else:
            total, kept = last_step(meta, interaction, pieces, outputs, base)
    return (kept.reshape(steps, rows, width), total.reshape(1, rows, width))


def solution(mesh):
    in_specs = (
        P(None, "rows", None),
        P("lag", "rows", None),
        P("rows", None, None),
        P(("rows", "lag"), None, None),
        P(("rows", "lag")),
        P(("rows", "lag")),
        P(("rows", "lag")),
        P(("rows", "lag"), None, None),
        P("rows", "lag"),
    )
    out_specs = (P(None, "rows", None), P("lag", "rows", None))
    return jax.shard_map(
        per_device, mesh=mesh, in_specs=in_specs, out_specs=out_specs, check_vma=False
    )
```

time: 167 us -> 151 us (0.904)
  Pallas kernels: 24.1 us -> 12 us
  starting transfers between devices: 95 us -> 88.5 us
  other arithmetic: 5.78 us -> 11.2 us
  waiting for transfers between devices: 34.8 us -> 30.6 us
    pallas_call x4 -> x7, Pallas kernels: 22 us -> 12 us  [the longest x3 6.96 us: others_step(): pl.pallas_call(others_kernel, out_shape=jax.ShapeDtypeStruct(base.shape,...]
    ppermute x28, starting transfers between devices: 57.4 us -> 49.5 us  [over_rows(): return lax.ppermute(value, 'rows', [(r, r ^ flip) for r in range(count)])]
    ppermute x16, waiting for transfers between devices: 32 us -> 26.7 us  [spread(): arrived = lax.ppermute(value, 'lag', pairs)]
    reduce_sum x1 -> x8, other arithmetic: 0.09 us -> 4.83 us  [the longest x1 0.91 us: slot_words(): rank = jnp.sum(earlier.astype(jnp.int32), axis=1)]
    ppermute x16, starting transfers between devices: 13.1 us -> 15.4 us  [spread(): arrived = lax.ppermute(value, 'lag', pairs)]
    pallas_call x1, Pallas kernels: 2.13 us -> 0.02 us  [first_solve(): pl.pallas_call(first_kernel, out_shape=jax.ShapeDtypeStruct(base.shape, j...]
    another operation x1 -> x0, other arithmetic: 1.76 us -> none  [per_device(): jnp.stack(outputs).reshape(steps, rows, width)]
    unnamed x85 -> x21, local copies, waits for them, and re-layouts: 3.4 us -> 4.54 us
  transfers between devices with their start and end apart: 48 -> 48, of which waited for: 9 -> 12; matrix products, arithmetic and copies ran while one was open for 2% -> 9% of each run, Pallas kernels for 0% -> 5%
where the time goes in v2:
time: 151 us; the launch traced here: 150 us
  starting transfers between devices  88.5 us (59%)
  waiting for transfers between devices  30.6 us (20%)
  Pallas kernels  12 us (8%)
  other arithmetic  11.2 us (7%)
  local copies, waits for them, and re-layouts  6.45 us (4%)
  between operations  1.79 us (1%)
    ppermute x28, starting transfers between devices, over_rows(): return lax.ppermute(value, 'rows', [(r, r ^ flip) for r in range(count)])  49.5 us
    ppermute x16, waiting for transfers between devices, spread(): arrived = lax.ppermute(value, 'lag', pairs)  26.7 us
    ppermute x4, starting transfers between devices, from_behind(): return lax.ppermute(value, 'lag', [(g + 1, g) for g in range(count - 1)])  23.6 us
    ppermute x16, starting transfers between devices, spread(): arrived = lax.ppermute(value, 'lag', pairs)  15.4 us
    pallas_call x3, Pallas kernels, others_step(): pl.pallas_call(others_kernel, out_shape=jax.ShapeDtypeStruct(base.shape,...  6.96 us
    unnamed x21, local copies, waits for them, and re-layouts  4.54 us
    ppermute x28, waiting for transfers between devices, over_rows(): return lax.ppermute(value, 'rows', [(r, r ^ flip) for r in range(count)])  3.88 us
    select_n x16, other arithmetic, spread(): value = jnp.where(takes, arrived, value)  3.66 us
  transfers between devices with their start and end apart: 48, of which 12 were waited for; matrix products, arithmetic and copies ran while one was open for 9% of the time, Pallas kernels for 5%

profile of v2, /device:TPU:25, one launch (start us, length us, event | category | flops | bytes accessed | tf_op | source)
XLA Modules:
  0.0 150.5 jit_solution(16122701518971446254)
XLA Ops:
  0.6 4.8 %collective-permute-start.11 = (f32[4,128,128]{2,1,0:T(8,128)}, f32[4,128,128]{2,1,0:T(8,128)S(1)}, u32[]{:S(2)}, u32[]{:S(2)}) collective-permute-start(f32[4,128,128]{2,1,0:T(8,128)} %bitcast.16), channel_id=1, source_target_pairs={{1,0},{2,1},{3,2},{4,3},{5,4},{6,5},{7,6},{8,7},{9,8},{10,9},{11,1... | collective-permute-start | bytes 786440 | tf_op jit(solution)/shard_map/ppermute | solution.py:200
  5.5 1.8 %fusion.3 = (bf16[1,512,128]{2,1,0:T(8,128)(2,1)}, bf16[1,512,128]{2,1,0:T(8,128)(2,1)}, bf16[1,512,128]{2,1,0:T(8,128)(2,1)S(1)}, bf16[1,512,128]{2,1,0:T(8,128)(2,1)}) fusion(bf16[4,512,128]{2,1,0:T(8,128)(2,1)} %param.9), kind=kLoop, calls=%fused_computation.44 | loop fusion | bytes 1048576 | tf_op jit(solution)/shard_map/slice | solution.py:250
  7.3 0.9 copy-done.1
  8.3 0.9 copy-done.7
  9.2 1.3 collective-permute-start
  11.2 1.3 multiply_add_fusion
  12.5 0.8 convert_reduce_fusion.2
  13.2 0.7 fusion.2
  14.0 0.7 broadcast_select_fusion.3
  14.6 1.3 collective-permute-start.1
  16.1 0.9 convert_reduce_fusion
  17.0 0.9 broadcast_select_fusion.7
  18.0 1.3 collective-permute-start.2
  19.3 0.7 select_reduce_fusion.2
  20.0 0.8 copy.13
  20.8 0.8 select_reduce_fusion.1
  21.6 0.9 broadcast_select_fusion.11
  22.5 1.3 collective-permute-start.3
  23.8 0.7 add_add_fusion
  24.6 5.0 %collective-permute-done.3 = bf16[4,128,128]{2,1,0:T(8,128)(2,1)} collective-permute-done((bf16[4,128,128]{2,1,0:T(8,128)(2,1)S(1)}, bf16[4,128,128]{2,1,0:T(8,128)(2,1)}, u32[]{:S(2)}, u32[]{:S(2)}) %collective-permute-start.3) | collective-permute-done | bytes 131104 | tf_op jit(solution)/shard_map/ppermute | solution.py:190
  29.6 0.9 broadcast_select_fusion.15.refs_0_.refs_8_
  30.5 3.8 %collective-permute-start.6 = (bf16[4,128,128]{2,1,0:T(8,128)(2,1)S(1)}, bf16[4,128,128]{2,1,0:T(8,128)(2,1)S(1)}, u32[]{:S(2)}, u32[]{:S(2)}) collective-permute-start(bf16[4,128,128]{2,1,0:T(8,128)(2,1)S(1)} %broadcast_select_fusion.15.refs_0_.refs_8_), channel_id=1, source_target_pairs={{0,96},{16,112},{32,64},{48,80},{64,32},{80,48},{96,0},{112,16},{1... | collective-permute-start | bytes 393224 | tf_op jit(solution)/shard_map/ppermute | solution.py:165
  35.0 0.7 convert_reduce_fusion.1
  35.7 2.7 %collective-permute-start.7 = (bf16[4,128,128]{2,1,0:T(8,128)(2,1)S(1)}, bf16[4,128,128]{2,1,0:T(8,128)(2,1)S(1)}, u32[]{:S(2)}, u32[]{:S(2)}) collective-permute-start(bf16[4,128,128]{2,1,0:T(8,128)(2,1)S(1)} %broadcast_select_fusion.15.refs_0_.refs_8_), channel_id=1, source_target_pairs={{0,16},{16,0},{32,48},{48,32},{64,80},{80,64},{96,112},{112,96},{1... | collective-permute-start | bytes 393224 | tf_op jit(solution)/shard_map/ppermute | solution.py:165
  38.4 2.6 %collective-permute-start.10 = (bf16[4,128,128]{2,1,0:T(8,128)(2,1)S(1)}, bf16[4,128,128]{2,1,0:T(8,128)(2,1)S(1)}, u32[]{:S(2)}, u32[]{:S(2)}) collective-permute-start(bf16[4,128,128]{2,1,0:T(8,128)(2,1)S(1)} %collective-permute-done.6.refs_3_), channel_id=1, source_target_pairs={{0,16},{16,0},{32,48},{48,32},{64,80},{80,64},{96,112},{112,96},{1... | collective-permute-start | bytes 393224 | tf_op jit(solution)/shard_map/ppermute | solution.py:165
  41.1 2.1 %collective-permute-start.9 = (bf16[4,128,128]{2,1,0:T(8,128)(2,1)S(1)}, bf16[4,128,128]{2,1,0:T(8,128)(2,1)S(1)}, u32[]{:S(2)}, u32[]{:S(2)}) collective-permute-start(bf16[4,128,128]{2,1,0:T(8,128)(2,1)S(1)} %collective-permute-done.5.refs_2_), channel_id=1, source_target_pairs={{0,16},{16,0},{32,48},{48,32},{64,80},{80,64},{96,112},{112,96},{1... | collective-permute-start | bytes 393224 | tf_op jit(solution)/shard_map/ppermute | solution.py:165
  43.2 0.8 pad_add_fusion.meta
  44.6 0.9 copy-done.2
  45.5 0.9 copy-done.6
  47.1 0.8 collective-permute-start.12
  47.9 0.7 collective-permute-start.13
  48.6 0.7 collective-permute-start.14
  49.4 1.3 collective-permute-start.15
  50.7 2.3 %shard_map.106 = f32[4,128,128]{2,1,0:T(8,128)S(1)} custom-call(s32[1]{0:T(128)} %bitcast.1.lag, s32[145]{0:T(256)S(1)} %pad_add_fusion.meta, bf16[96,128,128]{2,1,0:T(8,128)(2,1)S(1)} %copy-done, bf16[4,128,128]{2,1,0:T(8,128)(2,1)S(1)} %broadcast_select_fusion.15.refs_0_.refs_8_, bf16[4,128,128]{2,1,0:T(8,128)(2,1)S(1)} %collective-permute-done.4.refs_1_, ...), custom_call_target="tpu_custom_call" | custom-call | tf_op jit(solution)/shard_map/pallas_call | solution.py:139
  53.0 9.0 %collective-permute-done.15 = bf16[4,128,128]{2,1,0:T(8,128)(2,1)S(1)} collective-permute-done((bf16[4,128,128]{2,1,0:T(8,128)(2,1)S(1)}, bf16[4,128,128]{2,1,0:T(8,128)(2,1)S(1)}, u32[]{:S(2)}, u32[]{:S(2)}) %collective-permute-start.15) | collective-permute-done | bytes 131104 | tf_op jit(solution)/shard_map/ppermute | solution.py:190
  62.0 2.6 %collective-permute-start.18 = (bf16[4,128,128]{2,1,0:T(8,128)(2,1)S(1)}, bf16[4,128,128]{2,1,0:T(8,128)(2,1)S(1)}, u32[]{:S(2)}, u32[]{:S(2)}) collective-permute-start(bf16[4,128,128]{2,1,0:T(8,128)(2,1)S(1)} %broadcast_select_fusion.14.refs_0_.refs_9_), channel_id=1, source_target_pairs={{0,96},{16,112},{32,64},{48,80},{64,32},{80,48},{96,0},{112,16},{1... | collective-permute-start | bytes 393224 | tf_op jit(solution)/shard_map/ppermute | solution.py:165
  64.6 6.3 %collective-permute-start.23 = (f32[4,128,128]{2,1,0:T(8,128)S(1)}, f32[4,128,128]{2,1,0:T(8,128)S(1)}, u32[]{:S(2)}, u32[]{:S(2)}) collective-permute-start(f32[4,128,128]{2,1,0:T(8,128)S(1)} %shard_map.106), channel_id=1, source_target_pairs={{1,0},{2,1},{3,2},{4,3},{5,4},{6,5},{7,6},{8,7},{9,8},{10,9},{11,1... | collective-permute-start | bytes 786440 | tf_op jit(solution)/shard_map/ppermute | solution.py:200
  70.9 1.4 collective-permute-start.17
  72.3 4.0 %collective-permute-start.19 = (bf16[4,128,128]{2,1,0:T(8,128)(2,1)S(1)}, bf16[4,128,128]{2,1,0:T(8,128)(2,1)S(1)}, u32[]{:S(2)}, u32[]{:S(2)}) collective-permute-start(bf16[4,128,128]{2,1,0:T(8,128)(2,1)S(1)} %broadcast_select_fusion.14.refs_0_.refs_9_), channel_id=1, source_target_pairs={{0,16},{16,0},{32,48},{48,32},{64,80},{80,64},{96,112},{112,96},{1... | collective-permute-start | bytes 393224 | tf_op jit(solution)/shard_map/ppermute | solution.py:165
  76.3 4.7 %collective-permute-start.21 = (bf16[4,128,128]{2,1,0:T(8,128)(2,1)S(1)}, bf16[4,128,128]{2,1,0:T(8,128)(2,1)S(1)}, u32[]{:S(2)}, u32[]{:S(2)}) collective-permute-start(bf16[4,128,128]{2,1,0:T(8,128)(2,1)S(1)} %collective-permute-done.17.refs_2_), channel_id=1, source_target_pairs={{0,16},{16,0},{32,48},{48,32},{64,80},{80,64},{96,112},{112,96},{1... | collective-permute-start | bytes 393224 | tf_op jit(solution)/shard_map/ppermute | solution.py:165
  81.0 1.0 collective-permute-done.21.refs_6_
  83.0 0.8 collective-permute-start.24
  83.8 0.7 collective-permute-start.25
  84.6 0.7 collective-permute-start.26
  85.3 1.3 collective-permute-start.27
  86.6 2.3 %shard_map.108 = f32[4,128,128]{2,1,0:T(8,128)S(1)} custom-call(s32[1]{0:T(128)} %bitcast.1.lag, s32[145]{0:T(256)S(1)} %pad_add_fusion.meta, bf16[96,128,128]{2,1,0:T(8,128)(2,1)S(1)} %copy-done, bf16[4,128,128]{2,1,0:T(8,128)(2,1)S(1)} %broadcast_select_fusion.14.refs_0_.refs_9_, bf16[4,128,128]{2,1,0:T(8,128)(2,1)S(1)} %collective-permute-done.16.refs_1_, ...), custom_call_target="tpu_custom_call" | custom-call | tf_op jit(solution)/shard_map/pallas_call | solution.py:139
  88.9 6.5 %collective-permute-done.27 = bf16[4,128,128]{2,1,0:T(8,128)(2,1)S(1)} collective-permute-done((bf16[4,128,128]{2,1,0:T(8,128)(2,1)S(1)}, bf16[4,128,128]{2,1,0:T(8,128)(2,1)S(1)}, u32[]{:S(2)}, u32[]{:S(2)}) %collective-permute-start.27) | collective-permute-done | bytes 131104 | tf_op jit(solution)/shard_map/ppermute | solution.py:190
  95.4 1.2 collective-permute-start.30
  96.6 6.3 %collective-permute-start.35 = (f32[4,128,128]{2,1,0:T(8,128)S(1)}, f32[4,128,128]{2,1,0:T(8,128)S(1)}, u32[]{:S(2)}, u32[]{:S(2)}) collective-permute-start(f32[4,128,128]{2,1,0:T(8,128)S(1)} %shard_map.108), channel_id=1, source_target_pairs={{1,0},{2,1},{3,2},{4,3},{5,4},{6,5},{7,6},{8,7},{9,8},{10,9},{11,1... | collective-permute-start | bytes 786440 | tf_op jit(solution)/shard_map/ppermute | solution.py:200
  102.9 0.8 collective-permute-start.29
  103.7 1.5 %collective-permute-start.28 = (bf16[4,128,128]{2,1,0:T(8,128)(2,1)S(1)}, bf16[4,128,128]{2,1,0:T(8,128)(2,1)S(1)}, u32[]{:S(2)}, u32[]{:S(2)}) collective-permute-start(bf16[4,128,128]{2,1,0:T(8,128)(2,1)S(1)} %broadcast_select_fusion.13.refs_0_.refs_10_), channel_id=1, source_target_pairs={{0,32},{16,48},{32,0},{48,16},{64,96},{80,112},{96,64},{112,80},{1... | collective-permute-start | bytes 393224 | tf_op jit(solution)/shard_map/ppermute | solution.py:165
  105.3 4.5 %collective-permute-start.31 = (bf16[4,128,128]{2,1,0:T(8,128)(2,1)S(1)}, bf16[4,128,128]{2,1,0:T(8,128)(2,1)S(1)}, u32[]{:S(2)}, u32[]{:S(2)}) collective-permute-start(bf16[4,128,128]{2,1,0:T(8,128)(2,1)S(1)} %broadcast_select_fusion.13.refs_0_.refs_10_), channel_id=1, source_target_pairs={{0,16},{16,0},{32,48},{48,32},{64,80},{80,64},{96,112},{112,96},{1... | collective-permute-start | bytes 393224 | tf_op jit(solution)/shard_map/ppermute | solution.py:165
  109.8 3.8 %collective-permute-start.33 = (bf16[4,128,128]{2,1,0:T(8,128)(2,1)S(1)}, bf16[4,128,128]{2,1,0:T(8,128)(2,1)S(1)}, u32[]{:S(2)}, u32[]{:S(2)}) collective-permute-start(bf16[4,128,128]{2,1,0:T(8,128)(2,1)S(1)} %collective-permute-done.29.refs_2_), channel_id=1, source_target_pairs={{0,16},{16,0},{32,48},{48,32},{64,80},{80,64},{96,112},{112,96},{1... | collective-permute-start | bytes 393224 | tf_op jit(solution)/shard_map/ppermute | solution.py:165
  115.7 0.7 collective-permute-start.36
  117.2 0.7 collective-permute-start.38
  117.9 1.3 collective-permute-start.39
  119.2 2.3 %shard_map.110 = f32[4,128,128]{2,1,0:T(8,128)S(1)} custom-call(s32[1]{0:T(128)} %bitcast.1.lag, s32[145]{0:T(256)S(1)} %pad_add_fusion.meta, bf16[96,128,128]{2,1,0:T(8,128)(2,1)S(1)} %copy-done, bf16[4,128,128]{2,1,0:T(8,128)(2,1)S(1)} %broadcast_select_fusion.13.refs_0_.refs_10_, bf16[4,128,128]{2,1,0:T(8,128)(2,1)S(1)} %collective-permute-done.28.refs_1_, ...), custom_call_target="tpu_custom_call" | custom-call | tf_op jit(solution)/shard_map/pallas_call | solution.py:139
  121.5 6.2 %collective-permute-done.39 = bf16[4,128,128]{2,1,0:T(8,128)(2,1)S(1)} collective-permute-done((bf16[4,128,128]{2,1,0:T(8,128)(2,1)S(1)}, bf16[4,128,128]{2,1,0:T(8,128)(2,1)S(1)}, u32[]{:S(2)}, u32[]{:S(2)}) %collective-permute-start.39) | collective-permute-done | bytes 131104 | tf_op jit(solution)/shard_map/ppermute | solution.py:190
  127.8 1.3 collective-permute-start.42
  129.1 6.3 %collective-permute-start.47 = (f32[4,128,128]{2,1,0:T(8,128)S(1)}, f32[4,128,128]{2,1,0:T(8,128)S(1)}, u32[]{:S(2)}, u32[]{:S(2)}) collective-permute-start(f32[4,128,128]{2,1,0:T(8,128)S(1)} %shard_map.110), channel_id=1, source_target_pairs={{1,0},{2,1},{3,2},{4,3},{5,4},{6,5},{7,6},{8,7},{9,8},{10,9},{11,1... | collective-permute-start | bytes 786440 | tf_op jit(solution)/shard_map/ppermute | solution.py:200
  135.9 1.7 %collective-permute-start.40 = (bf16[4,128,128]{2,1,0:T(8,128)(2,1)S(1)}, bf16[4,128,128]{2,1,0:T(8,128)(2,1)S(1)}, u32[]{:S(2)}, u32[]{:S(2)}) collective-permute-start(bf16[4,128,128]{2,1,0:T(8,128)(2,1)S(1)} %broadcast_select_fusion.12.refs_0_.refs_11_), channel_id=1, source_target_pairs={{0,32},{16,48},{32,0},{48,16},{64,96},{80,112},{96,64},{112,80},{1... | collective-permute-start | bytes 393224 | tf_op jit(solution)/shard_map/ppermute | solution.py:165
  137.5 4.6 %collective-permute-start.43 = (bf16[4,128,128]{2,1,0:T(8,128)(2,1)S(1)}, bf16[4,128,128]{2,1,0:T(8,128)(2,1)S(1)}, u32[]{:S(2)}, u32[]{:S(2)}) collective-permute-start(bf16[4,128,128]{2,1,0:T(8,128)(2,1)S(1)} %broadcast_select_fusion.12.refs_0_.refs_11_), channel_id=1, source_target_pairs={{0,16},{16,0},{32,48},{48,32},{64,80},{80,64},{96,112},{112,96},{1... | collective-permute-start | bytes 393224 | tf_op jit(solution)/shard_map/ppermute | solution.py:165
  142.1 3.9 %collective-permute-start.45 = (bf16[4,128,128]{2,1,0:T(8,128)(2,1)S(1)}, bf16[4,128,128]{2,1,0:T(8,128)(2,1)S(1)}, u32[]{:S(2)}, u32[]{:S(2)}) collective-permute-start(bf16[4,128,128]{2,1,0:T(8,128)(2,1)S(1)} %collective-permute-done.41.refs_2_), channel_id=1, source_target_pairs={{0,16},{16,0},{32,48},{48,32},{64,80},{80,64},{96,112},{112,96},{1... | collective-permute-start | bytes 393224 | tf_op jit(solution)/shard_map/ppermute | solution.py:165
  147.4 3.1 %shard_map.111 = (f32[4,128,128]{2,1,0:T(8,128)}, bf16[4,4,128,128]{3,2,1,0:T(8,128)(2,1)}) custom-call(s32[145]{0:T(256)S(1)} %pad_add_fusion.meta, bf16[96,128,128]{2,1,0:T(8,128)(2,1)S(1)} %copy-done, bf16[4,128,128]{2,1,0:T(8,128)(2,1)S(1)} %broadcast_select_fusion.12.refs_0_.refs_11_, bf16[4,128,128]{2,1,0:T(8,128)(2,1)S(1)} %collective-permute-done.40.refs_1_, ...), custom_call_target="tpu_custom_call" | custom-call | tf_op jit(solution)/shard_map/pallas_call | solution.py:150
  (93 shorter events, 8.3 us)
Async XLA Ops:
  0.6 43.9 %copy-start = (bf16[96,128,128]{2,1,0:T(8,128)(2,1)S(1)}, bf16[96,128,128]{2,1,0:T(8,128)(2,1)}, u32[]{:S(2)}) copy-start(bf16[96,128,128]{2,1,0:T(8,128)(2,1)} %blocks.13) | copy-start | bytes 9437188
  0.6 43.3 %collective-permute-start.11 = (f32[4,128,128]{2,1,0:T(8,128)}, f32[4,128,128]{2,1,0:T(8,128)S(1)}, u32[]{:S(2)}, u32[]{:S(2)}) collective-permute-start(f32[4,128,128]{2,1,0:T(8,128)} %bitcast.16), channel_id=1, source_target_pairs={{1,0},{2,1},{3,2},{4,3},{5,4},{6,5},{7,6},{8,7},{9,8},{10,9},{11,1... | collective-permute-start | bytes 786440 | tf_op jit(solution)/shard_map/ppermute | solution.py:200
  7.3 0.9 copy-start.1
  8.3 0.9 copy-start.7
  9.2 4.7 %collective-permute-start = (bf16[4,128,128]{2,1,0:T(8,128)(2,1)S(1)}, bf16[4,128,128]{2,1,0:T(8,128)(2,1)}, u32[]{:S(2)}, u32[]{:S(2)}) collective-permute-start(bf16[4,128,128]{2,1,0:T(8,128)(2,1)S(1)} %shard_map.104), channel_id=1, source_target_pairs={{0,1},{16,17},{32,33},{48,49},{64,65},{80,81},{96,97},{112,113}} | collective-permute-start | bytes 393224 | tf_op jit(solution)/shard_map/ppermute | solution.py:190
  14.6 2.4 %collective-permute-start.1 = (bf16[4,128,128]{2,1,0:T(8,128)(2,1)}, bf16[4,128,128]{2,1,0:T(8,128)(2,1)}, u32[]{:S(2)}, u32[]{:S(2)}) collective-permute-start(bf16[4,128,128]{2,1,0:T(8,128)(2,1)} %broadcast_select_fusion.3), channel_id=1, source_target_pairs={{0,3},{1,2},{16,19},{17,18},{32,35},{33,34},{48,51},{49,50},{64,67... | collective-permute-start | bytes 393224 | tf_op jit(solution)/shard_map/ppermute | solution.py:190
  16.1 3.9 %copy-start.9 = (s32[4]{0:T(128)}, s32[4]{0:T(128)S(1)}, u32[]{:S(2)}) copy-start(s32[4]{0:T(128)S(1)} %select_reduce_fusion.3) | copy-start | bytes 52
  17.9 3.7 %copy-start.8 = (bf16[4,128,128]{2,1,0:T(8,128)(2,1)}, bf16[4,128,128]{2,1,0:T(8,128)(2,1)S(1)}, u32[]{:S(2)}) copy-start(bf16[4,128,128]{2,1,0:T(8,128)(2,1)S(1)} %broadcast_select_fusion.7) | copy-start | bytes 393220
  18.0 3.7 %collective-permute-start.2 = (bf16[4,128,128]{2,1,0:T(8,128)(2,1)S(1)}, bf16[4,128,128]{2,1,0:T(8,128)(2,1)}, u32[]{:S(2)}, u32[]{:S(2)}) collective-permute-start(bf16[4,128,128]{2,1,0:T(8,128)(2,1)S(1)} %broadcast_select_fusion.7), channel_id=1, source_target_pairs={{0,4},{1,5},{2,6},{3,7},{16,20},{17,21},{18,22},{19,23},{32,36},{3... | collective-permute-start | bytes 393224 | tf_op jit(solution)/shard_map/ppermute | solution.py:190
  22.5 7.0 %collective-permute-start.3 = (bf16[4,128,128]{2,1,0:T(8,128)(2,1)S(1)}, bf16[4,128,128]{2,1,0:T(8,128)(2,1)}, u32[]{:S(2)}, u32[]{:S(2)}) collective-permute-start(bf16[4,128,128]{2,1,0:T(8,128)(2,1)S(1)} %broadcast_select_fusion.11), channel_id=1, source_target_pairs={{0,12},{1,13},{2,14},{3,15},{4,8},{5,9},{6,10},{7,11},{16,28},{17,... | collective-permute-start | bytes 393224 | tf_op jit(solution)/shard_map/ppermute | solution.py:190
  30.5 7.9 %collective-permute-start.6 = (bf16[4,128,128]{2,1,0:T(8,128)(2,1)S(1)}, bf16[4,128,128]{2,1,0:T(8,128)(2,1)S(1)}, u32[]{:S(2)}, u32[]{:S(2)}) collective-permute-start(bf16[4,128,128]{2,1,0:T(8,128)(2,1)S(1)} %broadcast_select_fusion.15.refs_0_.refs_8_), channel_id=1, source_target_pairs={{0,96},{16,112},{32,64},{48,80},{64,32},{80,48},{96,0},{112,16},{1... | collective-permute-start | bytes 393224 | tf_op jit(solution)/shard_map/ppermute | solution.py:165
  34.3 6.7 %collective-permute-start.5 = (bf16[4,128,128]{2,1,0:T(8,128)(2,1)S(1)}, bf16[4,128,128]{2,1,0:T(8,128)(2,1)S(1)}, u32[]{:S(2)}, u32[]{:S(2)}) collective-permute-start(bf16[4,128,128]{2,1,0:T(8,128)(2,1)S(1)} %broadcast_select_fusion.15.refs_0_.refs_8_), channel_id=1, source_target_pairs={{0,64},{16,80},{32,96},{48,112},{64,0},{80,16},{96,32},{112,48},{1... | collective-permute-start | bytes 393224 | tf_op jit(solution)/shard_map/ppermute | solution.py:165
  34.3 8.9 %collective-permute-start.4 = (bf16[4,128,128]{2,1,0:T(8,128)(2,1)S(1)}, bf16[4,128,128]{2,1,0:T(8,128)(2,1)S(1)}, u32[]{:S(2)}, u32[]{:S(2)}) collective-permute-start(bf16[4,128,128]{2,1,0:T(8,128)(2,1)S(1)} %broadcast_select_fusion.15.refs_0_.refs_8_), channel_id=1, source_target_pairs={{0,32},{16,48},{32,0},{48,16},{64,96},{80,112},{96,64},{112,80},{1... | collective-permute-start | bytes 393224 | tf_op jit(solution)/shard_map/ppermute | solution.py:165
  35.7 8.3 %collective-permute-start.7 = (bf16[4,128,128]{2,1,0:T(8,128)(2,1)S(1)}, bf16[4,128,128]{2,1,0:T(8,128)(2,1)S(1)}, u32[]{:S(2)}, u32[]{:S(2)}) collective-permute-start(bf16[4,128,128]{2,1,0:T(8,128)(2,1)S(1)} %broadcast_select_fusion.15.refs_0_.refs_8_), channel_id=1, source_target_pairs={{0,16},{16,0},{32,48},{48,32},{64,80},{80,64},{96,112},{112,96},{1... | collective-permute-start | bytes 393224 | tf_op jit(solution)/shard_map/ppermute | solution.py:165
  38.4 5.6 %collective-permute-start.10 = (bf16[4,128,128]{2,1,0:T(8,128)(2,1)S(1)}, bf16[4,128,128]{2,1,0:T(8,128)(2,1)S(1)}, u32[]{:S(2)}, u32[]{:S(2)}) collective-permute-start(bf16[4,128,128]{2,1,0:T(8,128)(2,1)S(1)} %collective-permute-done.6.refs_3_), channel_id=1, source_target_pairs={{0,16},{16,0},{32,48},{48,32},{64,80},{80,64},{96,112},{112,96},{1... | collective-permute-start | bytes 393224 | tf_op jit(solution)/shard_map/ppermute | solution.py:165
  41.1 3.1 %collective-permute-start.9 = (bf16[4,128,128]{2,1,0:T(8,128)(2,1)S(1)}, bf16[4,128,128]{2,1,0:T(8,128)(2,1)S(1)}, u32[]{:S(2)}, u32[]{:S(2)}) collective-permute-start(bf16[4,128,128]{2,1,0:T(8,128)(2,1)S(1)} %collective-permute-done.5.refs_2_), channel_id=1, source_target_pairs={{0,16},{16,0},{32,48},{48,32},{64,80},{80,64},{96,112},{112,96},{1... | collective-permute-start | bytes 393224 | tf_op jit(solution)/shard_map/ppermute | solution.py:165
  43.2 1.3 collective-permute-start.8
  44.6 1.0 copy-start.2
  45.5 0.9 copy-start.6
  47.1 35.3 %copy-start.3 = (f32[4,128,128]{2,1,0:T(8,128)S(1)}, f32[4,128,128]{2,1,0:T(8,128)}, u32[]{:S(2)}) copy-start(f32[4,128,128]{2,1,0:T(8,128)} %refs_10_.5) | copy-start | bytes 786436
  47.1 35.2 %copy-start.5 = (bf16[1,512,128]{2,1,0:T(8,128)(2,1)S(1)}, bf16[1,512,128]{2,1,0:T(8,128)(2,1)}, u32[]{:S(2)}) copy-start(bf16[1,512,128]{2,1,0:T(8,128)(2,1)} %get-tuple-element.15) | copy-start | bytes 393220
  47.1 0.8 collective-permute-start.12
  47.9 0.7 collective-permute-start.13
  48.6 0.7 collective-permute-start.14
  49.4 12.6 %collective-permute-start.15 = (bf16[4,128,128]{2,1,0:T(8,128)(2,1)S(1)}, bf16[4,128,128]{2,1,0:T(8,128)(2,1)S(1)}, u32[]{:S(2)}, u32[]{:S(2)}) collective-permute-start(bf16[4,128,128]{2,1,0:T(8,128)(2,1)S(1)} %broadcast_select_fusion.10), channel_id=1, source_target_pairs={{0,12},{1,13},{2,14},{3,15},{4,8},{5,9},{6,10},{7,11},{16,28},{17,... | collective-permute-start | bytes 393224 | tf_op jit(solution)/shard_map/ppermute | solution.py:190
  62.0 14.3 %collective-permute-start.18 = (bf16[4,128,128]{2,1,0:T(8,128)(2,1)S(1)}, bf16[4,128,128]{2,1,0:T(8,128)(2,1)S(1)}, u32[]{:S(2)}, u32[]{:S(2)}) collective-permute-start(bf16[4,128,128]{2,1,0:T(8,128)(2,1)S(1)} %broadcast_select_fusion.14.refs_0_.refs_9_), channel_id=1, source_target_pairs={{0,96},{16,112},{32,64},{48,80},{64,32},{80,48},{96,0},{112,16},{1... | collective-permute-start | bytes 393224 | tf_op jit(solution)/shard_map/ppermute | solution.py:165
  64.6 16.4 %collective-permute-start.23 = (f32[4,128,128]{2,1,0:T(8,128)S(1)}, f32[4,128,128]{2,1,0:T(8,128)S(1)}, u32[]{:S(2)}, u32[]{:S(2)}) collective-permute-start(f32[4,128,128]{2,1,0:T(8,128)S(1)} %shard_map.106), channel_id=1, source_target_pairs={{1,0},{2,1},{3,2},{4,3},{5,4},{6,5},{7,6},{8,7},{9,8},{10,9},{11,1... | collective-permute-start | bytes 786440 | tf_op jit(solution)/shard_map/ppermute | solution.py:200
  70.9 5.4 %collective-permute-start.17 = (bf16[4,128,128]{2,1,0:T(8,128)(2,1)S(1)}, bf16[4,128,128]{2,1,0:T(8,128)(2,1)S(1)}, u32[]{:S(2)}, u32[]{:S(2)}) collective-permute-start(bf16[4,128,128]{2,1,0:T(8,128)(2,1)S(1)} %broadcast_select_fusion.14.refs_0_.refs_9_), channel_id=1, source_target_pairs={{0,64},{16,80},{32,96},{48,112},{64,0},{80,16},{96,32},{112,48},{1... | collective-permute-start | bytes 393224 | tf_op jit(solution)/shard_map/ppermute | solution.py:165
  72.3 8.7 %collective-permute-start.16 = (bf16[4,128,128]{2,1,0:T(8,128)(2,1)S(1)}, bf16[4,128,128]{2,1,0:T(8,128)(2,1)S(1)}, u32[]{:S(2)}, u32[]{:S(2)}) collective-permute-start(bf16[4,128,128]{2,1,0:T(8,128)(2,1)S(1)} %broadcast_select_fusion.14.refs_0_.refs_9_), channel_id=1, source_target_pairs={{0,32},{16,48},{32,0},{48,16},{64,96},{80,112},{96,64},{112,80},{1... | collective-permute-start | bytes 393224 | tf_op jit(solution)/shard_map/ppermute | solution.py:165
  72.3 8.7 %collective-permute-start.19 = (bf16[4,128,128]{2,1,0:T(8,128)(2,1)S(1)}, bf16[4,128,128]{2,1,0:T(8,128)(2,1)S(1)}, u32[]{:S(2)}, u32[]{:S(2)}) collective-permute-start(bf16[4,128,128]{2,1,0:T(8,128)(2,1)S(1)} %broadcast_select_fusion.14.refs_0_.refs_9_), channel_id=1, source_target_pairs={{0,16},{16,0},{32,48},{48,32},{64,80},{80,64},{96,112},{112,96},{1... | collective-permute-start | bytes 393224 | tf_op jit(solution)/shard_map/ppermute | solution.py:165
  76.3 4.7 %collective-permute-start.22 = (bf16[4,128,128]{2,1,0:T(8,128)(2,1)S(1)}, bf16[4,128,128]{2,1,0:T(8,128)(2,1)S(1)}, u32[]{:S(2)}, u32[]{:S(2)}) collective-permute-start(bf16[4,128,128]{2,1,0:T(8,128)(2,1)S(1)} %collective-permute-done.18.refs_3_), channel_id=1, source_target_pairs={{0,16},{16,0},{32,48},{48,32},{64,80},{80,64},{96,112},{112,96},{1... | collective-permute-start | bytes 393224 | tf_op jit(solution)/shard_map/ppermute | solution.py:165
  76.3 5.7 %collective-permute-start.21 = (bf16[4,128,128]{2,1,0:T(8,128)(2,1)S(1)}, bf16[4,128,128]{2,1,0:T(8,128)(2,1)S(1)}, u32[]{:S(2)}, u32[]{:S(2)}) collective-permute-start(bf16[4,128,128]{2,1,0:T(8,128)(2,1)S(1)} %collective-permute-done.17.refs_2_), channel_id=1, source_target_pairs={{0,16},{16,0},{32,48},{48,32},{64,80},{80,64},{96,112},{112,96},{1... | collective-permute-start | bytes 393224 | tf_op jit(solution)/shard_map/ppermute | solution.py:165
  81.0 1.3 collective-permute-start.20
  83.0 32.1 %copy-start.4 = (bf16[1,512,128]{2,1,0:T(8,128)(2,1)S(1)}, bf16[1,512,128]{2,1,0:T(8,128)(2,1)}, u32[]{:S(2)}) copy-start(bf16[1,512,128]{2,1,0:T(8,128)(2,1)} %get-tuple-element.12) | copy-start | bytes 393220
  83.0 0.8 collective-permute-start.24
  83.8 0.7 collective-permute-start.25
  84.6 0.7 collective-permute-start.26
  85.3 10.1 %collective-permute-start.27 = (bf16[4,128,128]{2,1,0:T(8,128)(2,1)S(1)}, bf16[4,128,128]{2,1,0:T(8,128)(2,1)S(1)}, u32[]{:S(2)}, u32[]{:S(2)}) collective-permute-start(bf16[4,128,128]{2,1,0:T(8,128)(2,1)S(1)} %broadcast_select_fusion.9), channel_id=1, source_target_pairs={{0,12},{1,13},{2,14},{3,15},{4,8},{5,9},{6,10},{7,11},{16,28},{17,... | collective-permute-start | bytes 393224 | tf_op jit(solution)/shard_map/ppermute | solution.py:190
  95.4 14.3 %collective-permute-start.30 = (bf16[4,128,128]{2,1,0:T(8,128)(2,1)S(1)}, bf16[4,128,128]{2,1,0:T(8,128)(2,1)S(1)}, u32[]{:S(2)}, u32[]{:S(2)}) collective-permute-start(bf16[4,128,128]{2,1,0:T(8,128)(2,1)S(1)} %broadcast_select_fusion.13.refs_0_.refs_10_), channel_id=1, source_target_pairs={{0,96},{16,112},{32,64},{48,80},{64,32},{80,48},{96,0},{112,16},{1... | collective-permute-start | bytes 393224 | tf_op jit(solution)/shard_map/ppermute | solution.py:165
  96.6 17.5 %collective-permute-start.35 = (f32[4,128,128]{2,1,0:T(8,128)S(1)}, f32[4,128,128]{2,1,0:T(8,128)S(1)}, u32[]{:S(2)}, u32[]{:S(2)}) collective-permute-start(f32[4,128,128]{2,1,0:T(8,128)S(1)} %shard_map.108), channel_id=1, source_target_pairs={{1,0},{2,1},{3,2},{4,3},{5,4},{6,5},{7,6},{8,7},{9,8},{10,9},{11,1... | collective-permute-start | bytes 786440 | tf_op jit(solution)/shard_map/ppermute | solution.py:200
  102.9 6.9 %collective-permute-start.29 = (bf16[4,128,128]{2,1,0:T(8,128)(2,1)S(1)}, bf16[4,128,128]{2,1,0:T(8,128)(2,1)S(1)}, u32[]{:S(2)}, u32[]{:S(2)}) collective-permute-start(bf16[4,128,128]{2,1,0:T(8,128)(2,1)S(1)} %broadcast_select_fusion.13.refs_0_.refs_10_), channel_id=1, source_target_pairs={{0,64},{16,80},{32,96},{48,112},{64,0},{80,16},{96,32},{112,48},{1... | collective-permute-start | bytes 393224 | tf_op jit(solution)/shard_map/ppermute | solution.py:165
  103.7 9.8 %collective-permute-start.28 = (bf16[4,128,128]{2,1,0:T(8,128)(2,1)S(1)}, bf16[4,128,128]{2,1,0:T(8,128)(2,1)S(1)}, u32[]{:S(2)}, u32[]{:S(2)}) collective-permute-start(bf16[4,128,128]{2,1,0:T(8,128)(2,1)S(1)} %broadcast_select_fusion.13.refs_0_.refs_10_), channel_id=1, source_target_pairs={{0,32},{16,48},{32,0},{48,16},{64,96},{80,112},{96,64},{112,80},{1... | collective-permute-start | bytes 393224 | tf_op jit(solution)/shard_map/ppermute | solution.py:165
  105.3 8.8 %collective-permute-start.31 = (bf16[4,128,128]{2,1,0:T(8,128)(2,1)S(1)}, bf16[4,128,128]{2,1,0:T(8,128)(2,1)S(1)}, u32[]{:S(2)}, u32[]{:S(2)}) collective-permute-start(bf16[4,128,128]{2,1,0:T(8,128)(2,1)S(1)} %broadcast_select_fusion.13.refs_0_.refs_10_), channel_id=1, source_target_pairs={{0,16},{16,0},{32,48},{48,32},{64,80},{80,64},{96,112},{112,96},{1... | collective-permute-start | bytes 393224 | tf_op jit(solution)/shard_map/ppermute | solution.py:165
  109.8 4.4 %collective-permute-start.34 = (bf16[4,128,128]{2,1,0:T(8,128)(2,1)S(1)}, bf16[4,128,128]{2,1,0:T(8,128)(2,1)S(1)}, u32[]{:S(2)}, u32[]{:S(2)}) collective-permute-start(bf16[4,128,128]{2,1,0:T(8,128)(2,1)S(1)} %collective-permute-done.30.refs_3_), channel_id=1, source_target_pairs={{0,16},{16,0},{32,48},{48,32},{64,80},{80,64},{96,112},{112,96},{1... | collective-permute-start | bytes 393224 | tf_op jit(solution)/shard_map/ppermute | solution.py:165
  109.8 4.8 %collective-permute-start.33 = (bf16[4,128,128]{2,1,0:T(8,128)(2,1)S(1)}, bf16[4,128,128]{2,1,0:T(8,128)(2,1)S(1)}, u32[]{:S(2)}, u32[]{:S(2)}) collective-permute-start(bf16[4,128,128]{2,1,0:T(8,128)(2,1)S(1)} %collective-permute-done.29.refs_2_), channel_id=1, source_target_pairs={{0,16},{16,0},{32,48},{48,32},{64,80},{80,64},{96,112},{112,96},{1... | collective-permute-start | bytes 393224 | tf_op jit(solution)/shard_map/ppermute | solution.py:165
  113.6 1.5 %collective-permute-start.32 = (bf16[4,128,128]{2,1,0:T(8,128)(2,1)S(1)}, bf16[4,128,128]{2,1,0:T(8,128)(2,1)S(1)}, u32[]{:S(2)}, u32[]{:S(2)}) collective-permute-start(bf16[4,128,128]{2,1,0:T(8,128)(2,1)S(1)} %collective-permute-done.28.refs_1_), channel_id=1, source_target_pairs={{0,16},{16,0},{32,48},{48,32},{64,80},{80,64},{96,112},{112,96},{1... | collective-permute-start | bytes 393224 | tf_op jit(solution)/shard_map/ppermute | solution.py:165
  115.7 0.7 collective-permute-start.36
  116.5 0.7 collective-permute-start.37
  117.2 0.7 collective-permute-start.38
  117.9 9.9 %collective-permute-start.39 = (bf16[4,128,128]{2,1,0:T(8,128)(2,1)S(1)}, bf16[4,128,128]{2,1,0:T(8,128)(2,1)S(1)}, u32[]{:S(2)}, u32[]{:S(2)}) collective-permute-start(bf16[4,128,128]{2,1,0:T(8,128)(2,1)S(1)} %broadcast_select_fusion.8), channel_id=1, source_target_pairs={{0,12},{1,13},{2,14},{3,15},{4,8},{5,9},{6,10},{7,11},{16,28},{17,... | collective-permute-start | bytes 393224 | tf_op jit(solution)/shard_map/ppermute | solution.py:190
  127.8 14.3 %collective-permute-start.42 = (bf16[4,128,128]{2,1,0:T(8,128)(2,1)S(1)}, bf16[4,128,128]{2,1,0:T(8,128)(2,1)S(1)}, u32[]{:S(2)}, u32[]{:S(2)}) collective-permute-start(bf16[4,128,128]{2,1,0:T(8,128)(2,1)S(1)} %broadcast_select_fusion.12.refs_0_.refs_11_), channel_id=1, source_target_pairs={{0,96},{16,112},{32,64},{48,80},{64,32},{80,48},{96,0},{112,16},{1... | collective-permute-start | bytes 393224 | tf_op jit(solution)/shard_map/ppermute | solution.py:165
  129.1 17.4 %collective-permute-start.47 = (f32[4,128,128]{2,1,0:T(8,128)S(1)}, f32[4,128,128]{2,1,0:T(8,128)S(1)}, u32[]{:S(2)}, u32[]{:S(2)}) collective-permute-start(f32[4,128,128]{2,1,0:T(8,128)S(1)} %shard_map.110), channel_id=1, source_target_pairs={{1,0},{2,1},{3,2},{4,3},{5,4},{6,5},{7,6},{8,7},{9,8},{10,9},{11,1... | collective-permute-start | bytes 786440 | tf_op jit(solution)/shard_map/ppermute | solution.py:200
  135.4 6.7 %collective-permute-start.41 = (bf16[4,128,128]{2,1,0:T(8,128)(2,1)S(1)}, bf16[4,128,128]{2,1,0:T(8,128)(2,1)S(1)}, u32[]{:S(2)}, u32[]{:S(2)}) collective-permute-start(bf16[4,128,128]{2,1,0:T(8,128)(2,1)S(1)} %broadcast_select_fusion.12.refs_0_.refs_11_), channel_id=1, source_target_pairs={{0,64},{16,80},{32,96},{48,112},{64,0},{80,16},{96,32},{112,48},{1... | collective-permute-start | bytes 393224 | tf_op jit(solution)/shard_map/ppermute | solution.py:165
  135.9 10.2 %collective-permute-start.40 = (bf16[4,128,128]{2,1,0:T(8,128)(2,1)S(1)}, bf16[4,128,128]{2,1,0:T(8,128)(2,1)S(1)}, u32[]{:S(2)}, u32[]{:S(2)}) collective-permute-start(bf16[4,128,128]{2,1,0:T(8,128)(2,1)S(1)} %broadcast_select_fusion.12.refs_0_.refs_11_), channel_id=1, source_target_pairs={{0,32},{16,48},{32,0},{48,16},{64,96},{80,112},{96,64},{112,80},{1... | collective-permute-start | bytes 393224 | tf_op jit(solution)/shard_map/ppermute | solution.py:165
  137.5 8.9 %collective-permute-start.43 = (bf16[4,128,128]{2,1,0:T(8,128)(2,1)S(1)}, bf16[4,128,128]{2,1,0:T(8,128)(2,1)S(1)}, u32[]{:S(2)}, u32[]{:S(2)}) collective-permute-start(bf16[4,128,128]{2,1,0:T(8,128)(2,1)S(1)} %broadcast_select_fusion.12.refs_0_.refs_11_), channel_id=1, source_target_pairs={{0,16},{16,0},{32,48},{48,32},{64,80},{80,64},{96,112},{112,96},{1... | collective-permute-start | bytes 393224 | tf_op jit(solution)/shard_map/ppermute | solution.py:165
  142.1 4.4 %collective-permute-start.46 = (bf16[4,128,128]{2,1,0:T(8,128)(2,1)S(1)}, bf16[4,128,128]{2,1,0:T(8,128)(2,1)S(1)}, u32[]{:S(2)}, u32[]{:S(2)}) collective-permute-start(bf16[4,128,128]{2,1,0:T(8,128)(2,1)S(1)} %collective-permute-done.42.refs_3_), channel_id=1, source_target_pairs={{0,16},{16,0},{32,48},{48,32},{64,80},{80,64},{96,112},{112,96},{1... | collective-permute-start | bytes 393224 | tf_op jit(solution)/shard_map/ppermute | solution.py:165
  142.1 4.9 %collective-permute-start.45 = (bf16[4,128,128]{2,1,0:T(8,128)(2,1)S(1)}, bf16[4,128,128]{2,1,0:T(8,128)(2,1)S(1)}, u32[]{:S(2)}, u32[]{:S(2)}) collective-permute-start(bf16[4,128,128]{2,1,0:T(8,128)(2,1)S(1)} %collective-permute-done.41.refs_2_), channel_id=1, source_target_pairs={{0,16},{16,0},{32,48},{48,32},{64,80},{80,64},{96,112},{112,96},{1... | collective-permute-start | bytes 393224 | tf_op jit(solution)/shard_map/ppermute | solution.py:165
  146.0 1.4 collective-permute-start.44

commit v3 on v2

--- a/solution.py
+++ b/solution.py
@@ -1,3 +1,5 @@
+import functools
+
 import jax
 import jax.numpy as jnp
 from jax import lax
@@ -7,10 +9,11 @@
 
 
 GROUP = 4
-UNROLL = 4
-PLACES = 112
+UNROLL = 9
+GROUPS = 27
+PLACES = GROUP * GROUPS
 ZERO_COLUMN = 32
-COUNT_WORD = 144
+COUNT_WORD = PLACES + GROUPS
 PIECES = 8
 
 
@@ -39,47 +42,116 @@
     lax.fori_loop(0, (meta[COUNT_WORD] + UNROLL - 1) // UNROLL, several, 0)
 
 
+def parts(value):
+    high = value.astype(jnp.bfloat16)
+    return high, (value - high.astype(jnp.float32)).astype(jnp.bfloat16)
+
+
 def solve(inverse, excitation, field, solved):
     for b in range(inverse.shape[0]):
+        high, low = parts(inverse[b])
+        right_high, right_low = parts(excitation[b].astype(jnp.float32) - field[b])
         solved[b] = jnp.dot(
-            inverse[b],
-            excitation[b].astype(jnp.float32) - field[b],
-            precision=lax.Precision.HIGHEST,
+            jnp.concatenate([high, high, low], axis=1),
+            jnp.concatenate([right_high, right_low, right_high], axis=0),
             preferred_element_type=jnp.float32,
         ).astype(solved.dtype)
 
 
-def first_kernel(lag, excitation, base, inverse, solved):
-    @pl.when(lag[0] == 0)
-    def _():
-        solve(inverse, excitation, base, solved)
-
-    @pl.when(lag[0] != 0)
+def words_kernel(place_of, tables, *refs):
+    kept, held_refs, (words, tally, arrivals) = refs[:3], refs[4:7], (refs[3],) + refs[7:]
+    moves = [
+        pltpu.make_async_copy(source, target, arrivals.at[at])
+        for at, (source, target) in enumerate(zip(kept, held_refs))
+    ]
+    for copy in moves:
+        copy.start()
+    slots = (tables.shape[0] - 2 * PIECES - 1) // 3
+    live = tables[3 * slots + 2 * PIECES]
+    rows = tally.shape[0]
+    for b in range(rows):
+        tally[b] = 0
+
+    def clear(at, carry):
+        words[at] = jnp.where(at < PLACES, ZERO_COLUMN, 0)
+        return carry
+
+    lax.fori_loop(0, COUNT_WORD + 1, clear, 0, unroll=8)
+
+    def count_row(slot, carry):
+        tally[tables[slot]] += 1
+        return carry
+
+    lax.fori_loop(0, live, count_row, 0)
+    first = 0
+    for b in range(rows):
+        groups = (tally[b] + GROUP - 1) // GROUP
+
+        def name_row(group, carry, b=b):
+            words[PLACES + group] = b
+            return carry
+
+        tally[b] = first * GROUP
+        lax.fori_loop(first, first + groups, name_row, 0)
+        first = first + groups
+    words[COUNT_WORD] = first
+
+    def put(slot, carry):
+        row = tables[slot]
+        place = tally[row]
+        tally[row] = place + 1
+        owner = tables[slots + slot]
+        apart = owner ^ place_of[1]
+        piece = (apart & 1) * (PIECES // 2) + (apart >> 1)
+        local = tables[3 * slots + tables[2 * slots + slot] * PIECES + owner]
+        words[place] = slot * 64 + piece * rows + local
+        return carry
+
+    lax.fori_loop(0, live, put, 0)
+    for copy in moves:
+        copy.wait()
+
+
+def first_kernel(place_of, excitation, base, inverse, solved, right, field, factors, arrivals):
+    @pl.when(place_of[0] == 0)
+    def _():
+        copies = [
+            pltpu.make_async_copy(excitation.at[0], right, arrivals.at[0]),
+            pltpu.make_async_copy(base, field, arrivals.at[1]),
+            pltpu.make_async_copy(inverse, factors, arrivals.at[2]),
+        ]
+        for copy in copies:
+            copy.start()
+        for copy in copies:
+            copy.wait()
+        solve(factors, right, field, solved)
+
+    @pl.when(place_of[0] != 0)
     def _():
         solved[...] = jnp.zeros(solved.shape, solved.dtype)
 
 
-def chain_kernel(lag, meta, blocks, *refs):
+def chain_kernel(t, place_of, meta, blocks, *refs):
     pieces, (base, excitation, inverse, solved, gathered, sums, arrivals) = refs[:PIECES], refs[PIECES:]
 
-    @pl.when(lag[0] == 0)
+    @pl.when(place_of[0] == 0)
     def _():
         accumulate(meta, blocks, pieces, base, gathered, sums, arrivals)
-        solve(inverse, excitation, sums, solved)
-
-    @pl.when(lag[0] != 0)
+        solve(inverse, excitation.at[t], sums, solved)
+
+    @pl.when(place_of[0] != 0)
     def _():
         solved[...] = jnp.zeros(solved.shape, solved.dtype)
 
 
-def others_kernel(lag, meta, blocks, *refs):
+def others_kernel(place_of, meta, blocks, *refs):
     pieces, (base, total, gathered, arrivals) = refs[:PIECES], refs[PIECES:]
 
-    @pl.when(lag[0] != 0)
+    @pl.when(place_of[0] != 0)
     def _():
         accumulate(meta, blocks, pieces, base, gathered, total, arrivals)
 
-    @pl.when(lag[0] == 0)
+    @pl.when(place_of[0] == 0)
     def _():
         total[...] = jnp.zeros(total.shape, total.dtype)
 
@@ -100,6 +172,7 @@
 SMEM = pl.BlockSpec(memory_space=pltpu.SMEM)
 VMEM = pl.BlockSpec(memory_space=pltpu.VMEM)
 ANY = pl.BlockSpec(memory_space=pl.ANY)
+HBM = pl.BlockSpec(memory_space=pltpu.HBM)
 
 
 def held(arrays):
@@ -113,29 +186,50 @@
     ]
 
 
-def first_solve(lag, excitation, base, inverse):
+def prepare(place_of, tables, kept, row_blocks):
+    shapes = [jax.ShapeDtypeStruct(each.shape, each.dtype) for each in kept]
+    words, *held_arrays = pl.pallas_call(
+        words_kernel,
+        out_shape=[jax.ShapeDtypeStruct((COUNT_WORD + 1,), jnp.int32)] + shapes,
+        in_specs=[SMEM, SMEM] + [HBM] * len(kept),
+        compiler_params=pltpu.CompilerParams(vmem_limit_bytes=48 * 1024 * 1024),
+        out_specs=[SMEM] + [VMEM] * len(kept),
+        scratch_shapes=[
+            pltpu.SMEM((row_blocks,), jnp.int32),
+            pltpu.SemaphoreType.DMA((len(kept),)),
+        ],
+    )(place_of, tables, *kept)
+    return words, held(held_arrays)
+
+
+def first_solve(place_of, excitation, base, inverse):
     return pl.pallas_call(
         first_kernel,
         out_shape=jax.ShapeDtypeStruct(base.shape, jnp.bfloat16),
-        in_specs=[SMEM, VMEM, VMEM, VMEM],
-        compiler_params=PARAMS,
+        in_specs=[SMEM, HBM, HBM, HBM],
         out_specs=VMEM,
-    )(lag, excitation, base, inverse)
-
-
-def chain_step(lag, meta, blocks, pieces, base, excitation, inverse):
+        scratch_shapes=[
+            pltpu.VMEM(base.shape, jnp.bfloat16),
+            pltpu.VMEM(base.shape, jnp.float32),
+            pltpu.VMEM(inverse.shape, jnp.float32),
+            pltpu.SemaphoreType.DMA((3,)),
+        ],
+    )(place_of, excitation, base, inverse)
+
+
+def chain_step(t, place_of, meta, blocks, pieces, base, excitation, inverse):
     gathered, arrivals = gathering(base)
     return pl.pallas_call(
-        chain_kernel,
+        functools.partial(chain_kernel, t),
         out_shape=jax.ShapeDtypeStruct(base.shape, jnp.bfloat16),
         in_specs=[SMEM, SMEM, VMEM] + [VMEM] * PIECES + [VMEM] * 3,
         compiler_params=PARAMS,
         out_specs=VMEM,
         scratch_shapes=[gathered, pltpu.VMEM(base.shape, jnp.float32), arrivals],
-    )(lag, meta, blocks, *held(pieces), base, excitation, inverse)
-
-
-def others_step(lag, meta, blocks, pieces, base):
+    )(place_of, meta, blocks, *held(pieces), base, excitation, inverse)
+
+
+def others_step(place_of, meta, blocks, pieces, base):
     return pl.pallas_call(
         others_kernel,
         out_shape=jax.ShapeDtypeStruct(base.shape, jnp.float32),
@@ -143,7 +237,7 @@
         compiler_params=PARAMS,
         out_specs=VMEM,
         scratch_shapes=gathering(base),
-    )(lag, meta, blocks, *held(pieces), base)
+    )(place_of, meta, blocks, *held(pieces), base)
 
 
 def last_step(meta, blocks, pieces, solved, base):
@@ -200,56 +294,34 @@
     return lax.ppermute(value, "lag", [(g + 1, g) for g in range(count - 1)])
 
 
-def slot_words(slot_row, slot_owner, slot_pos, needed, count, row_blocks):
-    slots = slot_row.shape[0]
-    at = jnp.arange(slots, dtype=jnp.int32)
-    live = at < count
-    table = needed.reshape(-1)
-    entry = slot_owner * needed.shape[-1] + slot_pos
-    entries = jnp.arange(table.shape[0], dtype=jnp.int32)
-    local = jnp.sum(jnp.where(entry[:, None] == entries[None, :], table[None, :], 0), axis=1)
-    apart = slot_owner ^ lax.axis_index("rows")
-    column = ((apart & 1) * 4 + (apart >> 1)) * row_blocks + local
-    word = at * 64 + column
-    earlier = (slot_row[None, :] == slot_row[:, None]) & (at[None, :] < at[:, None])
-    rank = jnp.sum(earlier.astype(jnp.int32), axis=1)
-    row_at = jnp.arange(row_blocks, dtype=jnp.int32)
-    in_row = (slot_row[None, :] == row_at[:, None]) & live[None, :]
-    groups = (jnp.sum(in_row.astype(jnp.int32), axis=1) + GROUP - 1) // GROUP
-    first = jnp.sum(jnp.where(row_at[None, :] < row_at[:, None], groups[None, :], 0), axis=1)
-    start = jnp.sum(jnp.where(slot_row[:, None] == row_at[None, :], first[None, :], 0), axis=1)
-    place = jnp.where(live, start * GROUP + rank, -1)
-    taken = place[None, :] == jnp.arange(PLACES, dtype=jnp.int32)[:, None]
-    words = ZERO_COLUMN + jnp.sum(jnp.where(taken, word[None, :] - ZERO_COLUMN, 0), axis=1)
-    group_at = jnp.arange(COUNT_WORD - PLACES, dtype=jnp.int32)
-    group_row = jnp.sum((group_at[:, None] >= first[None, :]).astype(jnp.int32), axis=1) - 1
-    return jnp.concatenate([words, group_row, jnp.sum(groups)[None]])
-
-
 def per_device(
     excitation, pending, inverse, interaction, slot_row, slot_owner, slot_pos, needed, block_count
 ):
     row_blocks, block_size, _ = inverse.shape
     steps, rows, width = excitation.shape
     excitation_blocks = excitation.reshape(steps, row_blocks, block_size, width)
-    lag = jnp.full((1,), lax.axis_index("lag"), jnp.int32)
+    place_of = jnp.stack([lax.axis_index("lag"), lax.axis_index("rows")]).astype(jnp.int32)
     total = pending[0].reshape(row_blocks, block_size, width)
-    solved = first_solve(lag, excitation_blocks[0], total, inverse)
-    slot_row, solved = lax.optimization_barrier((slot_row, solved))
-    meta = slot_words(slot_row, slot_owner, slot_pos, needed[0], block_count[0, 0], row_blocks)
+    solved = first_solve(place_of, excitation_blocks, total, inverse)
+    tables = (slot_row, slot_owner, slot_pos, needed.transpose(0, 2, 1), block_count)
+    tables = jnp.concatenate([table.reshape(-1) for table in tables])
+    meta, (blocks, excitation_held, inverse_held) = prepare(
+        place_of, tables, (interaction, excitation_blocks, inverse), row_blocks
+    )
     outputs = []
-    (interaction,) = held((interaction,))
     for t in range(steps):
         solved = spread(solved)
         outputs.append(solved)
         if t > 0:
-            total = others_step(lag, meta, interaction, pieces, base)
+            total = others_step(place_of, meta, blocks, pieces, base)
         base = from_behind(total)
         pieces = exchange(solved)
         if t + 1 < steps:
-            solved = chain_step(lag, meta, interaction, pieces, base, excitation_blocks[t + 1], inverse)
+            solved = chain_step(
+                t + 1, place_of, meta, blocks, pieces, base, excitation_held, inverse_held
+            )
         else:
-            total, kept = last_step(meta, interaction, pieces, outputs, base)
+            total, kept = last_step(meta, blocks, pieces, outputs, base)
     return (kept.reshape(steps, rows, width), total.reshape(1, rows, width))
 
 

time: 151 us -> 147 us (0.974)
  other arithmetic: 11.2 us -> 1.82 us
  Pallas kernels: 12 us -> 17.3 us
  local copies, waits for them, and re-layouts: 6.45 us -> 3.14 us
  starting transfers between devices: 88.5 us -> 90.7 us
    reduce_sum x8 -> x0, other arithmetic: 4.83 us -> none  [the longest x1 0.91 us: slot_words(): rank = jnp.sum(earlier.astype(jnp.int32), axis=1)]
    ppermute x28, starting transfers between devices: 49.5 us -> 52.7 us  [over_rows(): return lax.ppermute(value, 'rows', [(r, r ^ flip) for r in range(count)])]
    pallas_call x3 -> x4, Pallas kernels: 1.95 us -> 5.05 us  [the longest x1 3.08 us: prepare(): pl.pallas_call(words_kernel, out_shape=[jax.ShapeDtypeStruct((COUNT_WORD...]
    unnamed x21 -> x6, local copies, waits for them, and re-layouts: 4.54 us -> 1.61 us
    select_n x16, other arithmetic: 3.66 us -> 1.18 us  [spread(): value = jnp.where(takes, arrived, value)]
    ppermute x16, starting transfers between devices: 15.4 us -> 13.2 us  [spread(): arrived = lax.ppermute(value, 'lag', pairs)]
    slice x1 -> x0, local copies, waits for them, and re-layouts: 1.84 us -> none  [per_device(): excitation_blocks[t + 1]]
  transfers between devices with their start and end apart: 48 -> 48, of which waited for: 12 -> 10; matrix products, arithmetic and copies ran while one was open for 9% -> 1% of each run, Pallas kernels for 5% -> 7%
where the time goes in v3:
time: 147 us; the launch traced here: 146 us
  starting transfers between devices  90.7 us (62%)
  waiting for transfers between devices  31.3 us (21%)
  Pallas kernels  17.3 us (12%)
  local copies, waits for them, and re-layouts  3.14 us (2%)
  between operations  2.04 us (1%)
  other arithmetic  1.82 us (1%)
    ppermute x28, starting transfers between devices, over_rows(): return lax.ppermute(value, 'rows', [(r, r ^ flip) for r in range(count)])  52.7 us
    ppermute x16, waiting for transfers between devices, spread(): arrived = lax.ppermute(value, 'lag', pairs)  27.9 us
    ppermute x4, starting transfers between devices, from_behind(): return lax.ppermute(value, 'lag', [(g + 1, g) for g in range(count - 1)])  24.8 us
    ppermute x16, starting transfers between devices, spread(): arrived = lax.ppermute(value, 'lag', pairs)  13.2 us
    pallas_call x3, Pallas kernels, others_step(): pl.pallas_call(others_kernel, out_shape=jax.ShapeDtypeStruct(base.shape,...  7.67 us
    ppermute x28, waiting for transfers between devices, over_rows(): return lax.ppermute(value, 'rows', [(r, r ^ flip) for r in range(count)])  3.32 us
    pallas_call x1, Pallas kernels, last_step(): pl.pallas_call(last_kernel, out_shape=(jax.ShapeDtypeStruct(base.shape, j...  3.23 us
    pallas_call x1, Pallas kernels, prepare(): pl.pallas_call(words_kernel, out_shape=[jax.ShapeDtypeStruct((COUNT_WORD...  3.08 us
  transfers between devices with their start and end apart: 48, of which 10 were waited for; matrix products, arithmetic and copies ran while one was open for 1% of the time, Pallas kernels for 7%

profile of v3, /device:TPU:25, one launch (start us, length us, event | category | flops | bytes accessed | tf_op | source)
XLA Modules:
  0.0 146.3 jit_solution(16160535942531543207)
XLA Ops:
  0.6 0.6 pad_add_fusion.place_of
  1.3 1.4 shard_map.105
  2.7 0.7 collective-permute-start
  3.4 0.9 broadcast_select_fusion.3
  4.3 0.7 collective-permute-start.1
  5.0 0.7 collective-permute-start.2
  5.7 1.3 collective-permute-start.3
  7.1 12.2 %collective-permute-done.3 = bf16[4,128,128]{2,1,0:T(8,128)(2,1)S(1)} collective-permute-done((bf16[4,128,128]{2,1,0:T(8,128)(2,1)S(1)}, bf16[4,128,128]{2,1,0:T(8,128)(2,1)S(1)}, u32[]{:S(2)}, u32[]{:S(2)}) %collective-permute-start.3) | collective-permute-done | bytes 131104 | tf_op jit(solution)/shard_map/ppermute | solution.py:284
  19.3 3.8 %collective-permute-start.6 = (bf16[4,128,128]{2,1,0:T(8,128)(2,1)S(1)}, bf16[4,128,128]{2,1,0:T(8,128)(2,1)S(1)}, u32[]{:S(2)}, u32[]{:S(2)}) collective-permute-start(bf16[4,128,128]{2,1,0:T(8,128)(2,1)S(1)} %broadcast_select_fusion.15.refs_0_.refs_8_), channel_id=1, source_target_pairs={{0,96},{16,112},{32,64},{48,80},{64,32},{80,48},{96,0},{112,16},{1... | collective-permute-start | bytes 393224 | tf_op jit(solution)/shard_map/ppermute | solution.py:259
  23.1 6.0 %collective-permute-start.11 = (f32[4,128,128]{2,1,0:T(8,128)}, f32[4,128,128]{2,1,0:T(8,128)S(1)}, u32[]{:S(2)}, u32[]{:S(2)}) collective-permute-start(f32[4,128,128]{2,1,0:T(8,128)} %bitcast.12), channel_id=1, source_target_pairs={{1,0},{2,1},{3,2},{4,3},{5,4},{6,5},{7,6},{8,7},{9,8},{10,9},{11,1... | collective-permute-start | bytes 786440 | tf_op jit(solution)/shard_map/ppermute | solution.py:294
  29.2 0.6 collective-permute-start.4
  29.8 5.0 %collective-permute-start.7 = (bf16[4,128,128]{2,1,0:T(8,128)(2,1)S(1)}, bf16[4,128,128]{2,1,0:T(8,128)(2,1)S(1)}, u32[]{:S(2)}, u32[]{:S(2)}) collective-permute-start(bf16[4,128,128]{2,1,0:T(8,128)(2,1)S(1)} %broadcast_select_fusion.15.refs_0_.refs_8_), channel_id=1, source_target_pairs={{0,16},{16,0},{32,48},{48,32},{64,80},{80,64},{96,112},{112,96},{1... | collective-permute-start | bytes 393224 | tf_op jit(solution)/shard_map/ppermute | solution.py:259
  34.8 5.6 %collective-permute-start.9 = (bf16[4,128,128]{2,1,0:T(8,128)(2,1)S(1)}, bf16[4,128,128]{2,1,0:T(8,128)(2,1)S(1)}, u32[]{:S(2)}, u32[]{:S(2)}) collective-permute-start(bf16[4,128,128]{2,1,0:T(8,128)(2,1)S(1)} %collective-permute-done.5.refs_2_), channel_id=1, source_target_pairs={{0,16},{16,0},{32,48},{48,32},{64,80},{80,64},{96,112},{112,96},{1... | collective-permute-start | bytes 393224 | tf_op jit(solution)/shard_map/ppermute | solution.py:259
  41.0 0.8 reshape.19
  41.8 0.8 concatenate.3.tables
  42.5 0.9 copy-done.1
  43.5 0.7 copy-done.2
  44.1 3.1 %shard_map.104 = (s32[136]{0:T(256)S(1)}, bf16[96,128,128]{2,1,0:T(8,128)(2,1)S(1)}, bf16[4,4,128,128]{3,2,1,0:T(8,128)(2,1)S(1)}, f32[4,128,128]{2,1,0:T(8,128)S(1)}) custom-call(s32[2]{0:T(128)S(1)} %copy-done.2, s32[305]{0:T(512)S(1)} %concatenate.3.tables, bf16[96,128,128]{2,1,0:T(8,128)(2,1)} %refs_0_.1, bf16[4,4,128,128]{3,2,1,0:T(8,128)(2,1)S(1)} %bitcast.10, ...), custom_call_target="tpu_custom_call" | custom-call | tf_op jit(solution)/shard_map/pallas_call | solution.py:191
  47.3 0.7 shard_map.106
  47.9 0.7 collective-permute-start.12
  48.7 0.7 collective-permute-start.13
  49.4 0.7 collective-permute-start.14
  50.1 1.3 collective-permute-start.15
  51.4 2.5 %shard_map.107 = f32[4,128,128]{2,1,0:T(8,128)S(1)} custom-call(s32[2]{0:T(128)S(1)} %copy-done.2, s32[136]{0:T(256)S(1)} %get-tuple-element.8.meta, bf16[96,128,128]{2,1,0:T(8,128)(2,1)S(1)} %get-tuple-element.9.blocks, bf16[4,128,128]{2,1,0:T(8,128)(2,1)S(1)} %broadcast_select_fusion.15.refs_0_.refs_8_, ...), custom_call_target="tpu_custom_call" | custom-call | tf_op jit(solution)/shard_map/pallas_call | solution.py:233
  53.9 4.6 %collective-permute-done.15 = bf16[4,128,128]{2,1,0:T(8,128)(2,1)S(1)} collective-permute-done((bf16[4,128,128]{2,1,0:T(8,128)(2,1)S(1)}, bf16[4,128,128]{2,1,0:T(8,128)(2,1)S(1)}, u32[]{:S(2)}, u32[]{:S(2)}) %collective-permute-start.15) | collective-permute-done | bytes 131104 | tf_op jit(solution)/shard_map/ppermute | solution.py:284
  58.5 2.6 %collective-permute-start.18 = (bf16[4,128,128]{2,1,0:T(8,128)(2,1)S(1)}, bf16[4,128,128]{2,1,0:T(8,128)(2,1)S(1)}, u32[]{:S(2)}, u32[]{:S(2)}) collective-permute-start(bf16[4,128,128]{2,1,0:T(8,128)(2,1)S(1)} %broadcast_select_fusion.14.refs_0_.refs_9_), channel_id=1, source_target_pairs={{0,96},{16,112},{32,64},{48,80},{64,32},{80,48},{96,0},{112,16},{1... | collective-permute-start | bytes 393224 | tf_op jit(solution)/shard_map/ppermute | solution.py:259
  61.0 6.3 %collective-permute-start.23 = (f32[4,128,128]{2,1,0:T(8,128)S(1)}, f32[4,128,128]{2,1,0:T(8,128)S(1)}, u32[]{:S(2)}, u32[]{:S(2)}) collective-permute-start(f32[4,128,128]{2,1,0:T(8,128)S(1)} %shard_map.107), channel_id=1, source_target_pairs={{1,0},{2,1},{3,2},{4,3},{5,4},{6,5},{7,6},{8,7},{9,8},{10,9},{11,1... | collective-permute-start | bytes 786440 | tf_op jit(solution)/shard_map/ppermute | solution.py:294
  67.5 0.5 collective-permute-start.16
  68.0 4.9 %collective-permute-start.19 = (bf16[4,128,128]{2,1,0:T(8,128)(2,1)S(1)}, bf16[4,128,128]{2,1,0:T(8,128)(2,1)S(1)}, u32[]{:S(2)}, u32[]{:S(2)}) collective-permute-start(bf16[4,128,128]{2,1,0:T(8,128)(2,1)S(1)} %broadcast_select_fusion.14.refs_0_.refs_9_), channel_id=1, source_target_pairs={{0,16},{16,0},{32,48},{48,32},{64,80},{80,64},{96,112},{112,96},{1... | collective-permute-start | bytes 393224 | tf_op jit(solution)/shard_map/ppermute | solution.py:259
  72.9 4.7 %collective-permute-start.21 = (bf16[4,128,128]{2,1,0:T(8,128)(2,1)S(1)}, bf16[4,128,128]{2,1,0:T(8,128)(2,1)S(1)}, u32[]{:S(2)}, u32[]{:S(2)}) collective-permute-start(bf16[4,128,128]{2,1,0:T(8,128)(2,1)S(1)} %collective-permute-done.17.refs_2_), channel_id=1, source_target_pairs={{0,16},{16,0},{32,48},{48,32},{64,80},{80,64},{96,112},{112,96},{1... | collective-permute-start | bytes 393224 | tf_op jit(solution)/shard_map/ppermute | solution.py:259
  77.7 1.0 collective-permute-done.21.refs_6_
  79.0 0.7 shard_map.108
  79.6 0.7 collective-permute-start.24
  80.4 0.7 collective-permute-start.25
  81.1 0.7 collective-permute-start.26
  81.8 1.3 collective-permute-start.27
  83.1 2.5 %shard_map.109 = f32[4,128,128]{2,1,0:T(8,128)S(1)} custom-call(s32[2]{0:T(128)S(1)} %copy-done.2, s32[136]{0:T(256)S(1)} %get-tuple-element.8.meta, bf16[96,128,128]{2,1,0:T(8,128)(2,1)S(1)} %get-tuple-element.9.blocks, bf16[4,128,128]{2,1,0:T(8,128)(2,1)S(1)} %broadcast_select_fusion.14.refs_0_.refs_9_, ...), custom_call_target="tpu_custom_call" | custom-call | tf_op jit(solution)/shard_map/pallas_call | solution.py:233
  85.6 5.8 %collective-permute-done.27 = bf16[4,128,128]{2,1,0:T(8,128)(2,1)S(1)} collective-permute-done((bf16[4,128,128]{2,1,0:T(8,128)(2,1)S(1)}, bf16[4,128,128]{2,1,0:T(8,128)(2,1)S(1)}, u32[]{:S(2)}, u32[]{:S(2)}) %collective-permute-start.27) | collective-permute-done | bytes 131104 | tf_op jit(solution)/shard_map/ppermute | solution.py:284
  91.4 1.2 collective-permute-start.30
  92.6 6.3 %collective-permute-start.35 = (f32[4,128,128]{2,1,0:T(8,128)S(1)}, f32[4,128,128]{2,1,0:T(8,128)S(1)}, u32[]{:S(2)}, u32[]{:S(2)}) collective-permute-start(f32[4,128,128]{2,1,0:T(8,128)S(1)} %shard_map.109), channel_id=1, source_target_pairs={{1,0},{2,1},{3,2},{4,3},{5,4},{6,5},{7,6},{8,7},{9,8},{10,9},{11,1... | collective-permute-start | bytes 786440 | tf_op jit(solution)/shard_map/ppermute | solution.py:294
  98.9 0.6 collective-permute-start.29
  99.5 1.7 %collective-permute-start.28 = (bf16[4,128,128]{2,1,0:T(8,128)(2,1)S(1)}, bf16[4,128,128]{2,1,0:T(8,128)(2,1)S(1)}, u32[]{:S(2)}, u32[]{:S(2)}) collective-permute-start(bf16[4,128,128]{2,1,0:T(8,128)(2,1)S(1)} %broadcast_select_fusion.13.refs_0_.refs_10_), channel_id=1, source_target_pairs={{0,32},{16,48},{32,0},{48,16},{64,96},{80,112},{96,64},{112,80},{1... | collective-permute-start | bytes 393224 | tf_op jit(solution)/shard_map/ppermute | solution.py:259
  101.3 4.5 %collective-permute-start.31 = (bf16[4,128,128]{2,1,0:T(8,128)(2,1)S(1)}, bf16[4,128,128]{2,1,0:T(8,128)(2,1)S(1)}, u32[]{:S(2)}, u32[]{:S(2)}) collective-permute-start(bf16[4,128,128]{2,1,0:T(8,128)(2,1)S(1)} %broadcast_select_fusion.13.refs_0_.refs_10_), channel_id=1, source_target_pairs={{0,16},{16,0},{32,48},{48,32},{64,80},{80,64},{96,112},{112,96},{1... | collective-permute-start | bytes 393224 | tf_op jit(solution)/shard_map/ppermute | solution.py:259
  105.8 3.8 %collective-permute-start.33 = (bf16[4,128,128]{2,1,0:T(8,128)(2,1)S(1)}, bf16[4,128,128]{2,1,0:T(8,128)(2,1)S(1)}, u32[]{:S(2)}, u32[]{:S(2)}) collective-permute-start(bf16[4,128,128]{2,1,0:T(8,128)(2,1)S(1)} %collective-permute-done.29.refs_2_), channel_id=1, source_target_pairs={{0,16},{16,0},{32,48},{48,32},{64,80},{80,64},{96,112},{112,96},{1... | collective-permute-start | bytes 393224 | tf_op jit(solution)/shard_map/ppermute | solution.py:259
  109.5 0.5 collective-permute-start.32
  110.1 0.4 collective-permute-done.33.refs_6_
  110.5 0.5 collective-permute-done.32.refs_5_
  111.1 0.7 shard_map.110
  111.7 0.7 collective-permute-start.36
  112.4 0.7 collective-permute-start.37
  113.2 0.7 collective-permute-start.38
  113.9 1.3 collective-permute-start.39
  115.2 2.7 %shard_map.111 = f32[4,128,128]{2,1,0:T(8,128)S(1)} custom-call(s32[2]{0:T(128)S(1)} %copy-done.2, s32[136]{0:T(256)S(1)} %get-tuple-element.8.meta, bf16[96,128,128]{2,1,0:T(8,128)(2,1)S(1)} %get-tuple-element.9.blocks, bf16[4,128,128]{2,1,0:T(8,128)(2,1)S(1)} %broadcast_select_fusion.13.refs_0_.refs_10_, ...), custom_call_target="tpu_custom_call" | custom-call | tf_op jit(solution)/shard_map/pallas_call | solution.py:233
  117.9 5.4 %collective-permute-done.39 = bf16[4,128,128]{2,1,0:T(8,128)(2,1)S(1)} collective-permute-done((bf16[4,128,128]{2,1,0:T(8,128)(2,1)S(1)}, bf16[4,128,128]{2,1,0:T(8,128)(2,1)S(1)}, u32[]{:S(2)}, u32[]{:S(2)}) %collective-permute-start.39) | collective-permute-done | bytes 131104 | tf_op jit(solution)/shard_map/ppermute | solution.py:284
  123.2 1.3 collective-permute-start.42
  124.6 6.3 %collective-permute-start.47 = (f32[4,128,128]{2,1,0:T(8,128)S(1)}, f32[4,128,128]{2,1,0:T(8,128)S(1)}, u32[]{:S(2)}, u32[]{:S(2)}) collective-permute-start(f32[4,128,128]{2,1,0:T(8,128)S(1)} %shard_map.111), channel_id=1, source_target_pairs={{1,0},{2,1},{3,2},{4,3},{5,4},{6,5},{7,6},{8,7},{9,8},{10,9},{11,1... | collective-permute-start | bytes 786440 | tf_op jit(solution)/shard_map/ppermute | solution.py:294
  130.8 0.6 collective-permute-start.41
  131.4 1.6 %collective-permute-start.40 = (bf16[4,128,128]{2,1,0:T(8,128)(2,1)S(1)}, bf16[4,128,128]{2,1,0:T(8,128)(2,1)S(1)}, u32[]{:S(2)}, u32[]{:S(2)}) collective-permute-start(bf16[4,128,128]{2,1,0:T(8,128)(2,1)S(1)} %broadcast_select_fusion.12.refs_0_.refs_11_), channel_id=1, source_target_pairs={{0,32},{16,48},{32,0},{48,16},{64,96},{80,112},{96,64},{112,80},{1... | collective-permute-start | bytes 393224 | tf_op jit(solution)/shard_map/ppermute | solution.py:259
  133.0 4.6 %collective-permute-start.43 = (bf16[4,128,128]{2,1,0:T(8,128)(2,1)S(1)}, bf16[4,128,128]{2,1,0:T(8,128)(2,1)S(1)}, u32[]{:S(2)}, u32[]{:S(2)}) collective-permute-start(bf16[4,128,128]{2,1,0:T(8,128)(2,1)S(1)} %broadcast_select_fusion.12.refs_0_.refs_11_), channel_id=1, source_target_pairs={{0,16},{16,0},{32,48},{48,32},{64,80},{80,64},{96,112},{112,96},{1... | collective-permute-start | bytes 393224 | tf_op jit(solution)/shard_map/ppermute | solution.py:259
  137.6 3.9 %collective-permute-start.45 = (bf16[4,128,128]{2,1,0:T(8,128)(2,1)S(1)}, bf16[4,128,128]{2,1,0:T(8,128)(2,1)S(1)}, u32[]{:S(2)}, u32[]{:S(2)}) collective-permute-start(bf16[4,128,128]{2,1,0:T(8,128)(2,1)S(1)} %collective-permute-done.41.refs_2_), channel_id=1, source_target_pairs={{0,16},{16,0},{32,48},{48,32},{64,80},{80,64},{96,112},{112,96},{1... | collective-permute-start | bytes 393224 | tf_op jit(solution)/shard_map/ppermute | solution.py:259
  141.5 0.4 collective-permute-start.44
  141.9 0.5 collective-permute-done.45.refs_6_
  142.5 0.4 collective-permute-done.44.refs_5_
  142.9 3.2 %shard_map.112 = (f32[4,128,128]{2,1,0:T(8,128)}, bf16[4,4,128,128]{3,2,1,0:T(8,128)(2,1)}) custom-call(s32[136]{0:T(256)S(1)} %get-tuple-element.8.meta, bf16[96,128,128]{2,1,0:T(8,128)(2,1)S(1)} %get-tuple-element.9.blocks, bf16[4,128,128]{2,1,0:T(8,128)(2,1)S(1)} %broadcast_select_fusion.12.refs_0_.refs_11_, ...), custom_call_target="tpu_custom_call" | custom-call | tf_op jit(solution)/shard_map/pallas_call | solution.py:244
  (66 shorter events, 1.0 us)
Async XLA Ops:
  0.6 41.9 %copy-start = (bf16[4,512,128]{2,1,0:T(8,128)(2,1)S(1)}, bf16[4,512,128]{2,1,0:T(8,128)(2,1)}, u32[]{:S(2)}) copy-start(bf16[4,512,128]{2,1,0:T(8,128)(2,1)} %param.9) | copy-start | bytes 1572868
  2.7 0.7 collective-permute-start
  4.3 0.7 collective-permute-start.1
  5.0 0.7 collective-permute-start.2
  5.7 13.5 %collective-permute-start.3 = (bf16[4,128,128]{2,1,0:T(8,128)(2,1)S(1)}, bf16[4,128,128]{2,1,0:T(8,128)(2,1)S(1)}, u32[]{:S(2)}, u32[]{:S(2)}) collective-permute-start(bf16[4,128,128]{2,1,0:T(8,128)(2,1)S(1)} %broadcast_select_fusion.11), channel_id=1, source_target_pairs={{0,12},{1,13},{2,14},{3,15},{4,8},{5,9},{6,10},{7,11},{16,28},{17,... | collective-permute-start | bytes 393224 | tf_op jit(solution)/shard_map/ppermute | solution.py:284
  19.3 15.5 %collective-permute-start.6 = (bf16[4,128,128]{2,1,0:T(8,128)(2,1)S(1)}, bf16[4,128,128]{2,1,0:T(8,128)(2,1)S(1)}, u32[]{:S(2)}, u32[]{:S(2)}) collective-permute-start(bf16[4,128,128]{2,1,0:T(8,128)(2,1)S(1)} %broadcast_select_fusion.15.refs_0_.refs_8_), channel_id=1, source_target_pairs={{0,96},{16,112},{32,64},{48,80},{64,32},{80,48},{96,0},{112,16},{1... | collective-permute-start | bytes 393224 | tf_op jit(solution)/shard_map/ppermute | solution.py:259
  23.1 24.1 %collective-permute-start.11 = (f32[4,128,128]{2,1,0:T(8,128)}, f32[4,128,128]{2,1,0:T(8,128)S(1)}, u32[]{:S(2)}, u32[]{:S(2)}) collective-permute-start(f32[4,128,128]{2,1,0:T(8,128)} %bitcast.12), channel_id=1, source_target_pairs={{1,0},{2,1},{3,2},{4,3},{5,4},{6,5},{7,6},{8,7},{9,8},{10,9},{11,1... | collective-permute-start | bytes 786440 | tf_op jit(solution)/shard_map/ppermute | solution.py:294
  29.1 5.7 %collective-permute-start.5 = (bf16[4,128,128]{2,1,0:T(8,128)(2,1)S(1)}, bf16[4,128,128]{2,1,0:T(8,128)(2,1)S(1)}, u32[]{:S(2)}, u32[]{:S(2)}) collective-permute-start(bf16[4,128,128]{2,1,0:T(8,128)(2,1)S(1)} %broadcast_select_fusion.15.refs_0_.refs_8_), channel_id=1, source_target_pairs={{0,64},{16,80},{32,96},{48,112},{64,0},{80,16},{96,32},{112,48},{1... | collective-permute-start | bytes 393224 | tf_op jit(solution)/shard_map/ppermute | solution.py:259
  29.2 11.2 %collective-permute-start.4 = (bf16[4,128,128]{2,1,0:T(8,128)(2,1)S(1)}, bf16[4,128,128]{2,1,0:T(8,128)(2,1)S(1)}, u32[]{:S(2)}, u32[]{:S(2)}) collective-permute-start(bf16[4,128,128]{2,1,0:T(8,128)(2,1)S(1)} %broadcast_select_fusion.15.refs_0_.refs_8_), channel_id=1, source_target_pairs={{0,32},{16,48},{32,0},{48,16},{64,96},{80,112},{96,64},{112,80},{1... | collective-permute-start | bytes 393224 | tf_op jit(solution)/shard_map/ppermute | solution.py:259
  29.8 17.5 %collective-permute-start.7 = (bf16[4,128,128]{2,1,0:T(8,128)(2,1)S(1)}, bf16[4,128,128]{2,1,0:T(8,128)(2,1)S(1)}, u32[]{:S(2)}, u32[]{:S(2)}) collective-permute-start(bf16[4,128,128]{2,1,0:T(8,128)(2,1)S(1)} %broadcast_select_fusion.15.refs_0_.refs_8_), channel_id=1, source_target_pairs={{0,16},{16,0},{32,48},{48,32},{64,80},{80,64},{96,112},{112,96},{1... | collective-permute-start | bytes 393224 | tf_op jit(solution)/shard_map/ppermute | solution.py:259
  34.8 12.5 %collective-permute-start.10 = (bf16[4,128,128]{2,1,0:T(8,128)(2,1)S(1)}, bf16[4,128,128]{2,1,0:T(8,128)(2,1)S(1)}, u32[]{:S(2)}, u32[]{:S(2)}) collective-permute-start(bf16[4,128,128]{2,1,0:T(8,128)(2,1)S(1)} %collective-permute-done.6.refs_3_), channel_id=1, source_target_pairs={{0,16},{16,0},{32,48},{48,32},{64,80},{80,64},{96,112},{112,96},{1... | collective-permute-start | bytes 393224 | tf_op jit(solution)/shard_map/ppermute | solution.py:259
  34.8 12.5 %collective-permute-start.9 = (bf16[4,128,128]{2,1,0:T(8,128)(2,1)S(1)}, bf16[4,128,128]{2,1,0:T(8,128)(2,1)S(1)}, u32[]{:S(2)}, u32[]{:S(2)}) collective-permute-start(bf16[4,128,128]{2,1,0:T(8,128)(2,1)S(1)} %collective-permute-done.5.refs_2_), channel_id=1, source_target_pairs={{0,16},{16,0},{32,48},{48,32},{64,80},{80,64},{96,112},{112,96},{1... | collective-permute-start | bytes 393224 | tf_op jit(solution)/shard_map/ppermute | solution.py:259
  40.3 6.9 %collective-permute-start.8 = (bf16[4,128,128]{2,1,0:T(8,128)(2,1)S(1)}, bf16[4,128,128]{2,1,0:T(8,128)(2,1)S(1)}, u32[]{:S(2)}, u32[]{:S(2)}) collective-permute-start(bf16[4,128,128]{2,1,0:T(8,128)(2,1)S(1)} %collective-permute-done.4.refs_1_), channel_id=1, source_target_pairs={{0,16},{16,0},{32,48},{48,32},{64,80},{80,64},{96,112},{112,96},{1... | collective-permute-start | bytes 393224 | tf_op jit(solution)/shard_map/ppermute | solution.py:259
  42.5 1.0 copy-start.1
  43.5 0.7 copy-start.2
  47.9 0.7 collective-permute-start.12
  48.7 0.7 collective-permute-start.13
  49.4 0.7 collective-permute-start.14
  50.1 8.4 %collective-permute-start.15 = (bf16[4,128,128]{2,1,0:T(8,128)(2,1)S(1)}, bf16[4,128,128]{2,1,0:T(8,128)(2,1)S(1)}, u32[]{:S(2)}, u32[]{:S(2)}) collective-permute-start(bf16[4,128,128]{2,1,0:T(8,128)(2,1)S(1)} %broadcast_select_fusion.10), channel_id=1, source_target_pairs={{0,12},{1,13},{2,14},{3,15},{4,8},{5,9},{6,10},{7,11},{16,28},{17,... | collective-permute-start | bytes 393224 | tf_op jit(solution)/shard_map/ppermute | solution.py:284
  58.5 14.5 %collective-permute-start.18 = (bf16[4,128,128]{2,1,0:T(8,128)(2,1)S(1)}, bf16[4,128,128]{2,1,0:T(8,128)(2,1)S(1)}, u32[]{:S(2)}, u32[]{:S(2)}) collective-permute-start(bf16[4,128,128]{2,1,0:T(8,128)(2,1)S(1)} %broadcast_select_fusion.14.refs_0_.refs_9_), channel_id=1, source_target_pairs={{0,96},{16,112},{32,64},{48,80},{64,32},{80,48},{96,0},{112,16},{1... | collective-permute-start | bytes 393224 | tf_op jit(solution)/shard_map/ppermute | solution.py:259
  61.0 16.6 %collective-permute-start.23 = (f32[4,128,128]{2,1,0:T(8,128)S(1)}, f32[4,128,128]{2,1,0:T(8,128)S(1)}, u32[]{:S(2)}, u32[]{:S(2)}) collective-permute-start(f32[4,128,128]{2,1,0:T(8,128)S(1)} %shard_map.107), channel_id=1, source_target_pairs={{1,0},{2,1},{3,2},{4,3},{5,4},{6,5},{7,6},{8,7},{9,8},{10,9},{11,1... | collective-permute-start | bytes 786440 | tf_op jit(solution)/shard_map/ppermute | solution.py:294
  67.3 5.6 %collective-permute-start.17 = (bf16[4,128,128]{2,1,0:T(8,128)(2,1)S(1)}, bf16[4,128,128]{2,1,0:T(8,128)(2,1)S(1)}, u32[]{:S(2)}, u32[]{:S(2)}) collective-permute-start(bf16[4,128,128]{2,1,0:T(8,128)(2,1)S(1)} %broadcast_select_fusion.14.refs_0_.refs_9_), channel_id=1, source_target_pairs={{0,64},{16,80},{32,96},{48,112},{64,0},{80,16},{96,32},{112,48},{1... | collective-permute-start | bytes 393224 | tf_op jit(solution)/shard_map/ppermute | solution.py:259
  67.5 10.1 %collective-permute-start.16 = (bf16[4,128,128]{2,1,0:T(8,128)(2,1)S(1)}, bf16[4,128,128]{2,1,0:T(8,128)(2,1)S(1)}, u32[]{:S(2)}, u32[]{:S(2)}) collective-permute-start(bf16[4,128,128]{2,1,0:T(8,128)(2,1)S(1)} %broadcast_select_fusion.14.refs_0_.refs_9_), channel_id=1, source_target_pairs={{0,32},{16,48},{32,0},{48,16},{64,96},{80,112},{96,64},{112,80},{1... | collective-permute-start | bytes 393224 | tf_op jit(solution)/shard_map/ppermute | solution.py:259
  68.0 9.6 %collective-permute-start.19 = (bf16[4,128,128]{2,1,0:T(8,128)(2,1)S(1)}, bf16[4,128,128]{2,1,0:T(8,128)(2,1)S(1)}, u32[]{:S(2)}, u32[]{:S(2)}) collective-permute-start(bf16[4,128,128]{2,1,0:T(8,128)(2,1)S(1)} %broadcast_select_fusion.14.refs_0_.refs_9_), channel_id=1, source_target_pairs={{0,16},{16,0},{32,48},{48,32},{64,80},{80,64},{96,112},{112,96},{1... | collective-permute-start | bytes 393224 | tf_op jit(solution)/shard_map/ppermute | solution.py:259
  72.9 4.7 %collective-permute-start.22 = (bf16[4,128,128]{2,1,0:T(8,128)(2,1)S(1)}, bf16[4,128,128]{2,1,0:T(8,128)(2,1)S(1)}, u32[]{:S(2)}, u32[]{:S(2)}) collective-permute-start(bf16[4,128,128]{2,1,0:T(8,128)(2,1)S(1)} %collective-permute-done.18.refs_3_), channel_id=1, source_target_pairs={{0,16},{16,0},{32,48},{48,32},{64,80},{80,64},{96,112},{112,96},{1... | collective-permute-start | bytes 393224 | tf_op jit(solution)/shard_map/ppermute | solution.py:259
  72.9 5.7 %collective-permute-start.21 = (bf16[4,128,128]{2,1,0:T(8,128)(2,1)S(1)}, bf16[4,128,128]{2,1,0:T(8,128)(2,1)S(1)}, u32[]{:S(2)}, u32[]{:S(2)}) collective-permute-start(bf16[4,128,128]{2,1,0:T(8,128)(2,1)S(1)} %collective-permute-done.17.refs_2_), channel_id=1, source_target_pairs={{0,16},{16,0},{32,48},{48,32},{64,80},{80,64},{96,112},{112,96},{1... | collective-permute-start | bytes 393224 | tf_op jit(solution)/shard_map/ppermute | solution.py:259
  77.6 1.3 collective-permute-start.20
  79.6 0.7 collective-permute-start.24
  80.4 0.7 collective-permute-start.25
  81.1 0.7 collective-permute-start.26
  81.8 9.6 %collective-permute-start.27 = (bf16[4,128,128]{2,1,0:T(8,128)(2,1)S(1)}, bf16[4,128,128]{2,1,0:T(8,128)(2,1)S(1)}, u32[]{:S(2)}, u32[]{:S(2)}) collective-permute-start(bf16[4,128,128]{2,1,0:T(8,128)(2,1)S(1)} %broadcast_select_fusion.9), channel_id=1, source_target_pairs={{0,12},{1,13},{2,14},{3,15},{4,8},{5,9},{6,10},{7,11},{16,28},{17,... | collective-permute-start | bytes 393224 | tf_op jit(solution)/shard_map/ppermute | solution.py:284
  91.4 14.3 %collective-permute-start.30 = (bf16[4,128,128]{2,1,0:T(8,128)(2,1)S(1)}, bf16[4,128,128]{2,1,0:T(8,128)(2,1)S(1)}, u32[]{:S(2)}, u32[]{:S(2)}) collective-permute-start(bf16[4,128,128]{2,1,0:T(8,128)(2,1)S(1)} %broadcast_select_fusion.13.refs_0_.refs_10_), channel_id=1, source_target_pairs={{0,96},{16,112},{32,64},{48,80},{64,32},{80,48},{96,0},{112,16},{1... | collective-permute-start | bytes 393224 | tf_op jit(solution)/shard_map/ppermute | solution.py:259
  92.6 17.5 %collective-permute-start.35 = (f32[4,128,128]{2,1,0:T(8,128)S(1)}, f32[4,128,128]{2,1,0:T(8,128)S(1)}, u32[]{:S(2)}, u32[]{:S(2)}) collective-permute-start(f32[4,128,128]{2,1,0:T(8,128)S(1)} %shard_map.109), channel_id=1, source_target_pairs={{1,0},{2,1},{3,2},{4,3},{5,4},{6,5},{7,6},{8,7},{9,8},{10,9},{11,1... | collective-permute-start | bytes 786440 | tf_op jit(solution)/shard_map/ppermute | solution.py:294
  98.9 6.9 %collective-permute-start.29 = (bf16[4,128,128]{2,1,0:T(8,128)(2,1)S(1)}, bf16[4,128,128]{2,1,0:T(8,128)(2,1)S(1)}, u32[]{:S(2)}, u32[]{:S(2)}) collective-permute-start(bf16[4,128,128]{2,1,0:T(8,128)(2,1)S(1)} %broadcast_select_fusion.13.refs_0_.refs_10_), channel_id=1, source_target_pairs={{0,64},{16,80},{32,96},{48,112},{64,0},{80,16},{96,32},{112,48},{1... | collective-permute-start | bytes 393224 | tf_op jit(solution)/shard_map/ppermute | solution.py:259
  99.5 10.0 %collective-permute-start.28 = (bf16[4,128,128]{2,1,0:T(8,128)(2,1)S(1)}, bf16[4,128,128]{2,1,0:T(8,128)(2,1)S(1)}, u32[]{:S(2)}, u32[]{:S(2)}) collective-permute-start(bf16[4,128,128]{2,1,0:T(8,128)(2,1)S(1)} %broadcast_select_fusion.13.refs_0_.refs_10_), channel_id=1, source_target_pairs={{0,32},{16,48},{32,0},{48,16},{64,96},{80,112},{96,64},{112,80},{1... | collective-permute-start | bytes 393224 | tf_op jit(solution)/shard_map/ppermute | solution.py:259
  101.3 8.8 %collective-permute-start.31 = (bf16[4,128,128]{2,1,0:T(8,128)(2,1)S(1)}, bf16[4,128,128]{2,1,0:T(8,128)(2,1)S(1)}, u32[]{:S(2)}, u32[]{:S(2)}) collective-permute-start(bf16[4,128,128]{2,1,0:T(8,128)(2,1)S(1)} %broadcast_select_fusion.13.refs_0_.refs_10_), channel_id=1, source_target_pairs={{0,16},{16,0},{32,48},{48,32},{64,80},{80,64},{96,112},{112,96},{1... | collective-permute-start | bytes 393224 | tf_op jit(solution)/shard_map/ppermute | solution.py:259
  105.7 4.4 %collective-permute-start.34 = (bf16[4,128,128]{2,1,0:T(8,128)(2,1)S(1)}, bf16[4,128,128]{2,1,0:T(8,128)(2,1)S(1)}, u32[]{:S(2)}, u32[]{:S(2)}) collective-permute-start(bf16[4,128,128]{2,1,0:T(8,128)(2,1)S(1)} %collective-permute-done.30.refs_3_), channel_id=1, source_target_pairs={{0,16},{16,0},{32,48},{48,32},{64,80},{80,64},{96,112},{112,96},{1... | collective-permute-start | bytes 393224 | tf_op jit(solution)/shard_map/ppermute | solution.py:259
  105.8 4.8 %collective-permute-start.33 = (bf16[4,128,128]{2,1,0:T(8,128)(2,1)S(1)}, bf16[4,128,128]{2,1,0:T(8,128)(2,1)S(1)}, u32[]{:S(2)}, u32[]{:S(2)}) collective-permute-start(bf16[4,128,128]{2,1,0:T(8,128)(2,1)S(1)} %collective-permute-done.29.refs_2_), channel_id=1, source_target_pairs={{0,16},{16,0},{32,48},{48,32},{64,80},{80,64},{96,112},{112,96},{1... | collective-permute-start | bytes 393224 | tf_op jit(solution)/shard_map/ppermute | solution.py:259
  109.5 1.5 %collective-permute-start.32 = (bf16[4,128,128]{2,1,0:T(8,128)(2,1)S(1)}, bf16[4,128,128]{2,1,0:T(8,128)(2,1)S(1)}, u32[]{:S(2)}, u32[]{:S(2)}) collective-permute-start(bf16[4,128,128]{2,1,0:T(8,128)(2,1)S(1)} %collective-permute-done.28.refs_1_), channel_id=1, source_target_pairs={{0,16},{16,0},{32,48},{48,32},{64,80},{80,64},{96,112},{112,96},{1... | collective-permute-start | bytes 393224 | tf_op jit(solution)/shard_map/ppermute | solution.py:259
  111.7 0.7 collective-permute-start.36
  112.4 0.7 collective-permute-start.37
  113.2 0.7 collective-permute-start.38
  113.9 9.4 %collective-permute-start.39 = (bf16[4,128,128]{2,1,0:T(8,128)(2,1)S(1)}, bf16[4,128,128]{2,1,0:T(8,128)(2,1)S(1)}, u32[]{:S(2)}, u32[]{:S(2)}) collective-permute-start(bf16[4,128,128]{2,1,0:T(8,128)(2,1)S(1)} %broadcast_select_fusion.8), channel_id=1, source_target_pairs={{0,12},{1,13},{2,14},{3,15},{4,8},{5,9},{6,10},{7,11},{16,28},{17,... | collective-permute-start | bytes 393224 | tf_op jit(solution)/shard_map/ppermute | solution.py:284
  123.2 14.3 %collective-permute-start.42 = (bf16[4,128,128]{2,1,0:T(8,128)(2,1)S(1)}, bf16[4,128,128]{2,1,0:T(8,128)(2,1)S(1)}, u32[]{:S(2)}, u32[]{:S(2)}) collective-permute-start(bf16[4,128,128]{2,1,0:T(8,128)(2,1)S(1)} %broadcast_select_fusion.12.refs_0_.refs_11_), channel_id=1, source_target_pairs={{0,96},{16,112},{32,64},{48,80},{64,32},{80,48},{96,0},{112,16},{1... | collective-permute-start | bytes 393224 | tf_op jit(solution)/shard_map/ppermute | solution.py:259
  124.6 17.4 %collective-permute-start.47 = (f32[4,128,128]{2,1,0:T(8,128)S(1)}, f32[4,128,128]{2,1,0:T(8,128)S(1)}, u32[]{:S(2)}, u32[]{:S(2)}) collective-permute-start(f32[4,128,128]{2,1,0:T(8,128)S(1)} %shard_map.111), channel_id=1, source_target_pairs={{1,0},{2,1},{3,2},{4,3},{5,4},{6,5},{7,6},{8,7},{9,8},{10,9},{11,1... | collective-permute-start | bytes 786440 | tf_op jit(solution)/shard_map/ppermute | solution.py:294
  130.8 6.7 %collective-permute-start.41 = (bf16[4,128,128]{2,1,0:T(8,128)(2,1)S(1)}, bf16[4,128,128]{2,1,0:T(8,128)(2,1)S(1)}, u32[]{:S(2)}, u32[]{:S(2)}) collective-permute-start(bf16[4,128,128]{2,1,0:T(8,128)(2,1)S(1)} %broadcast_select_fusion.12.refs_0_.refs_11_), channel_id=1, source_target_pairs={{0,64},{16,80},{32,96},{48,112},{64,0},{80,16},{96,32},{112,48},{1... | collective-permute-start | bytes 393224 | tf_op jit(solution)/shard_map/ppermute | solution.py:259
  131.4 10.1 %collective-permute-start.40 = (bf16[4,128,128]{2,1,0:T(8,128)(2,1)S(1)}, bf16[4,128,128]{2,1,0:T(8,128)(2,1)S(1)}, u32[]{:S(2)}, u32[]{:S(2)}) collective-permute-start(bf16[4,128,128]{2,1,0:T(8,128)(2,1)S(1)} %broadcast_select_fusion.12.refs_0_.refs_11_), channel_id=1, source_target_pairs={{0,32},{16,48},{32,0},{48,16},{64,96},{80,112},{96,64},{112,80},{1... | collective-permute-start | bytes 393224 | tf_op jit(solution)/shard_map/ppermute | solution.py:259
  133.0 8.9 %collective-permute-start.43 = (bf16[4,128,128]{2,1,0:T(8,128)(2,1)S(1)}, bf16[4,128,128]{2,1,0:T(8,128)(2,1)S(1)}, u32[]{:S(2)}, u32[]{:S(2)}) collective-permute-start(bf16[4,128,128]{2,1,0:T(8,128)(2,1)S(1)} %broadcast_select_fusion.12.refs_0_.refs_11_), channel_id=1, source_target_pairs={{0,16},{16,0},{32,48},{48,32},{64,80},{80,64},{96,112},{112,96},{1... | collective-permute-start | bytes 393224 | tf_op jit(solution)/shard_map/ppermute | solution.py:259
  137.6 4.4 %collective-permute-start.46 = (bf16[4,128,128]{2,1,0:T(8,128)(2,1)S(1)}, bf16[4,128,128]{2,1,0:T(8,128)(2,1)S(1)}, u32[]{:S(2)}, u32[]{:S(2)}) collective-permute-start(bf16[4,128,128]{2,1,0:T(8,128)(2,1)S(1)} %collective-permute-done.42.refs_3_), channel_id=1, source_target_pairs={{0,16},{16,0},{32,48},{48,32},{64,80},{80,64},{96,112},{112,96},{1... | collective-permute-start | bytes 393224 | tf_op jit(solution)/shard_map/ppermute | solution.py:259
  137.6 4.9 %collective-permute-start.45 = (bf16[4,128,128]{2,1,0:T(8,128)(2,1)S(1)}, bf16[4,128,128]{2,1,0:T(8,128)(2,1)S(1)}, u32[]{:S(2)}, u32[]{:S(2)}) collective-permute-start(bf16[4,128,128]{2,1,0:T(8,128)(2,1)S(1)} %collective-permute-done.41.refs_2_), channel_id=1, source_target_pairs={{0,16},{16,0},{32,48},{48,32},{64,80},{80,64},{96,112},{112,96},{1... | collective-permute-start | bytes 393224 | tf_op jit(solution)/shard_map/ppermute | solution.py:259
  141.5 1.4 collective-permute-start.44

commit v4 on v3

--- a/solution.py
+++ b/solution.py
@@ -17,18 +17,12 @@
 PIECES = 8
 
 
-def accumulate(meta, blocks, pieces, base, gathered, sums, arrivals):
+def accumulate(meta, blocks, pieces, base, gathered, sums):
     rows = base.shape[0]
-    copies = [
-        pltpu.make_async_copy(piece, gathered.at[pl.ds(place * rows, rows)], arrivals.at[place])
-        for place, piece in enumerate(pieces)
-    ]
-    for copy in copies:
-        copy.start()
+    for place, piece in enumerate(pieces):
+        gathered[pl.ds(place * rows, rows)] = piece[...]
     gathered[ZERO_COLUMN] = jnp.zeros(gathered.shape[1:], gathered.dtype)
     sums[...] = base[...]
-    for copy in copies:
-        copy.wait()
 
     def several(at, carry):
         for offset in range(UNROLL):
@@ -58,7 +52,7 @@
         ).astype(solved.dtype)
 
 
-def words_kernel(place_of, tables, *refs):
+def words_kernel(tables, *refs):
     kept, held_refs, (words, tally, arrivals) = refs[:3], refs[4:7], (refs[3],) + refs[7:]
     moves = [
         pltpu.make_async_copy(source, target, arrivals.at[at])
@@ -66,7 +60,7 @@
     ]
     for copy in moves:
         copy.start()
-    slots = (tables.shape[0] - 2 * PIECES - 1) // 3
+    slots = (tables.shape[0] - 2 * PIECES - 2) // 3
     live = tables[3 * slots + 2 * PIECES]
     rows = tally.shape[0]
     for b in range(rows):
@@ -101,7 +95,7 @@
         place = tally[row]
         tally[row] = place + 1
         owner = tables[slots + slot]
-        apart = owner ^ place_of[1]
+        apart = owner ^ tables[tables.shape[0] - 1]
         piece = (apart & 1) * (PIECES // 2) + (apart >> 1)
         local = tables[3 * slots + tables[2 * slots + slot] * PIECES + owner]
         words[place] = slot * 64 + piece * rows + local
@@ -112,8 +106,8 @@
         copy.wait()
 
 
-def first_kernel(place_of, excitation, base, inverse, solved, right, field, factors, arrivals):
-    @pl.when(place_of[0] == 0)
+def first_kernel(lag, excitation, base, inverse, solved, right, field, factors, arrivals):
+    @pl.when(lag[0] == 0)
     def _():
         copies = [
             pltpu.make_async_copy(excitation.at[0], right, arrivals.at[0]),
@@ -126,44 +120,44 @@
             copy.wait()
         solve(factors, right, field, solved)
 
-    @pl.when(place_of[0] != 0)
+    @pl.when(lag[0] != 0)
     def _():
         solved[...] = jnp.zeros(solved.shape, solved.dtype)
 
 
-def chain_kernel(t, place_of, meta, blocks, *refs):
-    pieces, (base, excitation, inverse, solved, gathered, sums, arrivals) = refs[:PIECES], refs[PIECES:]
-
-    @pl.when(place_of[0] == 0)
-    def _():
-        accumulate(meta, blocks, pieces, base, gathered, sums, arrivals)
+def chain_kernel(t, lag, meta, blocks, *refs):
+    pieces, (base, excitation, inverse, solved, gathered, sums) = refs[:PIECES], refs[PIECES:]
+
+    @pl.when(lag[0] == 0)
+    def _():
+        accumulate(meta, blocks, pieces, base, gathered, sums)
         solve(inverse, excitation.at[t], sums, solved)
 
-    @pl.when(place_of[0] != 0)
+    @pl.when(lag[0] != 0)
     def _():
         solved[...] = jnp.zeros(solved.shape, solved.dtype)
 
 
-def others_kernel(place_of, meta, blocks, *refs):
-    pieces, (base, total, gathered, arrivals) = refs[:PIECES], refs[PIECES:]
-
-    @pl.when(place_of[0] != 0)
-    def _():
-        accumulate(meta, blocks, pieces, base, gathered, total, arrivals)
-
-    @pl.when(place_of[0] == 0)
+def others_kernel(lag, meta, blocks, *refs):
+    pieces, (base, total, gathered) = refs[:PIECES], refs[PIECES:]
+
+    @pl.when(lag[0] != 0)
+    def _():
+        accumulate(meta, blocks, pieces, base, gathered, total)
+
+    @pl.when(lag[0] == 0)
     def _():
         total[...] = jnp.zeros(total.shape, total.dtype)
 
 
 def last_kernel(meta, blocks, *refs):
-    pieces, solved, (base, total, kept, gathered, arrivals, placed) = refs[:PIECES], refs[PIECES:-6], refs[-6:]
+    pieces, solved, (base, total, kept, gathered, placed) = refs[:PIECES], refs[PIECES:-5], refs[-5:]
     copies = [
         pltpu.make_async_copy(each, kept.at[t], placed.at[t]) for t, each in enumerate(solved)
     ]
     for copy in copies:
         copy.start()
-    accumulate(meta, blocks, pieces, base, gathered, total, arrivals)
+    accumulate(meta, blocks, pieces, base, gathered, total)
     for copy in copies:
         copy.wait()
 
@@ -180,29 +174,26 @@
 
 
 def gathering(base):
-    return [
-        pltpu.VMEM((ZERO_COLUMN + 1,) + base.shape[1:], jnp.bfloat16),
-        pltpu.SemaphoreType.DMA((PIECES,)),
-    ]
-
-
-def prepare(place_of, tables, kept, row_blocks):
+    return pltpu.VMEM((ZERO_COLUMN + 1,) + base.shape[1:], jnp.bfloat16)
+
+
+def prepare(tables, kept, row_blocks):
     shapes = [jax.ShapeDtypeStruct(each.shape, each.dtype) for each in kept]
     words, *held_arrays = pl.pallas_call(
         words_kernel,
         out_shape=[jax.ShapeDtypeStruct((COUNT_WORD + 1,), jnp.int32)] + shapes,
-        in_specs=[SMEM, SMEM] + [HBM] * len(kept),
+        in_specs=[SMEM] + [HBM] * len(kept),
         compiler_params=pltpu.CompilerParams(vmem_limit_bytes=48 * 1024 * 1024),
         out_specs=[SMEM] + [VMEM] * len(kept),
         scratch_shapes=[
             pltpu.SMEM((row_blocks,), jnp.int32),
             pltpu.SemaphoreType.DMA((len(kept),)),
         ],
-    )(place_of, tables, *kept)
+    )(tables, *kept)
     return words, held(held_arrays)
 
 
-def first_solve(place_of, excitation, base, inverse):
+def first_solve(lag, excitation, base, inverse):
     return pl.pallas_call(
         first_kernel,
         out_shape=jax.ShapeDtypeStruct(base.shape, jnp.bfloat16),
@@ -214,30 +205,29 @@
             pltpu.VMEM(inverse.shape, jnp.float32),
             pltpu.SemaphoreType.DMA((3,)),
         ],
-    )(place_of, excitation, base, inverse)
-
-
-def chain_step(t, place_of, meta, blocks, pieces, base, excitation, inverse):
-    gathered, arrivals = gathering(base)
+    )(lag, excitation, base, inverse)
+
+
+def chain_step(t, lag, meta, blocks, pieces, base, excitation, inverse):
     return pl.pallas_call(
         functools.partial(chain_kernel, t),
         out_shape=jax.ShapeDtypeStruct(base.shape, jnp.bfloat16),
         in_specs=[SMEM, SMEM, VMEM] + [VMEM] * PIECES + [VMEM] * 3,
         compiler_params=PARAMS,
         out_specs=VMEM,
-        scratch_shapes=[gathered, pltpu.VMEM(base.shape, jnp.float32), arrivals],
-    )(place_of, meta, blocks, *held(pieces), base, excitation, inverse)
-
-
-def others_step(place_of, meta, blocks, pieces, base):
+        scratch_shapes=[gathering(base), pltpu.VMEM(base.shape, jnp.float32)],
+    )(lag, meta, blocks, *held(pieces), base, excitation, inverse)
+
+
+def others_step(lag, meta, blocks, pieces, base):
     return pl.pallas_call(
         others_kernel,
         out_shape=jax.ShapeDtypeStruct(base.shape, jnp.float32),
         in_specs=[SMEM, SMEM, VMEM] + [VMEM] * PIECES + [VMEM],
         compiler_params=PARAMS,
         out_specs=VMEM,
-        scratch_shapes=gathering(base),
-    )(place_of, meta, blocks, *held(pieces), base)
+        scratch_shapes=[gathering(base)],
+    )(lag, meta, blocks, *held(pieces), base)
 
 
 def last_step(meta, blocks, pieces, solved, base):
@@ -250,7 +240,7 @@
         in_specs=[SMEM, VMEM] + [VMEM] * PIECES + [ANY] * len(solved) + [VMEM],
         compiler_params=PARAMS,
         out_specs=(VMEM, ANY),
-        scratch_shapes=gathering(base) + [pltpu.SemaphoreType.DMA((len(solved),))],
+        scratch_shapes=[gathering(base), pltpu.SemaphoreType.DMA((len(solved),))],
     )(meta, blocks, *held(pieces), *solved, base)
 
 
@@ -300,25 +290,26 @@
     row_blocks, block_size, _ = inverse.shape
     steps, rows, width = excitation.shape
     excitation_blocks = excitation.reshape(steps, row_blocks, block_size, width)
-    place_of = jnp.stack([lax.axis_index("lag"), lax.axis_index("rows")]).astype(jnp.int32)
+    lag = jnp.full((1,), lax.axis_index("lag"), jnp.int32)
+    row_owner = jnp.full((1,), lax.axis_index("rows"), jnp.int32)
     total = pending[0].reshape(row_blocks, block_size, width)
-    solved = first_solve(place_of, excitation_blocks, total, inverse)
-    tables = (slot_row, slot_owner, slot_pos, needed.transpose(0, 2, 1), block_count)
+    solved = first_solve(lag, excitation_blocks, total, inverse)
+    tables = (slot_row, slot_owner, slot_pos, needed.transpose(0, 2, 1), block_count, row_owner)
     tables = jnp.concatenate([table.reshape(-1) for table in tables])
     meta, (blocks, excitation_held, inverse_held) = prepare(
-        place_of, tables, (interaction, excitation_blocks, inverse), row_blocks
+        tables, (interaction, excitation_blocks, inverse), row_blocks
     )
     outputs = []
     for t in range(steps):
         solved = spread(solved)
         outputs.append(solved)
         if t > 0:
-            total = others_step(place_of, meta, blocks, pieces, base)
+            total = others_step(lag, meta, blocks, pieces, base)
         base = from_behind(total)
         pieces = exchange(solved)
         if t + 1 < steps:
             solved = chain_step(
-                t + 1, place_of, meta, blocks, pieces, base, excitation_held, inverse_held
+                t + 1, lag, meta, blocks, pieces, base, excitation_held, inverse_held
             )
         else:
             total, kept = last_step(meta, blocks, pieces, outputs, base)

time: 147 us -> 143 us (0.973)
  Pallas kernels: 17.3 us -> 11.2 us
  waiting for transfers between devices: 31.3 us -> 34.7 us
    pallas_call x3, Pallas kernels: 7.67 us -> 3.55 us  [others_step(): pl.pallas_call(others_kernel, out_shape=jax.ShapeDtypeStruct(base.shape,...]
    ppermute x16, waiting for transfers between devices: 27.9 us -> 31.2 us  [spread(): arrived = lax.ppermute(value, 'lag', pairs)]
  transfers between devices with their start and end apart: 48 -> 48, of which waited for: 10 -> 10; matrix products, arithmetic and copies ran while one was open for 1% -> 1% of each run, Pallas kernels for 7% -> 5%
where the time goes in v4:
time: 143 us; the launch traced here: 142 us
  starting transfers between devices  90.7 us (63%)
  waiting for transfers between devices  34.7 us (24%)
  Pallas kernels  11.2 us (8%)
  local copies, waits for them, and re-layouts  2.48 us (2%)
  between operations  2.03 us (1%)
    ppermute x28, starting transfers between devices, over_rows(): return lax.ppermute(value, 'rows', [(r, r ^ flip) for r in range(count)])  52.6 us
    ppermute x16, waiting for transfers between devices, spread(): arrived = lax.ppermute(value, 'lag', pairs)  31.2 us
    ppermute x4, starting transfers between devices, from_behind(): return lax.ppermute(value, 'lag', [(g + 1, g) for g in range(count - 1)])  24.9 us
    ppermute x16, starting transfers between devices, spread(): arrived = lax.ppermute(value, 'lag', pairs)  13.2 us
    pallas_call x3, Pallas kernels, others_step(): pl.pallas_call(others_kernel, out_shape=jax.ShapeDtypeStruct(base.shape,...  3.55 us
    ppermute x28, waiting for transfers between devices, over_rows(): return lax.ppermute(value, 'rows', [(r, r ^ flip) for r in range(count)])  3.53 us
    pallas_call x1, Pallas kernels, prepare(): pl.pallas_call(words_kernel, out_shape=[jax.ShapeDtypeStruct((COUNT_WORD...  3.08 us
  transfers between devices with their start and end apart: 48, of which 10 were waited for; matrix products, arithmetic and copies ran while one was open for 1% of the time, Pallas kernels for 5%

profile of v4, /device:TPU:25, one launch (start us, length us, event | category | flops | bytes accessed | tf_op | source)
XLA Modules:
  0.0 142.3 jit_solution(2966449007987460128)
XLA Ops:
  0.6 0.7 shard_map.105
  1.4 0.7 collective-permute-start
  2.1 0.9 broadcast_select_fusion.3
  3.0 0.7 collective-permute-start.1
  3.7 0.7 collective-permute-start.2
  4.4 1.3 collective-permute-start.3
  5.8 12.2 %collective-permute-done.3 = bf16[4,128,128]{2,1,0:T(8,128)(2,1)S(1)} collective-permute-done((bf16[4,128,128]{2,1,0:T(8,128)(2,1)S(1)}, bf16[4,128,128]{2,1,0:T(8,128)(2,1)S(1)}, u32[]{:S(2)}, u32[]{:S(2)}) %collective-permute-start.3) | collective-permute-done | bytes 131104 | tf_op jit(solution)/shard_map/ppermute | solution.py:274
  18.0 3.8 %collective-permute-start.6 = (bf16[4,128,128]{2,1,0:T(8,128)(2,1)S(1)}, bf16[4,128,128]{2,1,0:T(8,128)(2,1)S(1)}, u32[]{:S(2)}, u32[]{:S(2)}) collective-permute-start(bf16[4,128,128]{2,1,0:T(8,128)(2,1)S(1)} %broadcast_select_fusion.15.refs_0_.refs_8_), channel_id=1, source_target_pairs={{0,96},{16,112},{32,64},{48,80},{64,32},{80,48},{96,0},{112,16},{1... | collective-permute-start | bytes 393224 | tf_op jit(solution)/shard_map/ppermute | solution.py:249
  21.8 6.0 %collective-permute-start.11 = (f32[4,128,128]{2,1,0:T(8,128)}, f32[4,128,128]{2,1,0:T(8,128)S(1)}, u32[]{:S(2)}, u32[]{:S(2)}) collective-permute-start(f32[4,128,128]{2,1,0:T(8,128)} %bitcast.12), channel_id=1, source_target_pairs={{1,0},{2,1},{3,2},{4,3},{5,4},{6,5},{7,6},{8,7},{9,8},{10,9},{11,1... | collective-permute-start | bytes 786440 | tf_op jit(solution)/shard_map/ppermute | solution.py:284
  27.9 0.6 collective-permute-start.4
  28.5 5.0 %collective-permute-start.7 = (bf16[4,128,128]{2,1,0:T(8,128)(2,1)S(1)}, bf16[4,128,128]{2,1,0:T(8,128)(2,1)S(1)}, u32[]{:S(2)}, u32[]{:S(2)}) collective-permute-start(bf16[4,128,128]{2,1,0:T(8,128)(2,1)S(1)} %broadcast_select_fusion.15.refs_0_.refs_8_), channel_id=1, source_target_pairs={{0,16},{16,0},{32,48},{48,32},{64,80},{80,64},{96,112},{112,96},{1... | collective-permute-start | bytes 393224 | tf_op jit(solution)/shard_map/ppermute | solution.py:249
  33.5 5.6 %collective-permute-start.9 = (bf16[4,128,128]{2,1,0:T(8,128)(2,1)S(1)}, bf16[4,128,128]{2,1,0:T(8,128)(2,1)S(1)}, u32[]{:S(2)}, u32[]{:S(2)}) collective-permute-start(bf16[4,128,128]{2,1,0:T(8,128)(2,1)S(1)} %collective-permute-done.5.refs_2_), channel_id=1, source_target_pairs={{0,16},{16,0},{32,48},{48,32},{64,80},{80,64},{96,112},{112,96},{1... | collective-permute-start | bytes 393224 | tf_op jit(solution)/shard_map/ppermute | solution.py:249
  39.7 0.8 reshape.19
  40.5 0.8 concatenate.3.tables
  41.2 0.9 copy-done.1
  42.2 3.1 %shard_map.104 = (s32[136]{0:T(256)S(1)}, bf16[96,128,128]{2,1,0:T(8,128)(2,1)S(1)}, bf16[4,4,128,128]{3,2,1,0:T(8,128)(2,1)S(1)}, f32[4,128,128]{2,1,0:T(8,128)S(1)}) custom-call(s32[306]{0:T(512)S(1)} %concatenate.3.tables, bf16[96,128,128]{2,1,0:T(8,128)(2,1)} %refs_0_.1, bf16[4,4,128,128]{3,2,1,0:T(8,128)(2,1)S(1)} %bitcast.10, f32[4,128,128]{2,1,0:T(8,128)S(1)} %copy-done.1), custom_call_target="tpu_custom_call" | custom-call | tf_op jit(solution)/shard_map/pallas_call | solution.py:182
  45.3 0.6 shard_map.106
  45.9 0.7 collective-permute-start.12
  46.6 0.7 collective-permute-start.13
  47.3 0.7 collective-permute-start.14
  48.0 1.3 collective-permute-start.15
  49.3 1.1 shard_map.107
  50.5 5.9 %collective-permute-done.15 = bf16[4,128,128]{2,1,0:T(8,128)(2,1)S(1)} collective-permute-done((bf16[4,128,128]{2,1,0:T(8,128)(2,1)S(1)}, bf16[4,128,128]{2,1,0:T(8,128)(2,1)S(1)}, u32[]{:S(2)}, u32[]{:S(2)}) %collective-permute-start.15) | collective-permute-done | bytes 131104 | tf_op jit(solution)/shard_map/ppermute | solution.py:274
  56.4 2.6 %collective-permute-start.18 = (bf16[4,128,128]{2,1,0:T(8,128)(2,1)S(1)}, bf16[4,128,128]{2,1,0:T(8,128)(2,1)S(1)}, u32[]{:S(2)}, u32[]{:S(2)}) collective-permute-start(bf16[4,128,128]{2,1,0:T(8,128)(2,1)S(1)} %broadcast_select_fusion.14.refs_0_.refs_9_), channel_id=1, source_target_pairs={{0,96},{16,112},{32,64},{48,80},{64,32},{80,48},{96,0},{112,16},{1... | collective-permute-start | bytes 393224 | tf_op jit(solution)/shard_map/ppermute | solution.py:249
  59.0 6.3 %collective-permute-start.23 = (f32[4,128,128]{2,1,0:T(8,128)S(1)}, f32[4,128,128]{2,1,0:T(8,128)S(1)}, u32[]{:S(2)}, u32[]{:S(2)}) collective-permute-start(f32[4,128,128]{2,1,0:T(8,128)S(1)} %shard_map.107), channel_id=1, source_target_pairs={{1,0},{2,1},{3,2},{4,3},{5,4},{6,5},{7,6},{8,7},{9,8},{10,9},{11,1... | collective-permute-start | bytes 786440 | tf_op jit(solution)/shard_map/ppermute | solution.py:284
  65.3 0.2 collective-permute-start.17
  65.5 0.5 collective-permute-start.16
  66.0 4.9 %collective-permute-start.19 = (bf16[4,128,128]{2,1,0:T(8,128)(2,1)S(1)}, bf16[4,128,128]{2,1,0:T(8,128)(2,1)S(1)}, u32[]{:S(2)}, u32[]{:S(2)}) collective-permute-start(bf16[4,128,128]{2,1,0:T(8,128)(2,1)S(1)} %broadcast_select_fusion.14.refs_0_.refs_9_), channel_id=1, source_target_pairs={{0,16},{16,0},{32,48},{48,32},{64,80},{80,64},{96,112},{112,96},{1... | collective-permute-start | bytes 393224 | tf_op jit(solution)/shard_map/ppermute | solution.py:249
  70.9 4.7 %collective-permute-start.21 = (bf16[4,128,128]{2,1,0:T(8,128)(2,1)S(1)}, bf16[4,128,128]{2,1,0:T(8,128)(2,1)S(1)}, u32[]{:S(2)}, u32[]{:S(2)}) collective-permute-start(bf16[4,128,128]{2,1,0:T(8,128)(2,1)S(1)} %collective-permute-done.17.refs_2_), channel_id=1, source_target_pairs={{0,16},{16,0},{32,48},{48,32},{64,80},{80,64},{96,112},{112,96},{1... | collective-permute-start | bytes 393224 | tf_op jit(solution)/shard_map/ppermute | solution.py:249
  75.6 1.0 collective-permute-done.21.refs_6_
  76.6 0.4 collective-permute-done.20.refs_5_
  77.0 0.6 shard_map.108
  77.5 0.7 collective-permute-start.24
  78.3 0.7 collective-permute-start.25
  79.0 0.7 collective-permute-start.26
  79.7 1.3 collective-permute-start.27
  81.0 1.1 shard_map.109
  82.1 6.7 %collective-permute-done.27 = bf16[4,128,128]{2,1,0:T(8,128)(2,1)S(1)} collective-permute-done((bf16[4,128,128]{2,1,0:T(8,128)(2,1)S(1)}, bf16[4,128,128]{2,1,0:T(8,128)(2,1)S(1)}, u32[]{:S(2)}, u32[]{:S(2)}) %collective-permute-start.27) | collective-permute-done | bytes 131104 | tf_op jit(solution)/shard_map/ppermute | solution.py:274
  88.8 1.2 collective-permute-start.30
  90.0 6.3 %collective-permute-start.35 = (f32[4,128,128]{2,1,0:T(8,128)S(1)}, f32[4,128,128]{2,1,0:T(8,128)S(1)}, u32[]{:S(2)}, u32[]{:S(2)}) collective-permute-start(f32[4,128,128]{2,1,0:T(8,128)S(1)} %shard_map.109), channel_id=1, source_target_pairs={{1,0},{2,1},{3,2},{4,3},{5,4},{6,5},{7,6},{8,7},{9,8},{10,9},{11,1... | collective-permute-start | bytes 786440 | tf_op jit(solution)/shard_map/ppermute | solution.py:284
  96.3 0.4 collective-permute-start.29
  96.7 1.9 %collective-permute-start.28 = (bf16[4,128,128]{2,1,0:T(8,128)(2,1)S(1)}, bf16[4,128,128]{2,1,0:T(8,128)(2,1)S(1)}, u32[]{:S(2)}, u32[]{:S(2)}) collective-permute-start(bf16[4,128,128]{2,1,0:T(8,128)(2,1)S(1)} %broadcast_select_fusion.13.refs_0_.refs_10_), channel_id=1, source_target_pairs={{0,32},{16,48},{32,0},{48,16},{64,96},{80,112},{96,64},{112,80},{1... | collective-permute-start | bytes 393224 | tf_op jit(solution)/shard_map/ppermute | solution.py:249
  98.7 4.5 %collective-permute-start.31 = (bf16[4,128,128]{2,1,0:T(8,128)(2,1)S(1)}, bf16[4,128,128]{2,1,0:T(8,128)(2,1)S(1)}, u32[]{:S(2)}, u32[]{:S(2)}) collective-permute-start(bf16[4,128,128]{2,1,0:T(8,128)(2,1)S(1)} %broadcast_select_fusion.13.refs_0_.refs_10_), channel_id=1, source_target_pairs={{0,16},{16,0},{32,48},{48,32},{64,80},{80,64},{96,112},{112,96},{1... | collective-permute-start | bytes 393224 | tf_op jit(solution)/shard_map/ppermute | solution.py:249
  103.2 3.8 %collective-permute-start.33 = (bf16[4,128,128]{2,1,0:T(8,128)(2,1)S(1)}, bf16[4,128,128]{2,1,0:T(8,128)(2,1)S(1)}, u32[]{:S(2)}, u32[]{:S(2)}) collective-permute-start(bf16[4,128,128]{2,1,0:T(8,128)(2,1)S(1)} %collective-permute-done.29.refs_2_), channel_id=1, source_target_pairs={{0,16},{16,0},{32,48},{48,32},{64,80},{80,64},{96,112},{112,96},{1... | collective-permute-start | bytes 393224 | tf_op jit(solution)/shard_map/ppermute | solution.py:249
  107.0 0.5 collective-permute-start.32
  107.5 0.4 collective-permute-done.33.refs_6_
  107.9 0.5 collective-permute-done.32.refs_5_
  108.5 0.6 shard_map.110
  109.1 0.7 collective-permute-start.36
  109.8 0.7 collective-permute-start.37
  110.5 0.7 collective-permute-start.38
  111.2 1.3 collective-permute-start.39
  112.5 1.3 shard_map.111
  113.8 6.3 %collective-permute-done.39 = bf16[4,128,128]{2,1,0:T(8,128)(2,1)S(1)} collective-permute-done((bf16[4,128,128]{2,1,0:T(8,128)(2,1)S(1)}, bf16[4,128,128]{2,1,0:T(8,128)(2,1)S(1)}, u32[]{:S(2)}, u32[]{:S(2)}) %collective-permute-start.39) | collective-permute-done | bytes 131104 | tf_op jit(solution)/shard_map/ppermute | solution.py:274
  120.2 1.6 %collective-permute-start.42 = (bf16[4,128,128]{2,1,0:T(8,128)(2,1)S(1)}, bf16[4,128,128]{2,1,0:T(8,128)(2,1)S(1)}, u32[]{:S(2)}, u32[]{:S(2)}) collective-permute-start(bf16[4,128,128]{2,1,0:T(8,128)(2,1)S(1)} %broadcast_select_fusion.12.refs_0_.refs_11_), channel_id=1, source_target_pairs={{0,96},{16,112},{32,64},{48,80},{64,32},{80,48},{96,0},{112,16},{1... | collective-permute-start | bytes 393224 | tf_op jit(solution)/shard_map/ppermute | solution.py:249
  121.8 6.4 %collective-permute-start.47 = (f32[4,128,128]{2,1,0:T(8,128)S(1)}, f32[4,128,128]{2,1,0:T(8,128)S(1)}, u32[]{:S(2)}, u32[]{:S(2)}) collective-permute-start(f32[4,128,128]{2,1,0:T(8,128)S(1)} %shard_map.111), channel_id=1, source_target_pairs={{1,0},{2,1},{3,2},{4,3},{5,4},{6,5},{7,6},{8,7},{9,8},{10,9},{11,1... | collective-permute-start | bytes 786440 | tf_op jit(solution)/shard_map/ppermute | solution.py:284
  128.2 0.5 collective-permute-start.41
  128.7 1.1 collective-permute-start.40
  129.8 4.7 %collective-permute-start.43 = (bf16[4,128,128]{2,1,0:T(8,128)(2,1)S(1)}, bf16[4,128,128]{2,1,0:T(8,128)(2,1)S(1)}, u32[]{:S(2)}, u32[]{:S(2)}) collective-permute-start(bf16[4,128,128]{2,1,0:T(8,128)(2,1)S(1)} %broadcast_select_fusion.12.refs_0_.refs_11_), channel_id=1, source_target_pairs={{0,16},{16,0},{32,48},{48,32},{64,80},{80,64},{96,112},{112,96},{1... | collective-permute-start | bytes 393224 | tf_op jit(solution)/shard_map/ppermute | solution.py:249
  134.5 4.2 %collective-permute-start.45 = (bf16[4,128,128]{2,1,0:T(8,128)(2,1)S(1)}, bf16[4,128,128]{2,1,0:T(8,128)(2,1)S(1)}, u32[]{:S(2)}, u32[]{:S(2)}) collective-permute-start(bf16[4,128,128]{2,1,0:T(8,128)(2,1)S(1)} %collective-permute-done.41.refs_2_), channel_id=1, source_target_pairs={{0,16},{16,0},{32,48},{48,32},{64,80},{80,64},{96,112},{112,96},{1... | collective-permute-start | bytes 393224 | tf_op jit(solution)/shard_map/ppermute | solution.py:249
  138.7 0.2 collective-permute-start.44
  138.9 0.8 collective-permute-done.45.refs_6_
  139.7 0.4 collective-permute-done.44.refs_5_
  140.0 2.1 %shard_map.112 = (f32[4,128,128]{2,1,0:T(8,128)}, bf16[4,4,128,128]{3,2,1,0:T(8,128)(2,1)}) custom-call(s32[136]{0:T(256)S(1)} %get-tuple-element.8.meta, bf16[96,128,128]{2,1,0:T(8,128)(2,1)S(1)} %get-tuple-element.9.blocks, bf16[4,128,128]{2,1,0:T(8,128)(2,1)S(1)} %broadcast_select_fusion.12.refs_0_.refs_11_, ...), custom_call_target="tpu_custom_call" | custom-call | tf_op jit(solution)/shard_map/pallas_call | solution.py:234
  (63 shorter events, 0.5 us)
Async XLA Ops:
  0.6 40.6 %copy-start = (bf16[4,512,128]{2,1,0:T(8,128)(2,1)S(1)}, bf16[4,512,128]{2,1,0:T(8,128)(2,1)}, u32[]{:S(2)}) copy-start(bf16[4,512,128]{2,1,0:T(8,128)(2,1)} %param.9) | copy-start | bytes 1572868
  1.4 0.7 collective-permute-start
  3.0 0.7 collective-permute-start.1
  3.7 0.7 collective-permute-start.2
  4.4 13.5 %collective-permute-start.3 = (bf16[4,128,128]{2,1,0:T(8,128)(2,1)S(1)}, bf16[4,128,128]{2,1,0:T(8,128)(2,1)S(1)}, u32[]{:S(2)}, u32[]{:S(2)}) collective-permute-start(bf16[4,128,128]{2,1,0:T(8,128)(2,1)S(1)} %broadcast_select_fusion.11), channel_id=1, source_target_pairs={{0,12},{1,13},{2,14},{3,15},{4,8},{5,9},{6,10},{7,11},{16,28},{17,... | collective-permute-start | bytes 393224 | tf_op jit(solution)/shard_map/ppermute | solution.py:274
  18.0 15.5 %collective-permute-start.6 = (bf16[4,128,128]{2,1,0:T(8,128)(2,1)S(1)}, bf16[4,128,128]{2,1,0:T(8,128)(2,1)S(1)}, u32[]{:S(2)}, u32[]{:S(2)}) collective-permute-start(bf16[4,128,128]{2,1,0:T(8,128)(2,1)S(1)} %broadcast_select_fusion.15.refs_0_.refs_8_), channel_id=1, source_target_pairs={{0,96},{16,112},{32,64},{48,80},{64,32},{80,48},{96,0},{112,16},{1... | collective-permute-start | bytes 393224 | tf_op jit(solution)/shard_map/ppermute | solution.py:249
  21.8 23.4 %collective-permute-start.11 = (f32[4,128,128]{2,1,0:T(8,128)}, f32[4,128,128]{2,1,0:T(8,128)S(1)}, u32[]{:S(2)}, u32[]{:S(2)}) collective-permute-start(f32[4,128,128]{2,1,0:T(8,128)} %bitcast.12), channel_id=1, source_target_pairs={{1,0},{2,1},{3,2},{4,3},{5,4},{6,5},{7,6},{8,7},{9,8},{10,9},{11,1... | collective-permute-start | bytes 786440 | tf_op jit(solution)/shard_map/ppermute | solution.py:284
  27.8 5.7 %collective-permute-start.5 = (bf16[4,128,128]{2,1,0:T(8,128)(2,1)S(1)}, bf16[4,128,128]{2,1,0:T(8,128)(2,1)S(1)}, u32[]{:S(2)}, u32[]{:S(2)}) collective-permute-start(bf16[4,128,128]{2,1,0:T(8,128)(2,1)S(1)} %broadcast_select_fusion.15.refs_0_.refs_8_), channel_id=1, source_target_pairs={{0,64},{16,80},{32,96},{48,112},{64,0},{80,16},{96,32},{112,48},{1... | collective-permute-start | bytes 393224 | tf_op jit(solution)/shard_map/ppermute | solution.py:249
  27.9 11.2 %collective-permute-start.4 = (bf16[4,128,128]{2,1,0:T(8,128)(2,1)S(1)}, bf16[4,128,128]{2,1,0:T(8,128)(2,1)S(1)}, u32[]{:S(2)}, u32[]{:S(2)}) collective-permute-start(bf16[4,128,128]{2,1,0:T(8,128)(2,1)S(1)} %broadcast_select_fusion.15.refs_0_.refs_8_), channel_id=1, source_target_pairs={{0,32},{16,48},{32,0},{48,16},{64,96},{80,112},{96,64},{112,80},{1... | collective-permute-start | bytes 393224 | tf_op jit(solution)/shard_map/ppermute | solution.py:249
  28.5 16.8 %collective-permute-start.7 = (bf16[4,128,128]{2,1,0:T(8,128)(2,1)S(1)}, bf16[4,128,128]{2,1,0:T(8,128)(2,1)S(1)}, u32[]{:S(2)}, u32[]{:S(2)}) collective-permute-start(bf16[4,128,128]{2,1,0:T(8,128)(2,1)S(1)} %broadcast_select_fusion.15.refs_0_.refs_8_), channel_id=1, source_target_pairs={{0,16},{16,0},{32,48},{48,32},{64,80},{80,64},{96,112},{112,96},{1... | collective-permute-start | bytes 393224 | tf_op jit(solution)/shard_map/ppermute | solution.py:249
  33.4 11.8 %collective-permute-start.10 = (bf16[4,128,128]{2,1,0:T(8,128)(2,1)S(1)}, bf16[4,128,128]{2,1,0:T(8,128)(2,1)S(1)}, u32[]{:S(2)}, u32[]{:S(2)}) collective-permute-start(bf16[4,128,128]{2,1,0:T(8,128)(2,1)S(1)} %collective-permute-done.6.refs_3_), channel_id=1, source_target_pairs={{0,16},{16,0},{32,48},{48,32},{64,80},{80,64},{96,112},{112,96},{1... | collective-permute-start | bytes 393224 | tf_op jit(solution)/shard_map/ppermute | solution.py:249
  33.5 11.8 %collective-permute-start.9 = (bf16[4,128,128]{2,1,0:T(8,128)(2,1)S(1)}, bf16[4,128,128]{2,1,0:T(8,128)(2,1)S(1)}, u32[]{:S(2)}, u32[]{:S(2)}) collective-permute-start(bf16[4,128,128]{2,1,0:T(8,128)(2,1)S(1)} %collective-permute-done.5.refs_2_), channel_id=1, source_target_pairs={{0,16},{16,0},{32,48},{48,32},{64,80},{80,64},{96,112},{112,96},{1... | collective-permute-start | bytes 393224 | tf_op jit(solution)/shard_map/ppermute | solution.py:249
  39.0 6.3 %collective-permute-start.8 = (bf16[4,128,128]{2,1,0:T(8,128)(2,1)S(1)}, bf16[4,128,128]{2,1,0:T(8,128)(2,1)S(1)}, u32[]{:S(2)}, u32[]{:S(2)}) collective-permute-start(bf16[4,128,128]{2,1,0:T(8,128)(2,1)S(1)} %collective-permute-done.4.refs_1_), channel_id=1, source_target_pairs={{0,16},{16,0},{32,48},{48,32},{64,80},{80,64},{96,112},{112,96},{1... | collective-permute-start | bytes 393224 | tf_op jit(solution)/shard_map/ppermute | solution.py:249
  41.2 1.0 copy-start.1
  45.9 0.7 collective-permute-start.12
  46.6 0.7 collective-permute-start.13
  47.3 0.7 collective-permute-start.14
  48.0 8.4 %collective-permute-start.15 = (bf16[4,128,128]{2,1,0:T(8,128)(2,1)S(1)}, bf16[4,128,128]{2,1,0:T(8,128)(2,1)S(1)}, u32[]{:S(2)}, u32[]{:S(2)}) collective-permute-start(bf16[4,128,128]{2,1,0:T(8,128)(2,1)S(1)} %broadcast_select_fusion.10), channel_id=1, source_target_pairs={{0,12},{1,13},{2,14},{3,15},{4,8},{5,9},{6,10},{7,11},{16,28},{17,... | collective-permute-start | bytes 393224 | tf_op jit(solution)/shard_map/ppermute | solution.py:274
  56.4 14.5 %collective-permute-start.18 = (bf16[4,128,128]{2,1,0:T(8,128)(2,1)S(1)}, bf16[4,128,128]{2,1,0:T(8,128)(2,1)S(1)}, u32[]{:S(2)}, u32[]{:S(2)}) collective-permute-start(bf16[4,128,128]{2,1,0:T(8,128)(2,1)S(1)} %broadcast_select_fusion.14.refs_0_.refs_9_), channel_id=1, source_target_pairs={{0,96},{16,112},{32,64},{48,80},{64,32},{80,48},{96,0},{112,16},{1... | collective-permute-start | bytes 393224 | tf_op jit(solution)/shard_map/ppermute | solution.py:249
  59.0 16.6 %collective-permute-start.23 = (f32[4,128,128]{2,1,0:T(8,128)S(1)}, f32[4,128,128]{2,1,0:T(8,128)S(1)}, u32[]{:S(2)}, u32[]{:S(2)}) collective-permute-start(f32[4,128,128]{2,1,0:T(8,128)S(1)} %shard_map.107), channel_id=1, source_target_pairs={{1,0},{2,1},{3,2},{4,3},{5,4},{6,5},{7,6},{8,7},{9,8},{10,9},{11,1... | collective-permute-start | bytes 786440 | tf_op jit(solution)/shard_map/ppermute | solution.py:284
  65.3 5.6 %collective-permute-start.17 = (bf16[4,128,128]{2,1,0:T(8,128)(2,1)S(1)}, bf16[4,128,128]{2,1,0:T(8,128)(2,1)S(1)}, u32[]{:S(2)}, u32[]{:S(2)}) collective-permute-start(bf16[4,128,128]{2,1,0:T(8,128)(2,1)S(1)} %broadcast_select_fusion.14.refs_0_.refs_9_), channel_id=1, source_target_pairs={{0,64},{16,80},{32,96},{48,112},{64,0},{80,16},{96,32},{112,48},{1... | collective-permute-start | bytes 393224 | tf_op jit(solution)/shard_map/ppermute | solution.py:249
  65.5 10.1 %collective-permute-start.16 = (bf16[4,128,128]{2,1,0:T(8,128)(2,1)S(1)}, bf16[4,128,128]{2,1,0:T(8,128)(2,1)S(1)}, u32[]{:S(2)}, u32[]{:S(2)}) collective-permute-start(bf16[4,128,128]{2,1,0:T(8,128)(2,1)S(1)} %broadcast_select_fusion.14.refs_0_.refs_9_), channel_id=1, source_target_pairs={{0,32},{16,48},{32,0},{48,16},{64,96},{80,112},{96,64},{112,80},{1... | collective-permute-start | bytes 393224 | tf_op jit(solution)/shard_map/ppermute | solution.py:249
  66.0 9.6 %collective-permute-start.19 = (bf16[4,128,128]{2,1,0:T(8,128)(2,1)S(1)}, bf16[4,128,128]{2,1,0:T(8,128)(2,1)S(1)}, u32[]{:S(2)}, u32[]{:S(2)}) collective-permute-start(bf16[4,128,128]{2,1,0:T(8,128)(2,1)S(1)} %broadcast_select_fusion.14.refs_0_.refs_9_), channel_id=1, source_target_pairs={{0,16},{16,0},{32,48},{48,32},{64,80},{80,64},{96,112},{112,96},{1... | collective-permute-start | bytes 393224 | tf_op jit(solution)/shard_map/ppermute | solution.py:249
  70.9 4.7 %collective-permute-start.22 = (bf16[4,128,128]{2,1,0:T(8,128)(2,1)S(1)}, bf16[4,128,128]{2,1,0:T(8,128)(2,1)S(1)}, u32[]{:S(2)}, u32[]{:S(2)}) collective-permute-start(bf16[4,128,128]{2,1,0:T(8,128)(2,1)S(1)} %collective-permute-done.18.refs_3_), channel_id=1, source_target_pairs={{0,16},{16,0},{32,48},{48,32},{64,80},{80,64},{96,112},{112,96},{1... | collective-permute-start | bytes 393224 | tf_op jit(solution)/shard_map/ppermute | solution.py:249
  70.9 5.7 %collective-permute-start.21 = (bf16[4,128,128]{2,1,0:T(8,128)(2,1)S(1)}, bf16[4,128,128]{2,1,0:T(8,128)(2,1)S(1)}, u32[]{:S(2)}, u32[]{:S(2)}) collective-permute-start(bf16[4,128,128]{2,1,0:T(8,128)(2,1)S(1)} %collective-permute-done.17.refs_2_), channel_id=1, source_target_pairs={{0,16},{16,0},{32,48},{48,32},{64,80},{80,64},{96,112},{112,96},{1... | collective-permute-start | bytes 393224 | tf_op jit(solution)/shard_map/ppermute | solution.py:249
  75.6 1.3 collective-permute-start.20
  77.5 0.7 collective-permute-start.24
  78.3 0.7 collective-permute-start.25
  79.0 0.7 collective-permute-start.26
  79.7 9.1 %collective-permute-start.27 = (bf16[4,128,128]{2,1,0:T(8,128)(2,1)S(1)}, bf16[4,128,128]{2,1,0:T(8,128)(2,1)S(1)}, u32[]{:S(2)}, u32[]{:S(2)}) collective-permute-start(bf16[4,128,128]{2,1,0:T(8,128)(2,1)S(1)} %broadcast_select_fusion.9), channel_id=1, source_target_pairs={{0,12},{1,13},{2,14},{3,15},{4,8},{5,9},{6,10},{7,11},{16,28},{17,... | collective-permute-start | bytes 393224 | tf_op jit(solution)/shard_map/ppermute | solution.py:274
  88.8 14.3 %collective-permute-start.30 = (bf16[4,128,128]{2,1,0:T(8,128)(2,1)S(1)}, bf16[4,128,128]{2,1,0:T(8,128)(2,1)S(1)}, u32[]{:S(2)}, u32[]{:S(2)}) collective-permute-start(bf16[4,128,128]{2,1,0:T(8,128)(2,1)S(1)} %broadcast_select_fusion.13.refs_0_.refs_10_), channel_id=1, source_target_pairs={{0,96},{16,112},{32,64},{48,80},{64,32},{80,48},{96,0},{112,16},{1... | collective-permute-start | bytes 393224 | tf_op jit(solution)/shard_map/ppermute | solution.py:249
  90.0 17.5 %collective-permute-start.35 = (f32[4,128,128]{2,1,0:T(8,128)S(1)}, f32[4,128,128]{2,1,0:T(8,128)S(1)}, u32[]{:S(2)}, u32[]{:S(2)}) collective-permute-start(f32[4,128,128]{2,1,0:T(8,128)S(1)} %shard_map.109), channel_id=1, source_target_pairs={{1,0},{2,1},{3,2},{4,3},{5,4},{6,5},{7,6},{8,7},{9,8},{10,9},{11,1... | collective-permute-start | bytes 786440 | tf_op jit(solution)/shard_map/ppermute | solution.py:284
  96.3 6.9 %collective-permute-start.29 = (bf16[4,128,128]{2,1,0:T(8,128)(2,1)S(1)}, bf16[4,128,128]{2,1,0:T(8,128)(2,1)S(1)}, u32[]{:S(2)}, u32[]{:S(2)}) collective-permute-start(bf16[4,128,128]{2,1,0:T(8,128)(2,1)S(1)} %broadcast_select_fusion.13.refs_0_.refs_10_), channel_id=1, source_target_pairs={{0,64},{16,80},{32,96},{48,112},{64,0},{80,16},{96,32},{112,48},{1... | collective-permute-start | bytes 393224 | tf_op jit(solution)/shard_map/ppermute | solution.py:249
  96.7 10.2 %collective-permute-start.28 = (bf16[4,128,128]{2,1,0:T(8,128)(2,1)S(1)}, bf16[4,128,128]{2,1,0:T(8,128)(2,1)S(1)}, u32[]{:S(2)}, u32[]{:S(2)}) collective-permute-start(bf16[4,128,128]{2,1,0:T(8,128)(2,1)S(1)} %broadcast_select_fusion.13.refs_0_.refs_10_), channel_id=1, source_target_pairs={{0,32},{16,48},{32,0},{48,16},{64,96},{80,112},{96,64},{112,80},{1... | collective-permute-start | bytes 393224 | tf_op jit(solution)/shard_map/ppermute | solution.py:249
  98.7 8.8 %collective-permute-start.31 = (bf16[4,128,128]{2,1,0:T(8,128)(2,1)S(1)}, bf16[4,128,128]{2,1,0:T(8,128)(2,1)S(1)}, u32[]{:S(2)}, u32[]{:S(2)}) collective-permute-start(bf16[4,128,128]{2,1,0:T(8,128)(2,1)S(1)} %broadcast_select_fusion.13.refs_0_.refs_10_), channel_id=1, source_target_pairs={{0,16},{16,0},{32,48},{48,32},{64,80},{80,64},{96,112},{112,96},{1... | collective-permute-start | bytes 393224 | tf_op jit(solution)/shard_map/ppermute | solution.py:249
  103.2 4.4 %collective-permute-start.34 = (bf16[4,128,128]{2,1,0:T(8,128)(2,1)S(1)}, bf16[4,128,128]{2,1,0:T(8,128)(2,1)S(1)}, u32[]{:S(2)}, u32[]{:S(2)}) collective-permute-start(bf16[4,128,128]{2,1,0:T(8,128)(2,1)S(1)} %collective-permute-done.30.refs_3_), channel_id=1, source_target_pairs={{0,16},{16,0},{32,48},{48,32},{64,80},{80,64},{96,112},{112,96},{1... | collective-permute-start | bytes 393224 | tf_op jit(solution)/shard_map/ppermute | solution.py:249
  103.2 4.8 %collective-permute-start.33 = (bf16[4,128,128]{2,1,0:T(8,128)(2,1)S(1)}, bf16[4,128,128]{2,1,0:T(8,128)(2,1)S(1)}, u32[]{:S(2)}, u32[]{:S(2)}) collective-permute-start(bf16[4,128,128]{2,1,0:T(8,128)(2,1)S(1)} %collective-permute-done.29.refs_2_), channel_id=1, source_target_pairs={{0,16},{16,0},{32,48},{48,32},{64,80},{80,64},{96,112},{112,96},{1... | collective-permute-start | bytes 393224 | tf_op jit(solution)/shard_map/ppermute | solution.py:249
  107.0 1.5 %collective-permute-start.32 = (bf16[4,128,128]{2,1,0:T(8,128)(2,1)S(1)}, bf16[4,128,128]{2,1,0:T(8,128)(2,1)S(1)}, u32[]{:S(2)}, u32[]{:S(2)}) collective-permute-start(bf16[4,128,128]{2,1,0:T(8,128)(2,1)S(1)} %collective-permute-done.28.refs_1_), channel_id=1, source_target_pairs={{0,16},{16,0},{32,48},{48,32},{64,80},{80,64},{96,112},{112,96},{1... | collective-permute-start | bytes 393224 | tf_op jit(solution)/shard_map/ppermute | solution.py:249
  109.1 0.7 collective-permute-start.36
  109.8 0.7 collective-permute-start.37
  110.5 0.7 collective-permute-start.38
  111.2 8.9 %collective-permute-start.39 = (bf16[4,128,128]{2,1,0:T(8,128)(2,1)S(1)}, bf16[4,128,128]{2,1,0:T(8,128)(2,1)S(1)}, u32[]{:S(2)}, u32[]{:S(2)}) collective-permute-start(bf16[4,128,128]{2,1,0:T(8,128)(2,1)S(1)} %broadcast_select_fusion.8), channel_id=1, source_target_pairs={{0,12},{1,13},{2,14},{3,15},{4,8},{5,9},{6,10},{7,11},{16,28},{17,... | collective-permute-start | bytes 393224 | tf_op jit(solution)/shard_map/ppermute | solution.py:274
  120.2 14.3 %collective-permute-start.42 = (bf16[4,128,128]{2,1,0:T(8,128)(2,1)S(1)}, bf16[4,128,128]{2,1,0:T(8,128)(2,1)S(1)}, u32[]{:S(2)}, u32[]{:S(2)}) collective-permute-start(bf16[4,128,128]{2,1,0:T(8,128)(2,1)S(1)} %broadcast_select_fusion.12.refs_0_.refs_11_), channel_id=1, source_target_pairs={{0,96},{16,112},{32,64},{48,80},{64,32},{80,48},{96,0},{112,16},{1... | collective-permute-start | bytes 393224 | tf_op jit(solution)/shard_map/ppermute | solution.py:249
  121.8 17.1 %collective-permute-start.47 = (f32[4,128,128]{2,1,0:T(8,128)S(1)}, f32[4,128,128]{2,1,0:T(8,128)S(1)}, u32[]{:S(2)}, u32[]{:S(2)}) collective-permute-start(f32[4,128,128]{2,1,0:T(8,128)S(1)} %shard_map.111), channel_id=1, source_target_pairs={{1,0},{2,1},{3,2},{4,3},{5,4},{6,5},{7,6},{8,7},{9,8},{10,9},{11,1... | collective-permute-start | bytes 786440 | tf_op jit(solution)/shard_map/ppermute | solution.py:284
  128.2 6.3 %collective-permute-start.41 = (bf16[4,128,128]{2,1,0:T(8,128)(2,1)S(1)}, bf16[4,128,128]{2,1,0:T(8,128)(2,1)S(1)}, u32[]{:S(2)}, u32[]{:S(2)}) collective-permute-start(bf16[4,128,128]{2,1,0:T(8,128)(2,1)S(1)} %broadcast_select_fusion.12.refs_0_.refs_11_), channel_id=1, source_target_pairs={{0,64},{16,80},{32,96},{48,112},{64,0},{80,16},{96,32},{112,48},{1... | collective-permute-start | bytes 393224 | tf_op jit(solution)/shard_map/ppermute | solution.py:249
  128.7 10.0 %collective-permute-start.40 = (bf16[4,128,128]{2,1,0:T(8,128)(2,1)S(1)}, bf16[4,128,128]{2,1,0:T(8,128)(2,1)S(1)}, u32[]{:S(2)}, u32[]{:S(2)}) collective-permute-start(bf16[4,128,128]{2,1,0:T(8,128)(2,1)S(1)} %broadcast_select_fusion.12.refs_0_.refs_11_), channel_id=1, source_target_pairs={{0,32},{16,48},{32,0},{48,16},{64,96},{80,112},{96,64},{112,80},{1... | collective-permute-start | bytes 393224 | tf_op jit(solution)/shard_map/ppermute | solution.py:249
  129.8 9.0 %collective-permute-start.43 = (bf16[4,128,128]{2,1,0:T(8,128)(2,1)S(1)}, bf16[4,128,128]{2,1,0:T(8,128)(2,1)S(1)}, u32[]{:S(2)}, u32[]{:S(2)}) collective-permute-start(bf16[4,128,128]{2,1,0:T(8,128)(2,1)S(1)} %broadcast_select_fusion.12.refs_0_.refs_11_), channel_id=1, source_target_pairs={{0,16},{16,0},{32,48},{48,32},{64,80},{80,64},{96,112},{112,96},{1... | collective-permute-start | bytes 393224 | tf_op jit(solution)/shard_map/ppermute | solution.py:249
  134.5 4.4 %collective-permute-start.46 = (bf16[4,128,128]{2,1,0:T(8,128)(2,1)S(1)}, bf16[4,128,128]{2,1,0:T(8,128)(2,1)S(1)}, u32[]{:S(2)}, u32[]{:S(2)}) collective-permute-start(bf16[4,128,128]{2,1,0:T(8,128)(2,1)S(1)} %collective-permute-done.42.refs_3_), channel_id=1, source_target_pairs={{0,16},{16,0},{32,48},{48,32},{64,80},{80,64},{96,112},{112,96},{1... | collective-permute-start | bytes 393224 | tf_op jit(solution)/shard_map/ppermute | solution.py:249
  134.5 5.2 %collective-permute-start.45 = (bf16[4,128,128]{2,1,0:T(8,128)(2,1)S(1)}, bf16[4,128,128]{2,1,0:T(8,128)(2,1)S(1)}, u32[]{:S(2)}, u32[]{:S(2)}) collective-permute-start(bf16[4,128,128]{2,1,0:T(8,128)(2,1)S(1)} %collective-permute-done.41.refs_2_), channel_id=1, source_target_pairs={{0,16},{16,0},{32,48},{48,32},{64,80},{80,64},{96,112},{112,96},{1... | collective-permute-start | bytes 393224 | tf_op jit(solution)/shard_map/ppermute | solution.py:249
  138.7 1.3 collective-permute-start.44

commit v5 on v4

--- a/solution.py
+++ b/solution.py
@@ -9,8 +9,8 @@
 
 
 GROUP = 4
-UNROLL = 9
-GROUPS = 27
+UNROLL = 14
+GROUPS = 28
 PLACES = GROUP * GROUPS
 ZERO_COLUMN = 32
 COUNT_WORD = PLACES + GROUPS
@@ -70,7 +70,7 @@
         words[at] = jnp.where(at < PLACES, ZERO_COLUMN, 0)
         return carry
 
-    lax.fori_loop(0, COUNT_WORD + 1, clear, 0, unroll=8)
+    lax.fori_loop(0, COUNT_WORD + 1, clear, 0, unroll=3)
 
     def count_row(slot, carry):
         tally[tables[slot]] += 1

time: 143 us -> 143 us (level)
  no operation moved by 1% of the time
where the time goes in v5:
time: 143 us; the launch traced here: 142 us
  starting transfers between devices  90.6 us (63%)
  waiting for transfers between devices  34.5 us (24%)
  Pallas kernels  11.7 us (8%)
  local copies, waits for them, and re-layouts  2.48 us (2%)
  between operations  2.03 us (1%)
    ppermute x28, starting transfers between devices, over_rows(): return lax.ppermute(value, 'rows', [(r, r ^ flip) for r in range(count)])  52.5 us
    ppermute x16, waiting for transfers between devices, spread(): arrived = lax.ppermute(value, 'lag', pairs)  30.9 us
    ppermute x4, starting transfers between devices, from_behind(): return lax.ppermute(value, 'lag', [(g + 1, g) for g in range(count - 1)])  24.9 us
    ppermute x16, starting transfers between devices, spread(): arrived = lax.ppermute(value, 'lag', pairs)  13.2 us
    pallas_call x3, Pallas kernels, others_step(): pl.pallas_call(others_kernel, out_shape=jax.ShapeDtypeStruct(base.shape,...  3.9 us
    ppermute x28, waiting for transfers between devices, over_rows(): return lax.ppermute(value, 'rows', [(r, r ^ flip) for r in range(count)])  3.53 us
    pallas_call x1, Pallas kernels, prepare(): pl.pallas_call(words_kernel, out_shape=[jax.ShapeDtypeStruct((COUNT_WORD...  3.08 us
  transfers between devices with their start and end apart: 48, of which 10 were waited for; matrix products, arithmetic and copies ran while one was open for 1% of the time, Pallas kernels for 5%

profile of v5, /device:TPU:25, one launch (start us, length us, event | category | flops | bytes accessed | tf_op | source)
XLA Modules:
  0.0 142.4 jit_solution(12120780447263257675)
XLA Ops:
  0.6 0.7 shard_map.105
  1.4 0.7 collective-permute-start
  2.1 0.9 broadcast_select_fusion.3
  3.0 0.7 collective-permute-start.1
  3.7 0.7 collective-permute-start.2
  4.4 1.3 collective-permute-start.3
  5.8 12.2 %collective-permute-done.3 = bf16[4,128,128]{2,1,0:T(8,128)(2,1)S(1)} collective-permute-done((bf16[4,128,128]{2,1,0:T(8,128)(2,1)S(1)}, bf16[4,128,128]{2,1,0:T(8,128)(2,1)S(1)}, u32[]{:S(2)}, u32[]{:S(2)}) %collective-permute-start.3) | collective-permute-done | bytes 131104 | tf_op jit(solution)/shard_map/ppermute | solution.py:274
  18.0 3.8 %collective-permute-start.6 = (bf16[4,128,128]{2,1,0:T(8,128)(2,1)S(1)}, bf16[4,128,128]{2,1,0:T(8,128)(2,1)S(1)}, u32[]{:S(2)}, u32[]{:S(2)}) collective-permute-start(bf16[4,128,128]{2,1,0:T(8,128)(2,1)S(1)} %broadcast_select_fusion.15.refs_0_.refs_8_), channel_id=1, source_target_pairs={{0,96},{16,112},{32,64},{48,80},{64,32},{80,48},{96,0},{112,16},{1... | collective-permute-start | bytes 393224 | tf_op jit(solution)/shard_map/ppermute | solution.py:249
  21.8 6.0 %collective-permute-start.11 = (f32[4,128,128]{2,1,0:T(8,128)}, f32[4,128,128]{2,1,0:T(8,128)S(1)}, u32[]{:S(2)}, u32[]{:S(2)}) collective-permute-start(f32[4,128,128]{2,1,0:T(8,128)} %bitcast.12), channel_id=1, source_target_pairs={{1,0},{2,1},{3,2},{4,3},{5,4},{6,5},{7,6},{8,7},{9,8},{10,9},{11,1... | collective-permute-start | bytes 786440 | tf_op jit(solution)/shard_map/ppermute | solution.py:284
  27.9 0.6 collective-permute-start.4
  28.5 5.0 %collective-permute-start.7 = (bf16[4,128,128]{2,1,0:T(8,128)(2,1)S(1)}, bf16[4,128,128]{2,1,0:T(8,128)(2,1)S(1)}, u32[]{:S(2)}, u32[]{:S(2)}) collective-permute-start(bf16[4,128,128]{2,1,0:T(8,128)(2,1)S(1)} %broadcast_select_fusion.15.refs_0_.refs_8_), channel_id=1, source_target_pairs={{0,16},{16,0},{32,48},{48,32},{64,80},{80,64},{96,112},{112,96},{1... | collective-permute-start | bytes 393224 | tf_op jit(solution)/shard_map/ppermute | solution.py:249
  33.5 5.6 %collective-permute-start.9 = (bf16[4,128,128]{2,1,0:T(8,128)(2,1)S(1)}, bf16[4,128,128]{2,1,0:T(8,128)(2,1)S(1)}, u32[]{:S(2)}, u32[]{:S(2)}) collective-permute-start(bf16[4,128,128]{2,1,0:T(8,128)(2,1)S(1)} %collective-permute-done.5.refs_2_), channel_id=1, source_target_pairs={{0,16},{16,0},{32,48},{48,32},{64,80},{80,64},{96,112},{112,96},{1... | collective-permute-start | bytes 393224 | tf_op jit(solution)/shard_map/ppermute | solution.py:249
  39.7 0.8 reshape.19
  40.5 0.8 concatenate.3.tables
  41.2 0.9 copy-done.1
  42.2 3.1 %shard_map.104 = (s32[141]{0:T(256)S(1)}, bf16[96,128,128]{2,1,0:T(8,128)(2,1)S(1)}, bf16[4,4,128,128]{3,2,1,0:T(8,128)(2,1)S(1)}, f32[4,128,128]{2,1,0:T(8,128)S(1)}) custom-call(s32[306]{0:T(512)S(1)} %concatenate.3.tables, bf16[96,128,128]{2,1,0:T(8,128)(2,1)} %refs_0_.1, bf16[4,4,128,128]{3,2,1,0:T(8,128)(2,1)S(1)} %bitcast.10, f32[4,128,128]{2,1,0:T(8,128)S(1)} %copy-done.1), custom_call_target="tpu_custom_call" | custom-call | tf_op jit(solution)/shard_map/pallas_call | solution.py:182
  45.3 0.6 shard_map.106
  45.9 0.7 collective-permute-start.12
  46.6 0.7 collective-permute-start.13
  47.3 0.7 collective-permute-start.14
  48.0 1.3 collective-permute-start.15
  49.3 1.3 shard_map.107
  50.6 5.9 %collective-permute-done.15 = bf16[4,128,128]{2,1,0:T(8,128)(2,1)S(1)} collective-permute-done((bf16[4,128,128]{2,1,0:T(8,128)(2,1)S(1)}, bf16[4,128,128]{2,1,0:T(8,128)(2,1)S(1)}, u32[]{:S(2)}, u32[]{:S(2)}) %collective-permute-start.15) | collective-permute-done | bytes 131104 | tf_op jit(solution)/shard_map/ppermute | solution.py:274
  56.5 2.5 %collective-permute-start.18 = (bf16[4,128,128]{2,1,0:T(8,128)(2,1)S(1)}, bf16[4,128,128]{2,1,0:T(8,128)(2,1)S(1)}, u32[]{:S(2)}, u32[]{:S(2)}) collective-permute-start(bf16[4,128,128]{2,1,0:T(8,128)(2,1)S(1)} %broadcast_select_fusion.14.refs_0_.refs_9_), channel_id=1, source_target_pairs={{0,96},{16,112},{32,64},{48,80},{64,32},{80,48},{96,0},{112,16},{1... | collective-permute-start | bytes 393224 | tf_op jit(solution)/shard_map/ppermute | solution.py:249
  59.0 6.3 %collective-permute-start.23 = (f32[4,128,128]{2,1,0:T(8,128)S(1)}, f32[4,128,128]{2,1,0:T(8,128)S(1)}, u32[]{:S(2)}, u32[]{:S(2)}) collective-permute-start(f32[4,128,128]{2,1,0:T(8,128)S(1)} %shard_map.107), channel_id=1, source_target_pairs={{1,0},{2,1},{3,2},{4,3},{5,4},{6,5},{7,6},{8,7},{9,8},{10,9},{11,1... | collective-permute-start | bytes 786440 | tf_op jit(solution)/shard_map/ppermute | solution.py:284
  65.3 0.2 collective-permute-start.17
  65.5 0.5 collective-permute-start.16
  66.0 5.0 %collective-permute-start.19 = (bf16[4,128,128]{2,1,0:T(8,128)(2,1)S(1)}, bf16[4,128,128]{2,1,0:T(8,128)(2,1)S(1)}, u32[]{:S(2)}, u32[]{:S(2)}) collective-permute-start(bf16[4,128,128]{2,1,0:T(8,128)(2,1)S(1)} %broadcast_select_fusion.14.refs_0_.refs_9_), channel_id=1, source_target_pairs={{0,16},{16,0},{32,48},{48,32},{64,80},{80,64},{96,112},{112,96},{1... | collective-permute-start | bytes 393224 | tf_op jit(solution)/shard_map/ppermute | solution.py:249
  71.0 4.6 %collective-permute-start.21 = (bf16[4,128,128]{2,1,0:T(8,128)(2,1)S(1)}, bf16[4,128,128]{2,1,0:T(8,128)(2,1)S(1)}, u32[]{:S(2)}, u32[]{:S(2)}) collective-permute-start(bf16[4,128,128]{2,1,0:T(8,128)(2,1)S(1)} %collective-permute-done.17.refs_2_), channel_id=1, source_target_pairs={{0,16},{16,0},{32,48},{48,32},{64,80},{80,64},{96,112},{112,96},{1... | collective-permute-start | bytes 393224 | tf_op jit(solution)/shard_map/ppermute | solution.py:249
  75.6 1.0 collective-permute-done.21.refs_6_
  76.6 0.4 collective-permute-done.20.refs_5_
  77.0 0.6 shard_map.108
  77.5 0.7 collective-permute-start.24
  78.3 0.7 collective-permute-start.25
  79.0 0.7 collective-permute-start.26
  79.7 1.3 collective-permute-start.27
  81.0 1.3 shard_map.109
  82.3 6.5 %collective-permute-done.27 = bf16[4,128,128]{2,1,0:T(8,128)(2,1)S(1)} collective-permute-done((bf16[4,128,128]{2,1,0:T(8,128)(2,1)S(1)}, bf16[4,128,128]{2,1,0:T(8,128)(2,1)S(1)}, u32[]{:S(2)}, u32[]{:S(2)}) %collective-permute-start.27) | collective-permute-done | bytes 131104 | tf_op jit(solution)/shard_map/ppermute | solution.py:274
  88.8 1.2 collective-permute-start.30
  90.0 6.3 %collective-permute-start.35 = (f32[4,128,128]{2,1,0:T(8,128)S(1)}, f32[4,128,128]{2,1,0:T(8,128)S(1)}, u32[]{:S(2)}, u32[]{:S(2)}) collective-permute-start(f32[4,128,128]{2,1,0:T(8,128)S(1)} %shard_map.109), channel_id=1, source_target_pairs={{1,0},{2,1},{3,2},{4,3},{5,4},{6,5},{7,6},{8,7},{9,8},{10,9},{11,1... | collective-permute-start | bytes 786440 | tf_op jit(solution)/shard_map/ppermute | solution.py:284
  96.3 0.3 collective-permute-start.29
  96.7 2.0 %collective-permute-start.28 = (bf16[4,128,128]{2,1,0:T(8,128)(2,1)S(1)}, bf16[4,128,128]{2,1,0:T(8,128)(2,1)S(1)}, u32[]{:S(2)}, u32[]{:S(2)}) collective-permute-start(bf16[4,128,128]{2,1,0:T(8,128)(2,1)S(1)} %broadcast_select_fusion.13.refs_0_.refs_10_), channel_id=1, source_target_pairs={{0,32},{16,48},{32,0},{48,16},{64,96},{80,112},{96,64},{112,80},{1... | collective-permute-start | bytes 393224 | tf_op jit(solution)/shard_map/ppermute | solution.py:249
  98.7 4.5 %collective-permute-start.31 = (bf16[4,128,128]{2,1,0:T(8,128)(2,1)S(1)}, bf16[4,128,128]{2,1,0:T(8,128)(2,1)S(1)}, u32[]{:S(2)}, u32[]{:S(2)}) collective-permute-start(bf16[4,128,128]{2,1,0:T(8,128)(2,1)S(1)} %broadcast_select_fusion.13.refs_0_.refs_10_), channel_id=1, source_target_pairs={{0,16},{16,0},{32,48},{48,32},{64,80},{80,64},{96,112},{112,96},{1... | collective-permute-start | bytes 393224 | tf_op jit(solution)/shard_map/ppermute | solution.py:249
  103.2 3.8 %collective-permute-start.33 = (bf16[4,128,128]{2,1,0:T(8,128)(2,1)S(1)}, bf16[4,128,128]{2,1,0:T(8,128)(2,1)S(1)}, u32[]{:S(2)}, u32[]{:S(2)}) collective-permute-start(bf16[4,128,128]{2,1,0:T(8,128)(2,1)S(1)} %collective-permute-done.29.refs_2_), channel_id=1, source_target_pairs={{0,16},{16,0},{32,48},{48,32},{64,80},{80,64},{96,112},{112,96},{1... | collective-permute-start | bytes 393224 | tf_op jit(solution)/shard_map/ppermute | solution.py:249
  107.0 0.5 collective-permute-start.32
  107.5 0.4 collective-permute-done.33.refs_6_
  107.9 0.5 collective-permute-done.32.refs_5_
  108.5 0.8 shard_map.110
  109.2 0.7 collective-permute-start.36
  110.0 0.7 collective-permute-start.37
  110.7 0.7 collective-permute-start.38
  111.4 1.3 collective-permute-start.39
  112.7 1.3 shard_map.111
  114.0 6.3 %collective-permute-done.39 = bf16[4,128,128]{2,1,0:T(8,128)(2,1)S(1)} collective-permute-done((bf16[4,128,128]{2,1,0:T(8,128)(2,1)S(1)}, bf16[4,128,128]{2,1,0:T(8,128)(2,1)S(1)}, u32[]{:S(2)}, u32[]{:S(2)}) %collective-permute-start.39) | collective-permute-done | bytes 131104 | tf_op jit(solution)/shard_map/ppermute | solution.py:274
  120.3 1.6 %collective-permute-start.42 = (bf16[4,128,128]{2,1,0:T(8,128)(2,1)S(1)}, bf16[4,128,128]{2,1,0:T(8,128)(2,1)S(1)}, u32[]{:S(2)}, u32[]{:S(2)}) collective-permute-start(bf16[4,128,128]{2,1,0:T(8,128)(2,1)S(1)} %broadcast_select_fusion.12.refs_0_.refs_11_), channel_id=1, source_target_pairs={{0,96},{16,112},{32,64},{48,80},{64,32},{80,48},{96,0},{112,16},{1... | collective-permute-start | bytes 393224 | tf_op jit(solution)/shard_map/ppermute | solution.py:249
  122.0 6.4 %collective-permute-start.47 = (f32[4,128,128]{2,1,0:T(8,128)S(1)}, f32[4,128,128]{2,1,0:T(8,128)S(1)}, u32[]{:S(2)}, u32[]{:S(2)}) collective-permute-start(f32[4,128,128]{2,1,0:T(8,128)S(1)} %shard_map.111), channel_id=1, source_target_pairs={{1,0},{2,1},{3,2},{4,3},{5,4},{6,5},{7,6},{8,7},{9,8},{10,9},{11,1... | collective-permute-start | bytes 786440 | tf_op jit(solution)/shard_map/ppermute | solution.py:284
  128.4 0.5 collective-permute-start.41
  128.9 1.1 collective-permute-start.40
  130.0 4.7 %collective-permute-start.43 = (bf16[4,128,128]{2,1,0:T(8,128)(2,1)S(1)}, bf16[4,128,128]{2,1,0:T(8,128)(2,1)S(1)}, u32[]{:S(2)}, u32[]{:S(2)}) collective-permute-start(bf16[4,128,128]{2,1,0:T(8,128)(2,1)S(1)} %broadcast_select_fusion.12.refs_0_.refs_11_), channel_id=1, source_target_pairs={{0,16},{16,0},{32,48},{48,32},{64,80},{80,64},{96,112},{112,96},{1... | collective-permute-start | bytes 393224 | tf_op jit(solution)/shard_map/ppermute | solution.py:249
  134.7 4.2 %collective-permute-start.45 = (bf16[4,128,128]{2,1,0:T(8,128)(2,1)S(1)}, bf16[4,128,128]{2,1,0:T(8,128)(2,1)S(1)}, u32[]{:S(2)}, u32[]{:S(2)}) collective-permute-start(bf16[4,128,128]{2,1,0:T(8,128)(2,1)S(1)} %collective-permute-done.41.refs_2_), channel_id=1, source_target_pairs={{0,16},{16,0},{32,48},{48,32},{64,80},{80,64},{96,112},{112,96},{1... | collective-permute-start | bytes 393224 | tf_op jit(solution)/shard_map/ppermute | solution.py:249
  138.9 0.2 collective-permute-start.44
  139.0 0.8 collective-permute-done.45.refs_6_
  139.9 0.4 collective-permute-done.44.refs_5_
  140.2 2.1 %shard_map.112 = (f32[4,128,128]{2,1,0:T(8,128)}, bf16[4,4,128,128]{3,2,1,0:T(8,128)(2,1)}) custom-call(s32[141]{0:T(256)S(1)} %get-tuple-element.8.meta, bf16[96,128,128]{2,1,0:T(8,128)(2,1)S(1)} %get-tuple-element.9.blocks, bf16[4,128,128]{2,1,0:T(8,128)(2,1)S(1)} %broadcast_select_fusion.12.refs_0_.refs_11_, ...), custom_call_target="tpu_custom_call" | custom-call | tf_op jit(solution)/shard_map/pallas_call | solution.py:234
  (63 shorter events, 0.5 us)
Async XLA Ops:
  0.6 40.6 %copy-start = (bf16[4,512,128]{2,1,0:T(8,128)(2,1)S(1)}, bf16[4,512,128]{2,1,0:T(8,128)(2,1)}, u32[]{:S(2)}) copy-start(bf16[4,512,128]{2,1,0:T(8,128)(2,1)} %param.9) | copy-start | bytes 1572868
  1.4 0.7 collective-permute-start
  3.0 0.7 collective-permute-start.1
  3.7 0.7 collective-permute-start.2
  4.4 13.5 %collective-permute-start.3 = (bf16[4,128,128]{2,1,0:T(8,128)(2,1)S(1)}, bf16[4,128,128]{2,1,0:T(8,128)(2,1)S(1)}, u32[]{:S(2)}, u32[]{:S(2)}) collective-permute-start(bf16[4,128,128]{2,1,0:T(8,128)(2,1)S(1)} %broadcast_select_fusion.11), channel_id=1, source_target_pairs={{0,12},{1,13},{2,14},{3,15},{4,8},{5,9},{6,10},{7,11},{16,28},{17,... | collective-permute-start | bytes 393224 | tf_op jit(solution)/shard_map/ppermute | solution.py:274
  18.0 15.5 %collective-permute-start.6 = (bf16[4,128,128]{2,1,0:T(8,128)(2,1)S(1)}, bf16[4,128,128]{2,1,0:T(8,128)(2,1)S(1)}, u32[]{:S(2)}, u32[]{:S(2)}) collective-permute-start(bf16[4,128,128]{2,1,0:T(8,128)(2,1)S(1)} %broadcast_select_fusion.15.refs_0_.refs_8_), channel_id=1, source_target_pairs={{0,96},{16,112},{32,64},{48,80},{64,32},{80,48},{96,0},{112,16},{1... | collective-permute-start | bytes 393224 | tf_op jit(solution)/shard_map/ppermute | solution.py:249
  21.8 23.4 %collective-permute-start.11 = (f32[4,128,128]{2,1,0:T(8,128)}, f32[4,128,128]{2,1,0:T(8,128)S(1)}, u32[]{:S(2)}, u32[]{:S(2)}) collective-permute-start(f32[4,128,128]{2,1,0:T(8,128)} %bitcast.12), channel_id=1, source_target_pairs={{1,0},{2,1},{3,2},{4,3},{5,4},{6,5},{7,6},{8,7},{9,8},{10,9},{11,1... | collective-permute-start | bytes 786440 | tf_op jit(solution)/shard_map/ppermute | solution.py:284
  27.8 5.7 %collective-permute-start.5 = (bf16[4,128,128]{2,1,0:T(8,128)(2,1)S(1)}, bf16[4,128,128]{2,1,0:T(8,128)(2,1)S(1)}, u32[]{:S(2)}, u32[]{:S(2)}) collective-permute-start(bf16[4,128,128]{2,1,0:T(8,128)(2,1)S(1)} %broadcast_select_fusion.15.refs_0_.refs_8_), channel_id=1, source_target_pairs={{0,64},{16,80},{32,96},{48,112},{64,0},{80,16},{96,32},{112,48},{1... | collective-permute-start | bytes 393224 | tf_op jit(solution)/shard_map/ppermute | solution.py:249
  27.9 11.2 %collective-permute-start.4 = (bf16[4,128,128]{2,1,0:T(8,128)(2,1)S(1)}, bf16[4,128,128]{2,1,0:T(8,128)(2,1)S(1)}, u32[]{:S(2)}, u32[]{:S(2)}) collective-permute-start(bf16[4,128,128]{2,1,0:T(8,128)(2,1)S(1)} %broadcast_select_fusion.15.refs_0_.refs_8_), channel_id=1, source_target_pairs={{0,32},{16,48},{32,0},{48,16},{64,96},{80,112},{96,64},{112,80},{1... | collective-permute-start | bytes 393224 | tf_op jit(solution)/shard_map/ppermute | solution.py:249
  28.5 16.8 %collective-permute-start.7 = (bf16[4,128,128]{2,1,0:T(8,128)(2,1)S(1)}, bf16[4,128,128]{2,1,0:T(8,128)(2,1)S(1)}, u32[]{:S(2)}, u32[]{:S(2)}) collective-permute-start(bf16[4,128,128]{2,1,0:T(8,128)(2,1)S(1)} %broadcast_select_fusion.15.refs_0_.refs_8_), channel_id=1, source_target_pairs={{0,16},{16,0},{32,48},{48,32},{64,80},{80,64},{96,112},{112,96},{1... | collective-permute-start | bytes 393224 | tf_op jit(solution)/shard_map/ppermute | solution.py:249
  33.4 11.8 %collective-permute-start.10 = (bf16[4,128,128]{2,1,0:T(8,128)(2,1)S(1)}, bf16[4,128,128]{2,1,0:T(8,128)(2,1)S(1)}, u32[]{:S(2)}, u32[]{:S(2)}) collective-permute-start(bf16[4,128,128]{2,1,0:T(8,128)(2,1)S(1)} %collective-permute-done.6.refs_3_), channel_id=1, source_target_pairs={{0,16},{16,0},{32,48},{48,32},{64,80},{80,64},{96,112},{112,96},{1... | collective-permute-start | bytes 393224 | tf_op jit(solution)/shard_map/ppermute | solution.py:249
  33.5 11.8 %collective-permute-start.9 = (bf16[4,128,128]{2,1,0:T(8,128)(2,1)S(1)}, bf16[4,128,128]{2,1,0:T(8,128)(2,1)S(1)}, u32[]{:S(2)}, u32[]{:S(2)}) collective-permute-start(bf16[4,128,128]{2,1,0:T(8,128)(2,1)S(1)} %collective-permute-done.5.refs_2_), channel_id=1, source_target_pairs={{0,16},{16,0},{32,48},{48,32},{64,80},{80,64},{96,112},{112,96},{1... | collective-permute-start | bytes 393224 | tf_op jit(solution)/shard_map/ppermute | solution.py:249
  39.0 6.3 %collective-permute-start.8 = (bf16[4,128,128]{2,1,0:T(8,128)(2,1)S(1)}, bf16[4,128,128]{2,1,0:T(8,128)(2,1)S(1)}, u32[]{:S(2)}, u32[]{:S(2)}) collective-permute-start(bf16[4,128,128]{2,1,0:T(8,128)(2,1)S(1)} %collective-permute-done.4.refs_1_), channel_id=1, source_target_pairs={{0,16},{16,0},{32,48},{48,32},{64,80},{80,64},{96,112},{112,96},{1... | collective-permute-start | bytes 393224 | tf_op jit(solution)/shard_map/ppermute | solution.py:249
  41.2 1.0 copy-start.1
  45.9 0.7 collective-permute-start.12
  46.6 0.7 collective-permute-start.13
  47.3 0.7 collective-permute-start.14
  48.0 8.5 %collective-permute-start.15 = (bf16[4,128,128]{2,1,0:T(8,128)(2,1)S(1)}, bf16[4,128,128]{2,1,0:T(8,128)(2,1)S(1)}, u32[]{:S(2)}, u32[]{:S(2)}) collective-permute-start(bf16[4,128,128]{2,1,0:T(8,128)(2,1)S(1)} %broadcast_select_fusion.10), channel_id=1, source_target_pairs={{0,12},{1,13},{2,14},{3,15},{4,8},{5,9},{6,10},{7,11},{16,28},{17,... | collective-permute-start | bytes 393224 | tf_op jit(solution)/shard_map/ppermute | solution.py:274
  56.5 14.4 %collective-permute-start.18 = (bf16[4,128,128]{2,1,0:T(8,128)(2,1)S(1)}, bf16[4,128,128]{2,1,0:T(8,128)(2,1)S(1)}, u32[]{:S(2)}, u32[]{:S(2)}) collective-permute-start(bf16[4,128,128]{2,1,0:T(8,128)(2,1)S(1)} %broadcast_select_fusion.14.refs_0_.refs_9_), channel_id=1, source_target_pairs={{0,96},{16,112},{32,64},{48,80},{64,32},{80,48},{96,0},{112,16},{1... | collective-permute-start | bytes 393224 | tf_op jit(solution)/shard_map/ppermute | solution.py:249
  59.0 16.6 %collective-permute-start.23 = (f32[4,128,128]{2,1,0:T(8,128)S(1)}, f32[4,128,128]{2,1,0:T(8,128)S(1)}, u32[]{:S(2)}, u32[]{:S(2)}) collective-permute-start(f32[4,128,128]{2,1,0:T(8,128)S(1)} %shard_map.107), channel_id=1, source_target_pairs={{1,0},{2,1},{3,2},{4,3},{5,4},{6,5},{7,6},{8,7},{9,8},{10,9},{11,1... | collective-permute-start | bytes 786440 | tf_op jit(solution)/shard_map/ppermute | solution.py:284
  65.3 5.6 %collective-permute-start.17 = (bf16[4,128,128]{2,1,0:T(8,128)(2,1)S(1)}, bf16[4,128,128]{2,1,0:T(8,128)(2,1)S(1)}, u32[]{:S(2)}, u32[]{:S(2)}) collective-permute-start(bf16[4,128,128]{2,1,0:T(8,128)(2,1)S(1)} %broadcast_select_fusion.14.refs_0_.refs_9_), channel_id=1, source_target_pairs={{0,64},{16,80},{32,96},{48,112},{64,0},{80,16},{96,32},{112,48},{1... | collective-permute-start | bytes 393224 | tf_op jit(solution)/shard_map/ppermute | solution.py:249
  65.5 10.1 %collective-permute-start.16 = (bf16[4,128,128]{2,1,0:T(8,128)(2,1)S(1)}, bf16[4,128,128]{2,1,0:T(8,128)(2,1)S(1)}, u32[]{:S(2)}, u32[]{:S(2)}) collective-permute-start(bf16[4,128,128]{2,1,0:T(8,128)(2,1)S(1)} %broadcast_select_fusion.14.refs_0_.refs_9_), channel_id=1, source_target_pairs={{0,32},{16,48},{32,0},{48,16},{64,96},{80,112},{96,64},{112,80},{1... | collective-permute-start | bytes 393224 | tf_op jit(solution)/shard_map/ppermute | solution.py:249
  66.0 9.6 %collective-permute-start.19 = (bf16[4,128,128]{2,1,0:T(8,128)(2,1)S(1)}, bf16[4,128,128]{2,1,0:T(8,128)(2,1)S(1)}, u32[]{:S(2)}, u32[]{:S(2)}) collective-permute-start(bf16[4,128,128]{2,1,0:T(8,128)(2,1)S(1)} %broadcast_select_fusion.14.refs_0_.refs_9_), channel_id=1, source_target_pairs={{0,16},{16,0},{32,48},{48,32},{64,80},{80,64},{96,112},{112,96},{1... | collective-permute-start | bytes 393224 | tf_op jit(solution)/shard_map/ppermute | solution.py:249
  70.9 4.7 %collective-permute-start.22 = (bf16[4,128,128]{2,1,0:T(8,128)(2,1)S(1)}, bf16[4,128,128]{2,1,0:T(8,128)(2,1)S(1)}, u32[]{:S(2)}, u32[]{:S(2)}) collective-permute-start(bf16[4,128,128]{2,1,0:T(8,128)(2,1)S(1)} %collective-permute-done.18.refs_3_), channel_id=1, source_target_pairs={{0,16},{16,0},{32,48},{48,32},{64,80},{80,64},{96,112},{112,96},{1... | collective-permute-start | bytes 393224 | tf_op jit(solution)/shard_map/ppermute | solution.py:249
  71.0 5.6 %collective-permute-start.21 = (bf16[4,128,128]{2,1,0:T(8,128)(2,1)S(1)}, bf16[4,128,128]{2,1,0:T(8,128)(2,1)S(1)}, u32[]{:S(2)}, u32[]{:S(2)}) collective-permute-start(bf16[4,128,128]{2,1,0:T(8,128)(2,1)S(1)} %collective-permute-done.17.refs_2_), channel_id=1, source_target_pairs={{0,16},{16,0},{32,48},{48,32},{64,80},{80,64},{96,112},{112,96},{1... | collective-permute-start | bytes 393224 | tf_op jit(solution)/shard_map/ppermute | solution.py:249
  75.6 1.3 collective-permute-start.20
  77.5 0.7 collective-permute-start.24
  78.3 0.7 collective-permute-start.25
  79.0 0.7 collective-permute-start.26
  79.7 9.1 %collective-permute-start.27 = (bf16[4,128,128]{2,1,0:T(8,128)(2,1)S(1)}, bf16[4,128,128]{2,1,0:T(8,128)(2,1)S(1)}, u32[]{:S(2)}, u32[]{:S(2)}) collective-permute-start(bf16[4,128,128]{2,1,0:T(8,128)(2,1)S(1)} %broadcast_select_fusion.9), channel_id=1, source_target_pairs={{0,12},{1,13},{2,14},{3,15},{4,8},{5,9},{6,10},{7,11},{16,28},{17,... | collective-permute-start | bytes 393224 | tf_op jit(solution)/shard_map/ppermute | solution.py:274
  88.8 14.3 %collective-permute-start.30 = (bf16[4,128,128]{2,1,0:T(8,128)(2,1)S(1)}, bf16[4,128,128]{2,1,0:T(8,128)(2,1)S(1)}, u32[]{:S(2)}, u32[]{:S(2)}) collective-permute-start(bf16[4,128,128]{2,1,0:T(8,128)(2,1)S(1)} %broadcast_select_fusion.13.refs_0_.refs_10_), channel_id=1, source_target_pairs={{0,96},{16,112},{32,64},{48,80},{64,32},{80,48},{96,0},{112,16},{1... | collective-permute-start | bytes 393224 | tf_op jit(solution)/shard_map/ppermute | solution.py:249
  90.0 17.5 %collective-permute-start.35 = (f32[4,128,128]{2,1,0:T(8,128)S(1)}, f32[4,128,128]{2,1,0:T(8,128)S(1)}, u32[]{:S(2)}, u32[]{:S(2)}) collective-permute-start(f32[4,128,128]{2,1,0:T(8,128)S(1)} %shard_map.109), channel_id=1, source_target_pairs={{1,0},{2,1},{3,2},{4,3},{5,4},{6,5},{7,6},{8,7},{9,8},{10,9},{11,1... | collective-permute-start | bytes 786440 | tf_op jit(solution)/shard_map/ppermute | solution.py:284
  96.3 6.9 %collective-permute-start.29 = (bf16[4,128,128]{2,1,0:T(8,128)(2,1)S(1)}, bf16[4,128,128]{2,1,0:T(8,128)(2,1)S(1)}, u32[]{:S(2)}, u32[]{:S(2)}) collective-permute-start(bf16[4,128,128]{2,1,0:T(8,128)(2,1)S(1)} %broadcast_select_fusion.13.refs_0_.refs_10_), channel_id=1, source_target_pairs={{0,64},{16,80},{32,96},{48,112},{64,0},{80,16},{96,32},{112,48},{1... | collective-permute-start | bytes 393224 | tf_op jit(solution)/shard_map/ppermute | solution.py:249
  96.7 10.3 %collective-permute-start.28 = (bf16[4,128,128]{2,1,0:T(8,128)(2,1)S(1)}, bf16[4,128,128]{2,1,0:T(8,128)(2,1)S(1)}, u32[]{:S(2)}, u32[]{:S(2)}) collective-permute-start(bf16[4,128,128]{2,1,0:T(8,128)(2,1)S(1)} %broadcast_select_fusion.13.refs_0_.refs_10_), channel_id=1, source_target_pairs={{0,32},{16,48},{32,0},{48,16},{64,96},{80,112},{96,64},{112,80},{1... | collective-permute-start | bytes 393224 | tf_op jit(solution)/shard_map/ppermute | solution.py:249
  98.7 8.8 %collective-permute-start.31 = (bf16[4,128,128]{2,1,0:T(8,128)(2,1)S(1)}, bf16[4,128,128]{2,1,0:T(8,128)(2,1)S(1)}, u32[]{:S(2)}, u32[]{:S(2)}) collective-permute-start(bf16[4,128,128]{2,1,0:T(8,128)(2,1)S(1)} %broadcast_select_fusion.13.refs_0_.refs_10_), channel_id=1, source_target_pairs={{0,16},{16,0},{32,48},{48,32},{64,80},{80,64},{96,112},{112,96},{1... | collective-permute-start | bytes 393224 | tf_op jit(solution)/shard_map/ppermute | solution.py:249
  103.1 4.4 %collective-permute-start.34 = (bf16[4,128,128]{2,1,0:T(8,128)(2,1)S(1)}, bf16[4,128,128]{2,1,0:T(8,128)(2,1)S(1)}, u32[]{:S(2)}, u32[]{:S(2)}) collective-permute-start(bf16[4,128,128]{2,1,0:T(8,128)(2,1)S(1)} %collective-permute-done.30.refs_3_), channel_id=1, source_target_pairs={{0,16},{16,0},{32,48},{48,32},{64,80},{80,64},{96,112},{112,96},{1... | collective-permute-start | bytes 393224 | tf_op jit(solution)/shard_map/ppermute | solution.py:249
  103.2 4.8 %collective-permute-start.33 = (bf16[4,128,128]{2,1,0:T(8,128)(2,1)S(1)}, bf16[4,128,128]{2,1,0:T(8,128)(2,1)S(1)}, u32[]{:S(2)}, u32[]{:S(2)}) collective-permute-start(bf16[4,128,128]{2,1,0:T(8,128)(2,1)S(1)} %collective-permute-done.29.refs_2_), channel_id=1, source_target_pairs={{0,16},{16,0},{32,48},{48,32},{64,80},{80,64},{96,112},{112,96},{1... | collective-permute-start | bytes 393224 | tf_op jit(solution)/shard_map/ppermute | solution.py:249
  107.0 1.5 %collective-permute-start.32 = (bf16[4,128,128]{2,1,0:T(8,128)(2,1)S(1)}, bf16[4,128,128]{2,1,0:T(8,128)(2,1)S(1)}, u32[]{:S(2)}, u32[]{:S(2)}) collective-permute-start(bf16[4,128,128]{2,1,0:T(8,128)(2,1)S(1)} %collective-permute-done.28.refs_1_), channel_id=1, source_target_pairs={{0,16},{16,0},{32,48},{48,32},{64,80},{80,64},{96,112},{112,96},{1... | collective-permute-start | bytes 393224 | tf_op jit(solution)/shard_map/ppermute | solution.py:249
  109.2 0.7 collective-permute-start.36
  110.0 0.7 collective-permute-start.37
  110.7 0.7 collective-permute-start.38
  111.4 8.9 %collective-permute-start.39 = (bf16[4,128,128]{2,1,0:T(8,128)(2,1)S(1)}, bf16[4,128,128]{2,1,0:T(8,128)(2,1)S(1)}, u32[]{:S(2)}, u32[]{:S(2)}) collective-permute-start(bf16[4,128,128]{2,1,0:T(8,128)(2,1)S(1)} %broadcast_select_fusion.8), channel_id=1, source_target_pairs={{0,12},{1,13},{2,14},{3,15},{4,8},{5,9},{6,10},{7,11},{16,28},{17,... | collective-permute-start | bytes 393224 | tf_op jit(solution)/shard_map/ppermute | solution.py:274
  120.3 14.3 %collective-permute-start.42 = (bf16[4,128,128]{2,1,0:T(8,128)(2,1)S(1)}, bf16[4,128,128]{2,1,0:T(8,128)(2,1)S(1)}, u32[]{:S(2)}, u32[]{:S(2)}) collective-permute-start(bf16[4,128,128]{2,1,0:T(8,128)(2,1)S(1)} %broadcast_select_fusion.12.refs_0_.refs_11_), channel_id=1, source_target_pairs={{0,96},{16,112},{32,64},{48,80},{64,32},{80,48},{96,0},{112,16},{1... | collective-permute-start | bytes 393224 | tf_op jit(solution)/shard_map/ppermute | solution.py:249
  122.0 17.1 %collective-permute-start.47 = (f32[4,128,128]{2,1,0:T(8,128)S(1)}, f32[4,128,128]{2,1,0:T(8,128)S(1)}, u32[]{:S(2)}, u32[]{:S(2)}) collective-permute-start(f32[4,128,128]{2,1,0:T(8,128)S(1)} %shard_map.111), channel_id=1, source_target_pairs={{1,0},{2,1},{3,2},{4,3},{5,4},{6,5},{7,6},{8,7},{9,8},{10,9},{11,1... | collective-permute-start | bytes 786440 | tf_op jit(solution)/shard_map/ppermute | solution.py:284
  128.4 6.3 %collective-permute-start.41 = (bf16[4,128,128]{2,1,0:T(8,128)(2,1)S(1)}, bf16[4,128,128]{2,1,0:T(8,128)(2,1)S(1)}, u32[]{:S(2)}, u32[]{:S(2)}) collective-permute-start(bf16[4,128,128]{2,1,0:T(8,128)(2,1)S(1)} %broadcast_select_fusion.12.refs_0_.refs_11_), channel_id=1, source_target_pairs={{0,64},{16,80},{32,96},{48,112},{64,0},{80,16},{96,32},{112,48},{1... | collective-permute-start | bytes 393224 | tf_op jit(solution)/shard_map/ppermute | solution.py:249
  128.9 10.0 %collective-permute-start.40 = (bf16[4,128,128]{2,1,0:T(8,128)(2,1)S(1)}, bf16[4,128,128]{2,1,0:T(8,128)(2,1)S(1)}, u32[]{:S(2)}, u32[]{:S(2)}) collective-permute-start(bf16[4,128,128]{2,1,0:T(8,128)(2,1)S(1)} %broadcast_select_fusion.12.refs_0_.refs_11_), channel_id=1, source_target_pairs={{0,32},{16,48},{32,0},{48,16},{64,96},{80,112},{96,64},{112,80},{1... | collective-permute-start | bytes 393224 | tf_op jit(solution)/shard_map/ppermute | solution.py:249
  130.0 9.0 %collective-permute-start.43 = (bf16[4,128,128]{2,1,0:T(8,128)(2,1)S(1)}, bf16[4,128,128]{2,1,0:T(8,128)(2,1)S(1)}, u32[]{:S(2)}, u32[]{:S(2)}) collective-permute-start(bf16[4,128,128]{2,1,0:T(8,128)(2,1)S(1)} %broadcast_select_fusion.12.refs_0_.refs_11_), channel_id=1, source_target_pairs={{0,16},{16,0},{32,48},{48,32},{64,80},{80,64},{96,112},{112,96},{1... | collective-permute-start | bytes 393224 | tf_op jit(solution)/shard_map/ppermute | solution.py:249
  134.7 4.4 %collective-permute-start.46 = (bf16[4,128,128]{2,1,0:T(8,128)(2,1)S(1)}, bf16[4,128,128]{2,1,0:T(8,128)(2,1)S(1)}, u32[]{:S(2)}, u32[]{:S(2)}) collective-permute-start(bf16[4,128,128]{2,1,0:T(8,128)(2,1)S(1)} %collective-permute-done.42.refs_3_), channel_id=1, source_target_pairs={{0,16},{16,0},{32,48},{48,32},{64,80},{80,64},{96,112},{112,96},{1... | collective-permute-start | bytes 393224 | tf_op jit(solution)/shard_map/ppermute | solution.py:249
  134.7 5.2 %collective-permute-start.45 = (bf16[4,128,128]{2,1,0:T(8,128)(2,1)S(1)}, bf16[4,128,128]{2,1,0:T(8,128)(2,1)S(1)}, u32[]{:S(2)}, u32[]{:S(2)}) collective-permute-start(bf16[4,128,128]{2,1,0:T(8,128)(2,1)S(1)} %collective-permute-done.41.refs_2_), channel_id=1, source_target_pairs={{0,16},{16,0},{32,48},{48,32},{64,80},{80,64},{96,112},{112,96},{1... | collective-permute-start | bytes 393224 | tf_op jit(solution)/shard_map/ppermute | solution.py:249
  138.9 1.3 collective-permute-start.44
